TPU v7x, 512 devices: a whole 4x8x8 slice. The times are simulated.
512 devices in a mesh: dp: 16 (over y, core), expert: 32 (over z, x).
Axes of the slice: x: 4, y: 8, z: 8, core: 2. Of those that a mesh axis runs over, the one named last changes fastest.
Arguments:
- x_in: bfloat16 [65536, 1024], P(('dp', 'expert')), may hold values from -6 to 6
- grad_out: bfloat16 [65536, 1024], P(('dp', 'expert')), may hold values from -6 to 6
- routes: int32 [65536, 8], P(('dp', 'expert')), may hold values from 0 to 31, as said below
- gate_probs: float32 [65536, 8], P(('dp', 'expert')), may hold values from 0.05 to 1
- gate_up: bfloat16 [32, 1024, 768], P('expert'), may hold values from -0.1875 to 0.1875
- down: bfloat16 [32, 1024, 384], P('expert'), may hold values from -0.3125 to 0.3125
Outputs:
- grad_in: bfloat16 [65536, 1024], P(('dp', 'expert'))
- grad_gate_up: float32 [32, 1024, 768], P('expert', 'dp')
- grad_down: float32 [32, 1024, 384], P('expert', 'dp')
Inputs may be any that keep to these rules, and one draw needn't show every extreme that they name: `routes`: each row names 8 different experts. Among the rows of one device no expert is named more than 36 times, and on every device some expert is named exactly 36 times.
All inputs are finite; a program needn't handle non-finite values.
Results may differ from a plain program's by a relative error of at most 0.02.
Values may be sent and summed in bfloat16 or wider, within the bound.
No kernel may reach another device: no remote copies, remote signals or barrier semaphores. Data moves between devices by JAX's collectives and lax.ppermute only.
A program may use at most 64 MiB of HBM per device.

v0:
```python
import jax
import jax.numpy as jnp
from jax import lax
from jax.sharding import PartitionSpec as P


def slot_ranks(flat_ids, experts):
    onehot = (flat_ids[:, None] == jnp.arange(experts, dtype=jnp.int32)[None, :]).astype(jnp.int32)
    before = jnp.cumsum(onehot, axis=0) - onehot
    return jnp.sum(before * onehot, axis=1)


def dispatch_table(route_block, experts, capacity):
    flat_ids = route_block.reshape(-1)
    count_rows = flat_ids.shape[0]
    slot_rank = slot_ranks(flat_ids, experts)
    entry_pos = flat_ids * capacity + slot_rank
    slot_table = jnp.full((experts * capacity,), count_rows, jnp.int32)
    slot_table = slot_table.at[entry_pos].set(jnp.arange(count_rows, dtype=jnp.int32))
    return (slot_table, entry_pos)


def send_rows(x_block, grad_block, prob_block, slot_table, top_count):
    width = x_block.shape[1]
    token_pos = slot_table // top_count
    x_padded = jnp.concatenate([x_block, jnp.zeros((1, width), jnp.bfloat16)], 0)
    grad_padded = jnp.concatenate([grad_block, jnp.zeros((1, width), jnp.bfloat16)], 0)
    prob_padded = jnp.concatenate([prob_block.reshape(-1), jnp.zeros((1,), jnp.float32)], 0)
    sent_rows = x_padded[token_pos]
    sent_grads = (
        prob_padded[slot_table][:, None] * grad_padded[token_pos].astype(jnp.float32)
    ).astype(jnp.bfloat16)
    return (sent_rows, sent_grads)


def expert_rows(rows_in, scaled, proj_weight, down_weight):
    hidden_units = down_weight.shape[1]
    projected = jnp.dot(rows_in, proj_weight, preferred_element_type=jnp.float32)
    gate_pre = projected[:, :hidden_units]
    up_part = projected[:, hidden_units:]
    sigmoid_v = jax.nn.sigmoid(gate_pre)
    activated = gate_pre * sigmoid_v
    hidden = (activated * up_part).astype(jnp.bfloat16)
    grad_hidden = jnp.dot(scaled, down_weight, preferred_element_type=jnp.float32)
    grad_gate = grad_hidden * up_part * sigmoid_v * (1.0 + gate_pre * (1.0 - sigmoid_v))
    grad_proj = jnp.concatenate([grad_gate, grad_hidden * activated], 1).astype(jnp.bfloat16)
    grad_rows = lax.dot_general(
        grad_proj, proj_weight, (((1,), (1,)), ((), ())), preferred_element_type=jnp.float32
    ).astype(jnp.bfloat16)
    return (grad_rows, grad_proj, hidden)


def weight_terms(rows_in, scaled, grad_proj, hidden):
    first = lax.dot_general(
        rows_in, grad_proj, (((0,), (0,)), ((), ())), preferred_element_type=jnp.float32
    )
    second = lax.dot_general(
        scaled, hidden, (((0,), (0,)), ((), ())), preferred_element_type=jnp.float32
    )
    return jnp.concatenate([first, second], 1)


def per_device(x_in, grad_out, routes, gate_probs, gate_up, down):
    owners = lax.axis_size("expert")
    tokens_here = x_in.shape[0]
    top_count = routes.shape[1]
    width = x_in.shape[1]
    capacity = min(tokens_here, tokens_here * top_count * 9 // (8 * owners))
    slot_table, entry_pos = dispatch_table(routes, owners, capacity)
    sent_rows, sent_grads = send_rows(x_in, grad_out, gate_probs, slot_table, top_count)
    sent_rows = sent_rows.reshape(owners, capacity, width)
    sent_grads = sent_grads.reshape(owners, capacity, width)
    proj_weight = gate_up[0]
    down_weight = down[0]
    recv_rows, recv_grads = (
        lax.all_to_all(sent_rows, "expert", split_axis=0, concat_axis=0, tiled=True),
        lax.all_to_all(sent_grads, "expert", split_axis=0, concat_axis=0, tiled=True),
    )
    rows_in = recv_rows.reshape(-1, width)
    scaled = recv_grads.reshape(-1, width)
    grad_rows, grad_proj, hidden = expert_rows(rows_in, scaled, proj_weight, down_weight)
    returned = lax.all_to_all(
        grad_rows.reshape(owners, capacity, width),
        "expert",
        split_axis=0,
        concat_axis=0,
        tiled=True,
    )
    hidden_units = hidden.shape[1]
    grad_term = weight_terms(rows_in, scaled, grad_proj, hidden)
    grad_share = lax.psum_scatter(
        grad_term.astype(jnp.bfloat16), "dp", scatter_dimension=0, tiled=True
    ).astype(jnp.float32)
    grad_gate_up = grad_share[None, :, : 2 * hidden_units]
    grad_down = grad_share[None, :, 2 * hidden_units :]
    entries = returned.reshape(-1, width)[entry_pos]
    grad_in = jnp.sum(
        entries.reshape(tokens_here, top_count, width).astype(jnp.float32), axis=1
    ).astype(jnp.bfloat16)
    return (grad_in, grad_gate_up, grad_down)


def solution(mesh):
    placed = (
        P(("dp", "expert"), None),
        P(("dp", "expert"), None),
        P(("dp", "expert"), None),
        P(("dp", "expert"), None),
        P("expert", None, None),
        P("expert", None, None),
    )
    return jax.shard_map(
        per_device,
        mesh=mesh,
        in_specs=placed,
        out_specs=(P(("dp", "expert"), None), P("expert", "dp", None), P("expert", "dp", None)),
        check_vma=False,
    )
```

profile of v0, /device:TPU:1, one launch (start us, length us, event | category | flops | bytes accessed | tf_op | source)
XLA Modules:
  0.0 284.0 jit_solution(5766573920304062413)
XLA Ops:
  7.2 0.8 broadcast_multiply_fusion
  8.0 0.8 copy.21
  9.2 9.0 %reduce-window.6 = s32[32,8,128]{2,1,0:T(8,128)S(1)} reduce-window(s32[32,8,128]{2,1,0:T(8,128)S(1)} %fusion.10, s32[]{:T(128)} %constant.16.clone.1), window={size=1x1x128 pad=0_0x0_0x127_0}, to_apply=%region_0.0 | reduce-window | flops 4161536 | bytes 262148 | tf_op jit(solution)/shard_map/reduce-window
  18.7 4.3 %scatter_custom_fusion = s32[1152]{0:T(1024)S(1)} fusion(s32[1024]{0:T(1024)S(1)} %bitcast.45, s32[1024]{0:T(1024)S(1)} %iota.11, s32[]{:T(128)} %constant.12.clone.1), kind=kCustom, calls=%fused_computation.45 | custom fusion | bytes 4612 | tf_op jit(solution)/shard_map/scatter | solution.py:19
  23.1 1.0 concatenate.19
  24.1 5.0 %gather_fusion.2 = bf16[1152,1024]{1,0:T(8,128)(2,1)} fusion(bf16[129,1024]{1,0:T(8,128)(2,1)S(1)} %concatenate.19, s32[2048]{0:T(1024)S(1)} %get-tuple-element.16), kind=kCustom, calls=%fused_computation.2 | custom fusion | bytes 4723200 | tf_op jit(solution)/shard_map/gather | solution.py:29
  29.1 4.1 %reshape.86 = bf16[32,36,1024]{2,1,0:T(8,128)(2,1)} reshape(bf16[1152,1024]{1,0:T(8,128)(2,1)} %gather_fusion.2) | data formatting | bytes 4718592 | tf_op jit(solution)/shard_map/reshape | solution.py:71
  33.2 14.0 %all-to-all-start.1 = ((bf16[32,36,1024]{2,1,0:T(8,128)(2,1)}), bf16[32,36,1024]{2,1,0:T(8,128)(2,1)}, u32[]{:S(2)}, u32[]{:S(2)}) async-start(bf16[32,36,1024]{2,1,0:T(8,128)(2,1)} %reshape.86), calls=%async_computation.1 | async-start | bytes 5242880 | tf_op jit(solution)/shard_map/all_to_all | solution.py:76
  47.4 6.5 %gather_fusion = f32[1152]{0:T(1024)S(1)} fusion(f32[1025]{0:T(1024)S(1)} %pad_maximum_fusion.4, s32[2048]{0:T(1024)S(1)} %get-tuple-element.17), kind=kCustom, calls=%fused_computation | custom fusion | bytes 13824 | tf_op jit(solution)/shard_map/gather | solution.py:31
  54.0 5.0 %gather_fusion.1 = bf16[1152,1024]{1,0:T(8,128)(2,1)} fusion(bf16[129,1024]{1,0:T(8,128)(2,1)S(1)} %concatenate.18, s32[2048]{0:T(1024)S(1)} %get-tuple-element.16), kind=kCustom, calls=%fused_computation.1 | custom fusion | bytes 4723200 | tf_op jit(solution)/shard_map/gather | solution.py:31
  59.0 4.6 %reshape.91 = f32[32,36,1024]{2,1,0:T(8,128)} reshape(bf16[1152,1024]{1,0:T(8,128)(2,1)} %gather_fusion.1) | data formatting | bytes 7077888 | tf_op jit(solution)/shard_map/convert_element_type | solution.py:31
  63.6 4.4 %multiply_convert_fusion = bf16[32,36,1024]{2,1,0:T(8,128)(2,1)} fusion(f32[32,36,1024]{2,1,0:T(8,128)} %reshape.91, f32[32,36]{1,0:T(8,128)S(1)} %mul.55), kind=kLoop, calls=%fused_computation.5 | loop fusion | flops 2359296 | bytes 7082496 | tf_op jit(solution)/shard_map/convert_element_type | solution.py:32
  68.0 38.9 %all-to-all-done.1 = bf16[32,36,1024]{2,1,0:T(8,128)(2,1)} async-done(((bf16[32,36,1024]{2,1,0:T(8,128)(2,1)}), bf16[32,36,1024]{2,1,0:T(8,128)(2,1)}, u32[]{:S(2)}, u32[]{:S(2)}) %all-to-all-start.1) | async-done | bytes 2359328 | tf_op jit(solution)/shard_map/all_to_all | solution.py:76
  106.9 7.1 %all-to-all-start = ((bf16[32,36,1024]{2,1,0:T(8,128)(2,1)}), bf16[32,36,1024]{2,1,0:T(8,128)(2,1)}, u32[]{:S(2)}, u32[]{:S(2)}) async-start(bf16[32,36,1024]{2,1,0:T(8,128)(2,1)} %multiply_convert_fusion), calls=%async_computation | async-start | bytes 5242880 | tf_op jit(solution)/shard_map/all_to_all | solution.py:77
  113.9 4.1 %reshape.87 = bf16[1152,1024]{1,0:T(8,128)(2,1)} reshape(bf16[32,36,1024]{2,1,0:T(8,128)(2,1)} %all-to-all-done.1) | data formatting | bytes 4718592 | tf_op jit(solution)/shard_map/reshape | solution.py:79
  118.0 5.8 %fusion.2 = f32[1152,768]{0,1:T(8,128)} fusion(bf16[1152,1024]{1,0:T(8,128)(2,1)} %reshape.87, bf16[1,1024,768]{2,1,0:T(8,128)(2,1)S(1)} %copy-done), kind=kOutput, calls=%fused_computation.17 | convolution fusion | flops 1811939328 | bytes 7471104 | tf_op jit(solution)/shard_map/dot_general | solution.py:38
  123.8 48.8 %all-to-all-done = bf16[32,36,1024]{2,1,0:T(8,128)(2,1)} async-done(((bf16[32,36,1024]{2,1,0:T(8,128)(2,1)}), bf16[32,36,1024]{2,1,0:T(8,128)(2,1)}, u32[]{:S(2)}, u32[]{:S(2)}) %all-to-all-start) | async-done | bytes 2359328 | tf_op jit(solution)/shard_map/all_to_all | solution.py:77
  172.7 4.1 %reshape.85 = bf16[1152,1024]{1,0:T(8,128)(2,1)} reshape(bf16[32,36,1024]{2,1,0:T(8,128)(2,1)} %all-to-all-done) | data formatting | bytes 4718592 | tf_op jit(solution)/shard_map/reshape | solution.py:80
  176.8 5.0 %convolution_convert_fusion.2 = bf16[1024,384]{0,1:T(8,128)(2,1)} fusion(bf16[1152,1024]{1,0:T(8,128)(2,1)} %reshape.85, f32[1152,768]{0,1:T(8,128)} %fusion.2), kind=kOutput, calls=%fused_computation.19 | convolution fusion | flops 909017088 | bytes 6684672 | tf_op jit(solution)/shard_map/dot_general | solution.py:57
  181.8 1.8 multiply_convert_fusion.3
  183.6 2.2 convolution_convert_fusion.1
  185.8 3.5 %convolution_convert_fusion = bf16[1152,1024]{1,0:T(8,128)(2,1)} fusion(bf16[1,1024,768]{2,1,0:T(8,128)(2,1)S(1)} %copy-done, bf16[1152,384]{0,1:T(8,128)(2,1)S(1)} %get-tuple-element.13, bf16[1152,384]{0,1:T(8,128)(2,1)S(1)} %get-tuple-element.12), kind=kOutput, calls=%fused_computation.6 | convolution fusion | flops 1816657920 | bytes 5701632 | tf_op jit(solution)/shard_map/dot_general | solution.py:47
  189.3 4.1 %reshape.88 = bf16[32,36,1024]{2,1,0:T(8,128)(2,1)} reshape(bf16[1152,1024]{1,0:T(8,128)(2,1)} %convolution_convert_fusion) | data formatting | bytes 4718592 | tf_op jit(solution)/shard_map/reshape | solution.py:83
  193.3 6.8 %all-to-all-start.2 = ((bf16[32,36,1024]{2,1,0:T(8,128)(2,1)}), bf16[32,36,1024]{2,1,0:T(8,128)(2,1)}, u32[]{:S(2)}, u32[]{:S(2)}) async-start(bf16[32,36,1024]{2,1,0:T(8,128)(2,1)} %reshape.88), calls=%async_computation.2 | async-start | bytes 5242880 | tf_op jit(solution)/shard_map/all_to_all | solution.py:82
  200.4 2.8 pad_maximum_fusion
  203.3 4.3 %copy.27 = bf16[1024,1152]{1,0:T(8,128)(2,1)} copy(bf16[1024,1152]{0,1:T(8,128)(2,1)} %pad_maximum_fusion) | data formatting | bytes 4718592
  207.6 50.9 %all-to-all-done.2 = bf16[32,36,1024]{2,1,0:T(8,128)(2,1)} async-done(((bf16[32,36,1024]{2,1,0:T(8,128)(2,1)}), bf16[32,36,1024]{2,1,0:T(8,128)(2,1)}, u32[]{:S(2)}, u32[]{:S(2)}) %all-to-all-start.2) | async-done | bytes 2359328 | tf_op jit(solution)/shard_map/all_to_all | solution.py:82
  258.5 4.1 %reshape.89 = bf16[1152,1024]{1,0:T(8,128)(2,1)} reshape(bf16[32,36,1024]{2,1,0:T(8,128)(2,1)} %all-to-all-done.2) | data formatting | bytes 4718592 | tf_op jit(solution)/shard_map/reshape | solution.py:96
  262.6 8.0 %gather_fusion.3 = bf16[1024,1024]{1,0:T(8,128)(2,1)} fusion(bf16[1152,1024]{1,0:T(8,128)(2,1)} %reshape.89, s32[1024]{0:T(1024)S(1)} %broadcast_clamp_fusion), kind=kCustom, calls=%fused_computation.3 | custom fusion | bytes 4198400 | tf_op jit(solution)/shard_map/gather | solution.py:96
  270.6 3.7 %bitcast_reduce_fusion = bf16[128,1024]{1,0:T(8,128)(2,1)} fusion(bf16[1024,1024]{1,0:T(8,128)(2,1)} %gather_fusion.3), kind=kLoop, calls=%fused_computation.8 | loop fusion | flops 917504 | bytes 2359296 | tf_op jit(solution)/shard_map/reduce_sum | solution.py:97
  274.3 1.1 copy.28
  275.6 0.8 copy.25
  (43 shorter events, 2.4 us)
Async XLA Ops:
  7.2 110.9 %copy-start = (bf16[1,1024,768]{2,1,0:T(8,128)(2,1)S(1)}, bf16[1,1024,768]{2,1,0:T(8,128)(2,1)}, u32[]{:S(2)}) copy-start(bf16[1,1024,768]{2,1,0:T(8,128)(2,1)} %param.10) | copy-start | bytes 4718596
  33.2 14.0 %copy-start.4 = (f32[128,8]{0,1:T(8,128)S(1)}, f32[128,8]{0,1:T(8,128)}, u32[]{:S(2)}) copy-start(f32[128,8]{0,1:T(8,128)} %param.9) | copy-start | bytes 12292
  33.2 73.7 %all-to-all-start.1 = ((bf16[32,36,1024]{2,1,0:T(8,128)(2,1)}), bf16[32,36,1024]{2,1,0:T(8,128)(2,1)}, u32[]{:S(2)}, u32[]{:S(2)}) async-start(bf16[32,36,1024]{2,1,0:T(8,128)(2,1)} %reshape.86), calls=%async_computation.1 | async-start | bytes 5242880 | tf_op jit(solution)/shard_map/all_to_all | solution.py:76
  47.3 6.6 %copy-start.3 = (bf16[128,1024]{1,0:T(8,128)(2,1)S(1)}, bf16[128,1024]{1,0:T(8,128)(2,1)}, u32[]{:S(2)}) copy-start(bf16[128,1024]{1,0:T(8,128)(2,1)} %param.7) | copy-start | bytes 786436
  106.9 65.8 %all-to-all-start = ((bf16[32,36,1024]{2,1,0:T(8,128)(2,1)}), bf16[32,36,1024]{2,1,0:T(8,128)(2,1)}, u32[]{:S(2)}, u32[]{:S(2)}) async-start(bf16[32,36,1024]{2,1,0:T(8,128)(2,1)} %multiply_convert_fusion), calls=%async_computation | async-start | bytes 5242880 | tf_op jit(solution)/shard_map/all_to_all | solution.py:77
  176.8 5.0 %copy-start.2 = (bf16[1152,1024]{1,0:T(8,128)(2,1)S(1)}, bf16[1152,1024]{1,0:T(8,128)(2,1)}, u32[]{:S(2)}) copy-start(bf16[1152,1024]{1,0:T(8,128)(2,1)} %reshape.85) | copy-start | bytes 7077892
  176.8 5.0 %copy-start.5 = (bf16[1,1024,384]{2,1,0:T(8,128)(2,1)S(1)}, bf16[1,1024,384]{2,1,0:T(8,128)(2,1)}, u32[]{:S(2)}) copy-start(bf16[1,1024,384]{2,1,0:T(8,128)(2,1)} %param.11) | copy-start | bytes 2359300
  176.8 5.0 %copy-start.6 = (f32[1152,768]{0,1:T(8,128)S(1)}, f32[1152,768]{0,1:T(8,128)}, u32[]{:S(2)}) copy-start(f32[1152,768]{0,1:T(8,128)} %fusion.2) | copy-start | bytes 10616836
  181.8 1.8 copy-start.1
  193.3 65.2 %all-to-all-start.2 = ((bf16[32,36,1024]{2,1,0:T(8,128)(2,1)}), bf16[32,36,1024]{2,1,0:T(8,128)(2,1)}, u32[]{:S(2)}, u32[]{:S(2)}) async-start(bf16[32,36,1024]{2,1,0:T(8,128)(2,1)} %reshape.88), calls=%async_computation.2 | async-start | bytes 5242880 | tf_op jit(solution)/shard_map/all_to_all | solution.py:82
  200.2 74.2 %reduce-scatter.4.cloned.1.call-start = ((), (), s32[]{:S(2)}) async-start(), calls=%async_computation.4 | async-start | bytes 2506752
Sparse Core Ops, SparseCore 0:
  207.7 65.0 reduce-scatter.3
where the time goes:
time: 288 us; the launch traced here: 284 us
  waiting for transfers between devices  139 us (48%)
  local copies, waits for them, and re-layouts  63.8 us (22%)
  starting transfers between devices  28.1 us (10%)
  other arithmetic  21 us (7%)
  matrix products  18.2 us (6%)
  between operations  14.3 us (5%)
    all_to_all x1, waiting for transfers between devices, per_device(): lax.all_to_all(grad_rows.reshape(owners, capacity, width), 'expert', spli...  50.9 us
    all_to_all x1, waiting for transfers between devices, per_device(): lax.all_to_all(sent_grads, 'expert', split_axis=0, concat_axis=0, tiled=T...  48.8 us
    all_to_all x1, waiting for transfers between devices, per_device(): lax.all_to_all(sent_rows, 'expert', split_axis=0, concat_axis=0, tiled=True)  38.9 us
    all_to_all x1, starting transfers between devices, per_device(): lax.all_to_all(sent_rows, 'expert', split_axis=0, concat_axis=0, tiled=True)  14 us
    another operation x3, other arithmetic  9.15 us
    gather x1, local copies, waits for them, and re-layouts, per_device(): entries = returned.reshape(-1, width)[entry_pos]  8.03 us
    unnamed x20, local copies, waits for them, and re-layouts  7.95 us
    all_to_all x1, starting transfers between devices, per_device(): lax.all_to_all(sent_grads, 'expert', split_axis=0, concat_axis=0, tiled=T...  7.06 us
  transfers between devices with their start and end apart: 4, of which 3 were waited for; matrix products, arithmetic and copies ran while one was open for 19% of the time, Pallas kernels for 0%

commit v1 on v0

v1 whole, which is shorter than its diff:
```python
import functools

import jax
import jax.numpy as jnp
from jax import lax
from jax.experimental import pallas as pl
from jax.experimental.pallas import tpu as pltpu
from jax.sharding import Mesh, PartitionSpec as P

F32 = jnp.float32
BF16 = jnp.bfloat16
LANES = 128
CORES = 2
X_RING = 4


def params(limit=14):
    return pltpu.CompilerParams(vmem_limit_bytes=limit << 20)


def cost(flops, bytes_accessed):
    return pl.CostEstimate(flops=int(flops), bytes_accessed=int(bytes_accessed), transcendentals=0)


def place(top, part):
    row = lax.broadcasted_iota(jnp.int32, (top, LANES), 0)
    lane = lax.broadcasted_iota(jnp.int32, (top, LANES), 1)
    return (lane == row + part * top).astype(BF16)


def payload_kernel(x_ref, g_ref, routes_ref, probs_ref, out_ref):
    width = x_ref.shape[1]
    top = routes_ref.shape[1]
    out_ref[:, :width] = x_ref[...]
    out_ref[:, width : 2 * width] = g_ref[...]
    routes = routes_ref[...].astype(F32).astype(BF16)
    probs = probs_ref[...]
    high = probs.astype(BF16)
    rest = probs - high.astype(F32)
    middle = rest.astype(BF16)
    low = (rest - middle.astype(F32)).astype(BF16)
    info = jnp.zeros((x_ref.shape[0], LANES), F32)
    for part, piece in enumerate((routes, high, middle, low)):
        info += jnp.dot(piece, place(top, part), preferred_element_type=F32)
    out_ref[:, 2 * width :] = info.astype(BF16)


def payload(x_in, grad_out, routes, gate_probs):
    tokens, width = x_in.shape
    return pl.pallas_call(
        payload_kernel,
        out_shape=jax.ShapeDtypeStruct((tokens, 2 * width + LANES), BF16),
        compiler_params=params(),
        cost_estimate=cost(1e6, 8 * tokens * width),
        name="payload",
    )(x_in, grad_out, routes, gate_probs)


def pack_kernel(top, capacity, width, split, *refs):
    base_ref, refs = refs[0], refs[1:]
    out_ref, pick_ref = refs[-2:]
    refs = refs[:-2]
    rows = out_ref.shape[1]
    if split:
        joined = [jnp.concatenate([refs[-2][...], refs[-1][...]], axis=0)]
        blocks = [ref[...] for ref in refs[:-2]] + joined
    else:
        blocks = [ref[...] for ref in refs]
    tokens = blocks[0].shape[0]
    before = (
        lax.broadcasted_iota(jnp.int32, (tokens, tokens), 0)
        < lax.broadcasted_iota(jnp.int32, (tokens, tokens), 1)
    ).astype(BF16)
    slots = lax.broadcasted_iota(jnp.int32, (rows, tokens), 0).astype(F32)
    sublanes = lax.broadcasted_iota(jnp.int32, (8, tokens), 0)
    base = base_ref[0].astype(F32)
    weights = [jnp.zeros((rows, 1), F32) for _ in range(X_RING)]
    for index, block in enumerate(blocks):
        info = block[:, 2 * width :].astype(F32).T
        routes = info[:top]
        probs = info[top : 2 * top] + info[2 * top : 3 * top] + info[3 * top : 4 * top]
        masks = []
        chances = []
        stacked = jnp.zeros((8, tokens), F32)
        for expert in range(X_RING):
            same = routes == base + float(expert)
            mask = jnp.sum(jnp.where(same, 1.0, 0.0), axis=0, keepdims=True)
            masks.append(mask)
            chances.append(jnp.sum(jnp.where(same, probs, 0.0), axis=0, keepdims=True))
            stacked = jnp.where(sublanes == expert, mask, stacked)
        rank = jnp.dot(stacked.astype(BF16), before, preferred_element_type=F32)
        for expert in range(X_RING):
            where_to = jnp.where(
                masks[expert] > 0.0, rank[expert : expert + 1] + float(index * capacity), -1.0
            )
            hit = slots == where_to
            weights[expert] += jnp.sum(jnp.where(hit, chances[expert], 0.0), axis=1, keepdims=True)
            pick_ref[index, expert] = jnp.where(hit, 1.0, 0.0).astype(BF16)
    step = 512
    for expert in range(X_RING):
        for start in range(0, 2 * width, step):
            total = jnp.zeros((rows, step), F32)
            for index, block in enumerate(blocks):
                total += jnp.dot(
                    pick_ref[index, expert],
                    block[:, start : start + step],
                    preferred_element_type=F32,
                )
            if start >= width:
                total = total * weights[expert]
            out_ref[expert, :, start : start + step] = total.astype(BF16)


def pack(base, blocks, count, rows, top, capacity, width, split):
    tokens = blocks[0].shape[0]
    return pl.pallas_call(
        functools.partial(pack_kernel, top, capacity, width, split),
        out_shape=(
            jax.ShapeDtypeStruct((X_RING, rows, 2 * width), BF16),
            jax.ShapeDtypeStruct((count, X_RING, rows, tokens), BF16),
        ),
        in_specs=[pl.BlockSpec(memory_space=pltpu.SMEM)]
        + [pl.BlockSpec(memory_space=pltpu.VMEM)] * len(blocks),
        compiler_params=params(),
        cost_estimate=cost(
            16 * count * rows * tokens * width, 16 * rows * width + 4 * count * tokens * width
        ),
        name="pack",
    )(base, *blocks)


def expert_kernel(rows_ref, proj_ref, down_ref, back_ref, terms_ref):
    width = proj_ref.shape[0]
    hidden_units = down_ref.shape[1]
    projected = jnp.dot(rows_ref[:, :width], proj_ref[...], preferred_element_type=F32)
    grad_hidden = jnp.dot(rows_ref[:, width:], down_ref[...], preferred_element_type=F32)
    gate_pre = projected[:, :hidden_units]
    up_part = projected[:, hidden_units:]
    sigmoid_v = jax.nn.sigmoid(gate_pre)
    activated = gate_pre * sigmoid_v
    grad_gate = grad_hidden * up_part * sigmoid_v * (1.0 + gate_pre * (1.0 - sigmoid_v))
    terms_ref[:, :hidden_units] = grad_gate.astype(BF16)
    terms_ref[:, hidden_units : 2 * hidden_units] = (grad_hidden * activated).astype(BF16)
    terms_ref[:, 2 * hidden_units :] = (activated * up_part).astype(BF16)
    back_ref[...] = lax.dot_general(
        terms_ref[:, : 2 * hidden_units],
        proj_ref[...],
        (((1,), (1,)), ((), ())),
        preferred_element_type=F32,
    ).astype(BF16)


def expert_rows(rows_in, proj_weight, down_weight):
    count = rows_in.shape[0]
    width, hidden_units = down_weight.shape
    return pl.pallas_call(
        expert_kernel,
        out_shape=(
            jax.ShapeDtypeStruct((count, width), BF16),
            jax.ShapeDtypeStruct((count, 3 * hidden_units), BF16),
        ),
        compiler_params=params(),
        cost_estimate=cost(
            10 * count * width * hidden_units, 6 * width * hidden_units + 8 * count * width
        ),
        name="expert",
    )(rows_in, proj_weight, down_weight)


def weight_kernel(pairs, *refs):
    core_ref, refs = refs[0], refs[1:]
    keep_ref, send_ref, held = refs[-3:]
    share = held.shape[1]
    split = refs[2].shape[1] // 3 * 2
    block = refs[0].shape[1]
    first = jnp.zeros((block, split), F32)
    second = jnp.zeros((block, split // 2), F32)
    dims = (((0,), (0,)), ((), ()))
    for pair in range(pairs):
        x_ref, g_ref, terms_ref = refs[3 * pair : 3 * pair + 3]
        first += lax.dot_general(x_ref[...], terms_ref[:, :split], dims, preferred_element_type=F32)
        second += lax.dot_general(g_ref[...], terms_ref[:, split:], dims, preferred_element_type=F32)
    for part in range(held.shape[0]):
        held[part, :, :split] = first[part * share : (part + 1) * share]
        held[part, :, split:] = second[part * share : (part + 1) * share]
    core = core_ref[0]
    for pair in range(keep_ref.shape[0]):
        keep_ref[pair] = held[CORES * pair + core]
        send_ref[pair] = held[CORES * pair + (CORES - 1) - core].astype(BF16)


def weight_terms(core, row_list, term_list, width, owners):
    columns = term_list[0].shape[1]
    share = width // owners
    block = 256
    steps = width // block
    pieces = block // share
    operands = [core]
    specs = [pl.BlockSpec(memory_space=pltpu.SMEM)]
    total = 0
    for rows, terms in zip(row_list, term_list):
        count = rows.shape[0]
        total += count
        operands += [rows, rows, terms]
        specs += [
            pl.BlockSpec((count, block), lambda i: (0, i)),
            pl.BlockSpec((count, block), lambda i: (0, i + steps)),
            pl.BlockSpec((count, columns), lambda i: (0, 0)),
        ]
    result = pl.BlockSpec((pieces // CORES, share, columns), lambda i: (i, 0, 0))
    shape = (owners // CORES, share, columns)
    return pl.pallas_call(
        functools.partial(weight_kernel, len(row_list)),
        grid=(steps,),
        out_shape=(jax.ShapeDtypeStruct(shape, F32), jax.ShapeDtypeStruct(shape, BF16)),
        in_specs=specs,
        out_specs=(result, result),
        scratch_shapes=[pltpu.VMEM((pieces, share, columns), F32)],
        compiler_params=params(20),
        cost_estimate=cost(
            2 * total * width * columns, 2 * total * (2 * width + columns) + 3 * width * columns
        ),
        name="weight_terms",
    )(*operands)


def combine_kernel(rows_ref, pick_ref, *out_refs):
    for index, out_ref in enumerate(out_refs):
        total = jnp.zeros(out_ref.shape, F32)
        for expert in range(X_RING):
            total += lax.dot_general(
                pick_ref[index, expert],
                rows_ref[expert],
                (((0,), (0,)), ((), ())),
                preferred_element_type=F32,
            )
        out_ref[...] = total.astype(out_ref.dtype)


def combine(rows_back, picks):
    count, _, rows, tokens = picks.shape
    width = rows_back.shape[2]
    return pl.pallas_call(
        combine_kernel,
        out_shape=tuple(jax.ShapeDtypeStruct((tokens, width), BF16) for _ in range(count)),
        compiler_params=params(),
        cost_estimate=cost(
            8 * count * rows * tokens * width, 8 * rows * width + 2 * count * tokens * width
        ),
        name="combine",
    )(rows_back, picks)


def shift(value, size, by):
    return lax.ppermute(value, "z", [(i, (i + by) % size) for i in range(size)])


def per_device(x_in, grad_out, routes, gate_probs, gate_up, down):
    z_size = lax.axis_size("z")
    tokens, width = x_in.shape
    top = routes.shape[1]
    capacity = min(tokens, tokens * top * 9 // (8 * z_size * X_RING))
    proj_weight = gate_up[0]
    down_weight = down[0]
    base = (lax.axis_index("z") * X_RING).astype(jnp.int32).reshape(1)
    half = tokens // 2
    own = payload(x_in, grad_out, routes, gate_probs)

    def packed_group(blocks, count, split):
        rows = -(-capacity * count // 8) * 8
        return pack(base, blocks, count, rows, top, capacity, width, split)

    def crossed(value):
        return lax.all_to_all(value, "x", split_axis=0, concat_axis=0, tiled=True)

    fore1 = shift(own, z_size, 1)
    back1 = shift(own, z_size, -1)
    fore2 = shift(fore1, z_size, 1)
    back2 = shift(back1, z_size, -1)
    packed1, picks1 = packed_group([own, fore1, back1], 3, False)
    fore2, back2, packed1 = lax.optimization_barrier((fore2, back2, packed1))
    fore3 = shift(fore2, z_size, 1)
    back3 = shift(back2, z_size, -1)
    packed2, picks2 = packed_group([fore2, back2], 2, False)
    rows1 = crossed(packed1)
    fore3, back3, packed2, rows1 = lax.optimization_barrier((fore3, back3, packed2, rows1))
    fore4 = shift(fore3[:half], z_size, 1)
    back4 = shift(back3[half:], z_size, -1)

    def flat(value):
        return value.reshape(-1, value.shape[-1])

    def folded(value):
        return value.reshape(X_RING, -1, width)

    rows1 = flat(rows1)
    away1, terms1 = expert_rows(rows1, proj_weight, down_weight)
    rows2 = crossed(packed2)
    fore4, back4, rows2, away1 = lax.optimization_barrier((fore4, back4, rows2, away1))
    packed3, picks3 = packed_group([fore3, back3, fore4, back4], 3, True)
    rows2 = flat(rows2)
    away2, terms2 = expert_rows(rows2, proj_weight, down_weight)
    rows3 = crossed(packed3)
    rows3, away1, away2 = lax.optimization_barrier((rows3, away1, away2))
    home1 = crossed(folded(away1))
    rows3 = flat(rows3)
    away3, terms3 = expert_rows(rows3, proj_weight, down_weight)
    home1, away2, away3, terms3 = lax.optimization_barrier((home1, away2, away3, terms3))
    home2 = crossed(folded(away2))
    parts1 = combine(home1, picks1)
    home2, away3, terms3, *parts1 = lax.optimization_barrier((home2, away3, terms3, *parts1))
    home3 = crossed(folded(away3))
    parts2 = combine(home2, picks2)
    owners = lax.axis_size("y") * CORES
    core = lax.axis_index("c").astype(jnp.int32).reshape(1)
    keep, send = weight_terms(
        core, (rows1, rows2, rows3), (terms1, terms2, terms3), width, owners
    )
    home3, keep, send, *parts2 = lax.optimization_barrier((home3, keep, send, *parts2))
    parts3 = combine(home3, picks3)
    parts = (parts1, parts2, parts3)
    (part0, part_f1, part_b1), (part_f2, part_b2), (part_f3, part_b3, part4) = parts
    over = shift(part4[:half], z_size, 1)
    under = shift(part4[half:], z_size, -1)
    part_b3 = jnp.concatenate(
        [(part_b3[:half].astype(F32) + over.astype(F32)).astype(BF16), part_b3[half:]], 0
    )
    part_f3 = jnp.concatenate(
        [part_f3[:half], (part_f3[half:].astype(F32) + under.astype(F32)).astype(BF16)], 0
    )
    grad_in = part0.astype(F32)
    for part, by in (
        (part_f1, -1),
        (part_b1, 1),
        (part_f2, -2),
        (part_b2, 2),
        (part_f3, -3),
        (part_b3, 3),
    ):
        grad_in = grad_in + shift(part, z_size, by).astype(F32)
    grad_in = grad_in.astype(BF16)
    other = lax.ppermute(send, "c", [(0, 1), (1, 0)])
    pair = (keep + other.astype(F32)).astype(BF16)
    share = lax.psum_scatter(pair, "y", scatter_dimension=0, tiled=True).astype(F32)
    split = share.shape[2] // 3 * 2
    return (grad_in, share[:, :, :split], share[:, :, split:])


def solution(mesh):
    dp, experts = mesh.shape["dp"], mesh.shape["expert"]
    fine = Mesh(
        mesh.devices.reshape(dp // CORES, CORES, experts // X_RING, X_RING), ("y", "c", "z", "x")
    )
    placed = (P(("y", "c", "z", "x"), None),) * 4 + (P(("z", "x"), None, None),) * 2
    return jax.shard_map(
        per_device,
        mesh=fine,
        in_specs=placed,
        out_specs=(
            P(("y", "c", "z", "x"), None),
            P(("z", "x"), ("y", "c"), None),
            P(("z", "x"), ("y", "c"), None),
        ),
        check_vma=False,
    )
```

time: 288 us -> 253 us (0.88)
  waiting for transfers between devices: 139 us -> 70.4 us
  starting transfers between devices: 28.1 us -> 92.7 us
  Pallas kernels: 0 us -> 27.6 us
  local copies, waits for them, and re-layouts: 63.8 us -> 41.9 us
  matrix products: 18.2 us -> 0 us
  other arithmetic: 21 us -> 4.08 us
    all_to_all x3 -> x6, waiting for transfers between devices: 139 us -> 20.4 us  [crossed(): return lax.all_to_all(value, 'x', split_axis=0, concat_axis=0, tiled=True)]
    ppermute x0 -> x17, starting transfers between devices: none -> 68 us  [the longest x16 58.4 us: shift(): return lax.ppermute(value, 'z', [(i, (i + by) % size) for i in range(size)])]
    ppermute x0 -> x17, waiting for transfers between devices: none -> 50 us  [the longest x16 47.4 us: shift(): return lax.ppermute(value, 'z', [(i, (i + by) % size) for i in range(size)])]
    unnamed x20 -> x86, local copies, waits for them, and re-layouts: 7.95 us -> 36.8 us
    pallas_call x0 -> x11, Pallas kernels: none -> 27.6 us  [the longest x3 8.83 us: expert_rows(): pl.pallas_call(expert_kernel, out_shape=(jax.ShapeDtypeStruct((count, wid...]
    gather x4 -> x0, local copies, waits for them, and re-layouts: 24.5 us -> none  [the longest x1 8.03 us: per_device(): entries = returned.reshape(-1, width)[entry_pos]]
    reshape x6 -> x0, local copies, waits for them, and re-layouts: 20.5 us -> none  [the longest x1 4.11 us: per_device(): sent_rows = sent_rows.reshape(owners, capacity, width)]
    dot_general x5 -> x0, matrix products: 18.2 us -> none  [the longest x1 5.81 us: expert_rows(): jnp.dot(rows_in, proj_weight, preferred_element_type=jnp.float32)]
  transfers between devices with their start and end apart: 4 -> 24, of which waited for: 3 -> 14; matrix products, arithmetic and copies ran while one was open for 19% -> 1% of each run, Pallas kernels for 0% -> 10%
where the time goes in v1:
time: 253 us; the launch traced here: 251 us
  starting transfers between devices  92.7 us (37%)
  waiting for transfers between devices  70.4 us (28%)
  local copies, waits for them, and re-layouts  41.9 us (17%)
  Pallas kernels  27.6 us (11%)
  between operations  14.6 us (6%)
  other arithmetic  4.08 us (2%)
    ppermute x16, starting transfers between devices, shift(): return lax.ppermute(value, 'z', [(i, (i + by) % size) for i in range(size)])  58.4 us
    ppermute x16, waiting for transfers between devices, shift(): return lax.ppermute(value, 'z', [(i, (i + by) % size) for i in range(size)])  47.4 us
    unnamed x86, local copies, waits for them, and re-layouts  36.8 us
    all_to_all x6, starting transfers between devices, crossed(): return lax.all_to_all(value, 'x', split_axis=0, concat_axis=0, tiled=True)  24.6 us
    all_to_all x6, waiting for transfers between devices, crossed(): return lax.all_to_all(value, 'x', split_axis=0, concat_axis=0, tiled=True)  20.4 us
    ppermute x1, starting transfers between devices, per_device(): other = lax.ppermute(send, 'c', [(0, 1), (1, 0)])  9.52 us
    pallas_call x3, Pallas kernels, expert_rows(): pl.pallas_call(expert_kernel, out_shape=(jax.ShapeDtypeStruct((count, wid...  8.83 us
    pallas_call x1, Pallas kernels, weight_terms(): pl.pallas_call(functools.partial(weight_kernel, len(row_list)), grid=(ste...  6.62 us
  transfers between devices with their start and end apart: 24, of which 14 were waited for; matrix products, arithmetic and copies ran while one was open for 1% of the time, Pallas kernels for 10%

profile of v1, /device:TPU:1, one launch (start us, length us, event | category | flops | bytes accessed | tf_op | source)
XLA Modules:
  0.0 251.3 jit_solution(12662001380810912068)
XLA Ops:
  10.8 4.8 %collective-permute-start = (bf16[128,2176]{1,0:T(8,128)(2,1)S(1)}, bf16[128,2176]{1,0:T(8,128)(2,1)S(1)}, u32[]{:S(2)}, u32[]{:S(2)}) collective-permute-start(bf16[128,2176]{1,0:T(8,128)(2,1)S(1)} %payload.1.refs_1_), channel_id=1, source_target_pairs={{0,4},{4,8},{8,12},{12,16},{16,20},{20,24},{24,28},{28,0},{1,5},{5... | collective-permute-start | bytes 1671176 | tf_op jit(solution)/shard_map/ppermute | solution.py:255
  15.6 8.6 %collective-permute-start.2 = (bf16[128,2176]{1,0:T(8,128)(2,1)S(1)}, bf16[128,2176]{1,0:T(8,128)(2,1)S(1)}, u32[]{:S(2)}, u32[]{:S(2)}) collective-permute-start(bf16[128,2176]{1,0:T(8,128)(2,1)S(1)} %payload.1.refs_1_), channel_id=1, source_target_pairs={{0,28},{4,0},{8,4},{12,8},{16,12},{20,16},{24,20},{28,24},{1,29},{... | collective-permute-start | bytes 1671176 | tf_op jit(solution)/shard_map/ppermute | solution.py:255
  24.2 10.4 %collective-permute-done.refs_2_ = bf16[128,2176]{1,0:T(8,128)(2,1)S(1)} collective-permute-done((bf16[128,2176]{1,0:T(8,128)(2,1)S(1)}, bf16[128,2176]{1,0:T(8,128)(2,1)S(1)}, u32[]{:S(2)}, u32[]{:S(2)}) %collective-permute-start) | collective-permute-done | bytes 557088 | tf_op jit(solution)/shard_map/ppermute | solution.py:255
  36.6 4.6 %collective-permute-start.3 = (bf16[128,2176]{1,0:T(8,128)(2,1)S(1)}, bf16[128,2176]{1,0:T(8,128)(2,1)}, u32[]{:S(2)}, u32[]{:S(2)}) collective-permute-start(bf16[128,2176]{1,0:T(8,128)(2,1)S(1)} %collective-permute-done.2.refs_3_), channel_id=1, source_target_pairs={{0,28},{4,0},{8,4},{12,8},{16,12},{20,16},{24,20},{28,24},{1,29},{... | collective-permute-start | bytes 1671176 | tf_op jit(solution)/shard_map/ppermute | solution.py:255
  45.0 5.8 %collective-permute-done.1.refs_1_ = bf16[128,2176]{1,0:T(8,128)(2,1)} collective-permute-done((bf16[128,2176]{1,0:T(8,128)(2,1)S(1)}, bf16[128,2176]{1,0:T(8,128)(2,1)}, u32[]{:S(2)}, u32[]{:S(2)}) %collective-permute-start.1) | collective-permute-done | bytes 557088 | tf_op jit(solution)/shard_map/ppermute | solution.py:255
  51.6 4.0 %all-to-all-start = ((bf16[4,112,2048]{2,1,0:T(8,128)(2,1)}), bf16[4,112,2048]{2,1,0:T(8,128)(2,1)S(1)}, u32[]{:S(2)}, u32[]{:S(2)}) async-start(bf16[4,112,2048]{2,1,0:T(8,128)(2,1)} %copy-done.1), calls=%async_computation | async-start | bytes 3670016 | tf_op jit(solution)/shard_map/all_to_all | solution.py:274
  57.5 5.4 %collective-permute-start.5 = (bf16[128,2176]{1,0:T(8,128)(2,1)}, bf16[128,2176]{1,0:T(8,128)(2,1)S(1)}, u32[]{:S(2)}, u32[]{:S(2)}) collective-permute-start(bf16[128,2176]{1,0:T(8,128)(2,1)} %collective-permute-done.3.refs_2_), channel_id=1, source_target_pairs={{0,28},{4,0},{8,4},{12,8},{16,12},{20,16},{24,20},{28,24},{1,29},{... | collective-permute-start | bytes 1671176 | tf_op jit(solution)/shard_map/ppermute | solution.py:255
  62.9 2.3 pack.4
  66.2 5.2 %collective-permute-done.4.refs_1_ = bf16[128,2176]{1,0:T(8,128)(2,1)S(1)} collective-permute-done((bf16[128,2176]{1,0:T(8,128)(2,1)}, bf16[128,2176]{1,0:T(8,128)(2,1)S(1)}, u32[]{:S(2)}, u32[]{:S(2)}) %collective-permute-start.4) | collective-permute-done | bytes 557088 | tf_op jit(solution)/shard_map/ppermute | solution.py:255
  72.4 4.0 %all-to-all-done = bf16[4,112,2048]{2,1,0:T(8,128)(2,1)S(1)} async-done(((bf16[4,112,2048]{2,1,0:T(8,128)(2,1)}), bf16[4,112,2048]{2,1,0:T(8,128)(2,1)S(1)}, u32[]{:S(2)}, u32[]{:S(2)}) %all-to-all-start) | async-done | bytes 1835040 | tf_op jit(solution)/shard_map/all_to_all | solution.py:274
  76.4 3.5 %all-to-all-start.1 = ((bf16[4,72,2048]{2,1,0:T(8,128)(2,1)}), bf16[4,72,2048]{2,1,0:T(8,128)(2,1)S(1)}, u32[]{:S(2)}, u32[]{:S(2)}) async-start(bf16[4,72,2048]{2,1,0:T(8,128)(2,1)} %copy-done.3), calls=%async_computation.1 | async-start | bytes 2359296 | tf_op jit(solution)/shard_map/all_to_all | solution.py:274
  83.8 5.4 %collective-permute-start.7 = (bf16[64,2176]{1,0:T(8,128)(2,1)S(1)}, bf16[64,2176]{1,0:T(8,128)(2,1)S(1)}, u32[]{:S(2)}, u32[]{:S(2)}) collective-permute-start(bf16[64,2176]{1,0:T(8,128)(2,1)S(1)} %slice.31), channel_id=1, source_target_pairs={{0,28},{4,0},{8,4},{12,8},{16,12},{20,16},{24,20},{28,24},{1,29},{... | collective-permute-start | bytes 835592 | tf_op jit(solution)/shard_map/ppermute | solution.py:255
  91.8 2.7 %expert.3 = (bf16[448,1024]{1,0:T(8,128)(2,1)S(1)}, bf16[448,1152]{1,0:T(8,128)(2,1)S(1)}) custom-call(bf16[448,2048]{1,0:T(8,128)(2,1)S(1)} %bitcast.10, bf16[1024,768]{1,0:T(8,128)(2,1)S(1)} %bitcast.19, bf16[1024,384]{1,0:T(8,128)(2,1)S(1)} %bitcast.22), custom_call_target="tpu_custom_call" | custom-call | flops 1761607680 | bytes 6029312 | tf_op jit(solution)/shard_map/expert/pallas_call | solution.py:156
  105.7 4.4 %all-to-all-start.2 = ((bf16[4,112,2048]{2,1,0:T(8,128)(2,1)}), bf16[4,112,2048]{2,1,0:T(8,128)(2,1)}, u32[]{:S(2)}, u32[]{:S(2)}) async-start(bf16[4,112,2048]{2,1,0:T(8,128)(2,1)} %copy-done.2), calls=%async_computation.2 | async-start | bytes 3670016 | tf_op jit(solution)/shard_map/all_to_all | solution.py:274
  116.3 13.2 %all-to-all-done.2 = bf16[4,112,2048]{2,1,0:T(8,128)(2,1)} async-done(((bf16[4,112,2048]{2,1,0:T(8,128)(2,1)}), bf16[4,112,2048]{2,1,0:T(8,128)(2,1)}, u32[]{:S(2)}, u32[]{:S(2)}) %all-to-all-start.2) | async-done | bytes 1835040 | tf_op jit(solution)/shard_map/all_to_all | solution.py:274
  129.5 4.2 %all-to-all-start.3 = ((bf16[4,112,1024]{2,1,0:T(8,128)(2,1)}), bf16[4,112,1024]{2,1,0:T(8,128)(2,1)}, u32[]{:S(2)}, u32[]{:S(2)}) async-start(bf16[4,112,1024]{2,1,0:T(8,128)(2,1)} %bitcast.17), calls=%async_computation.3 | async-start | bytes 1835008 | tf_op jit(solution)/shard_map/all_to_all | solution.py:274
  136.3 4.2 %expert.5 = (bf16[448,1024]{1,0:T(8,128)(2,1)S(1)}, bf16[448,1152]{1,0:T(8,128)(2,1)S(1)}) custom-call(bf16[448,2048]{1,0:T(8,128)(2,1)} %bitcast.6.rows_ref.refs_7_.refs_8_, bf16[1024,768]{1,0:T(8,128)(2,1)S(1)} %bitcast.21, bf16[1024,384]{1,0:T(8,128)(2,1)S(1)} %bitcast.24), custom_call_target="tpu_custom_call" | custom-call | flops 1761607680 | bytes 6029312 | tf_op jit(solution)/shard_map/expert/pallas_call | solution.py:156
  142.8 4.1 %all-to-all-start.4 = ((bf16[4,72,1024]{2,1,0:T(8,128)(2,1)}), bf16[4,72,1024]{2,1,0:T(8,128)(2,1)}, u32[]{:S(2)}, u32[]{:S(2)}) async-start(bf16[4,72,1024]{2,1,0:T(8,128)(2,1)} %bitcast.18), calls=%async_computation.4 | async-start | bytes 1179648 | tf_op jit(solution)/shard_map/all_to_all | solution.py:274
  151.6 2.8 %all-to-all-done.4.rows_ref = bf16[4,72,1024]{2,1,0:T(8,128)(2,1)} async-done(((bf16[4,72,1024]{2,1,0:T(8,128)(2,1)}), bf16[4,72,1024]{2,1,0:T(8,128)(2,1)}, u32[]{:S(2)}, u32[]{:S(2)}) %all-to-all-start.4) | async-done | bytes 589856 | tf_op jit(solution)/shard_map/all_to_all | solution.py:274
  154.3 4.2 %all-to-all-start.5 = ((bf16[4,112,1024]{2,1,0:T(8,128)(2,1)}), bf16[4,112,1024]{2,1,0:T(8,128)(2,1)}, u32[]{:S(2)}, u32[]{:S(2)}) async-start(bf16[4,112,1024]{2,1,0:T(8,128)(2,1)} %bitcast.16), calls=%async_computation.5 | async-start | bytes 1835008 | tf_op jit(solution)/shard_map/all_to_all | solution.py:274
  165.5 6.6 %weight_terms.1 = (f32[8,64,1152]{2,1,0:T(8,128)S(1)}, bf16[8,64,1152]{2,1,0:T(8,128)(2,1)S(1)}) custom-call(s32[1]{0:T(128)} %bitcast.9.refs_0_, bf16[448,2048]{1,0:T(8,128)(2,1)S(1)} %bitcast.11, bf16[448,2048]{1,0:T(8,128)(2,1)S(1)} %bitcast.12, bf16[448,1152]{1,0:T(8,128)(2,1)S(1)} %copy-done.5, bf16[288,2048]{1,0:T(8,128)(2,1)S(1)} %bitcast.14, ...), custom_call_target="tpu_custom_call" | custom-call | flops 2793406464 | bytes 11116544 | tf_op jit(solution)/shard_map/weight_terms/pallas_call | solution.py:212
  174.6 9.5 %collective-permute-start.16 = (bf16[8,64,1152]{2,1,0:T(8,128)(2,1)}, bf16[8,64,1152]{2,1,0:T(8,128)(2,1)S(1)}, u32[]{:S(2)}, u32[]{:S(2)}) collective-permute-start(bf16[8,64,1152]{2,1,0:T(8,128)(2,1)} %copy-done.22), channel_id=1, source_target_pairs={{0,32},{32,0},{1,33},{33,1},{2,34},{34,2},{3,35},{35,3},{4,36},{36... | collective-permute-start | bytes 3538952 | tf_op jit(solution)/shard_map/ppermute | solution.py:342
  184.1 2.7 %collective-permute-done.16 = bf16[8,64,1152]{2,1,0:T(8,128)(2,1)S(1)} collective-permute-done((bf16[8,64,1152]{2,1,0:T(8,128)(2,1)}, bf16[8,64,1152]{2,1,0:T(8,128)(2,1)S(1)}, u32[]{:S(2)}, u32[]{:S(2)}) %collective-permute-start.16) | collective-permute-done | bytes 1179680 | tf_op jit(solution)/shard_map/ppermute | solution.py:342
  186.8 3.0 %add_convert_fusion = bf16[8,64,1152]{2,1,0:T(8,128)(2,1)} fusion(f32[8,64,1152]{2,1,0:T(8,128)} %copy-done, bf16[8,64,1152]{2,1,0:T(8,128)(2,1)S(1)} %collective-permute-done.16), kind=kLoop, calls=%fused_computation | loop fusion | flops 1769472 | bytes 4718592 | tf_op jit(solution)/shard_map/convert_element_type | solution.py:343
  192.1 3.4 %collective-permute-start.12 = (bf16[64,1024]{1,0:T(8,128)(2,1)S(1)}, bf16[64,1024]{1,0:T(8,128)(2,1)S(1)}, u32[]{:S(2)}, u32[]{:S(2)}) collective-permute-start(bf16[64,1024]{1,0:T(8,128)(2,1)S(1)} %get-tuple-element.105), channel_id=1, source_target_pairs={{0,28},{4,0},{8,4},{12,8},{16,12},{20,16},{24,20},{28,24},{1,29},{... | collective-permute-start | bytes 393224 | tf_op jit(solution)/shard_map/ppermute | solution.py:255
  197.4 3.4 %collective-permute-start.9 = (bf16[128,1024]{1,0:T(8,128)(2,1)S(1)}, bf16[128,1024]{1,0:T(8,128)(2,1)S(1)}, u32[]{:S(2)}, u32[]{:S(2)}) collective-permute-start(bf16[128,1024]{1,0:T(8,128)(2,1)S(1)} %copy-done.31), channel_id=1, source_target_pairs={{0,4},{4,8},{8,12},{12,16},{16,20},{20,24},{24,28},{28,0},{1,5},{5... | collective-permute-start | bytes 786440 | tf_op jit(solution)/shard_map/ppermute | solution.py:255
  202.8 4.3 %collective-permute-start.10 = (bf16[128,1024]{1,0:T(8,128)(2,1)S(1)}, bf16[128,1024]{1,0:T(8,128)(2,1)S(1)}, u32[]{:S(2)}, u32[]{:S(2)}) collective-permute-start(bf16[128,1024]{1,0:T(8,128)(2,1)S(1)} %copy-done.37), channel_id=1, source_target_pairs={{0,24},{4,28},{8,0},{12,4},{16,8},{20,12},{24,16},{28,20},{1,25},{... | collective-permute-start | bytes 786440 | tf_op jit(solution)/shard_map/ppermute | solution.py:255
  210.2 3.2 %collective-permute-start.13 = (bf16[128,1024]{1,0:T(8,128)(2,1)S(1)}, bf16[128,1024]{1,0:T(8,128)(2,1)S(1)}, u32[]{:S(2)}, u32[]{:S(2)}) collective-permute-start(bf16[128,1024]{1,0:T(8,128)(2,1)S(1)} %pad_maximum_fusion), channel_id=1, source_target_pairs={{0,20},{4,24},{8,28},{12,0},{16,4},{20,8},{24,12},{28,16},{1,21},{... | collective-permute-start | bytes 786440 | tf_op jit(solution)/shard_map/ppermute | solution.py:255
  213.5 3.9 %collective-permute-start.15 = (bf16[128,1024]{1,0:T(8,128)(2,1)S(1)}, bf16[128,1024]{1,0:T(8,128)(2,1)S(1)}, u32[]{:S(2)}, u32[]{:S(2)}) collective-permute-start(bf16[128,1024]{1,0:T(8,128)(2,1)S(1)} %pad_maximum_fusion.1), channel_id=1, source_target_pairs={{0,12},{4,16},{8,20},{12,24},{16,28},{20,0},{24,4},{28,8},{1,13},{... | collective-permute-start | bytes 786440 | tf_op jit(solution)/shard_map/ppermute | solution.py:255
  217.4 4.3 %collective-permute-done.10 = bf16[128,1024]{1,0:T(8,128)(2,1)S(1)} collective-permute-done((bf16[128,1024]{1,0:T(8,128)(2,1)S(1)}, bf16[128,1024]{1,0:T(8,128)(2,1)S(1)}, u32[]{:S(2)}, u32[]{:S(2)}) %collective-permute-start.10) | collective-permute-done | bytes 262176 | tf_op jit(solution)/shard_map/ppermute | solution.py:255
  221.7 12.0 %collective-permute-done.13 = bf16[128,1024]{1,0:T(8,128)(2,1)S(1)} collective-permute-done((bf16[128,1024]{1,0:T(8,128)(2,1)S(1)}, bf16[128,1024]{1,0:T(8,128)(2,1)S(1)}, u32[]{:S(2)}, u32[]{:S(2)}) %collective-permute-start.13) | collective-permute-done | bytes 262176 | tf_op jit(solution)/shard_map/ppermute | solution.py:255
  233.7 6.7 %collective-permute-done.15 = bf16[128,1024]{1,0:T(8,128)(2,1)S(1)} collective-permute-done((bf16[128,1024]{1,0:T(8,128)(2,1)S(1)}, bf16[128,1024]{1,0:T(8,128)(2,1)S(1)}, u32[]{:S(2)}, u32[]{:S(2)}) %collective-permute-start.15) | collective-permute-done | bytes 262176 | tf_op jit(solution)/shard_map/ppermute | solution.py:255
  (127 shorter events, 69.9 us)
Async XLA Ops:
  10.8 23.8 %collective-permute-start = (bf16[128,2176]{1,0:T(8,128)(2,1)S(1)}, bf16[128,2176]{1,0:T(8,128)(2,1)S(1)}, u32[]{:S(2)}, u32[]{:S(2)}) collective-permute-start(bf16[128,2176]{1,0:T(8,128)(2,1)S(1)} %payload.1.refs_1_), channel_id=1, source_target_pairs={{0,4},{4,8},{8,12},{12,16},{16,20},{20,24},{24,28},{28,0},{1,5},{5... | collective-permute-start | bytes 1671176 | tf_op jit(solution)/shard_map/ppermute | solution.py:255
  15.6 20.9 %collective-permute-start.2 = (bf16[128,2176]{1,0:T(8,128)(2,1)S(1)}, bf16[128,2176]{1,0:T(8,128)(2,1)S(1)}, u32[]{:S(2)}, u32[]{:S(2)}) collective-permute-start(bf16[128,2176]{1,0:T(8,128)(2,1)S(1)} %payload.1.refs_1_), channel_id=1, source_target_pairs={{0,28},{4,0},{8,4},{12,8},{16,12},{20,16},{24,20},{28,24},{1,29},{... | collective-permute-start | bytes 1671176 | tf_op jit(solution)/shard_map/ppermute | solution.py:255
  34.7 16.1 %collective-permute-start.1 = (bf16[128,2176]{1,0:T(8,128)(2,1)S(1)}, bf16[128,2176]{1,0:T(8,128)(2,1)}, u32[]{:S(2)}, u32[]{:S(2)}) collective-permute-start(bf16[128,2176]{1,0:T(8,128)(2,1)S(1)} %collective-permute-done.refs_2_), channel_id=1, source_target_pairs={{0,4},{4,8},{8,12},{12,16},{16,20},{20,24},{24,28},{28,0},{1,5},{5... | collective-permute-start | bytes 1671176 | tf_op jit(solution)/shard_map/ppermute | solution.py:255
  36.6 15.0 %collective-permute-start.3 = (bf16[128,2176]{1,0:T(8,128)(2,1)S(1)}, bf16[128,2176]{1,0:T(8,128)(2,1)}, u32[]{:S(2)}, u32[]{:S(2)}) collective-permute-start(bf16[128,2176]{1,0:T(8,128)(2,1)S(1)} %collective-permute-done.2.refs_3_), channel_id=1, source_target_pairs={{0,28},{4,0},{8,4},{12,8},{16,12},{20,16},{24,20},{28,24},{1,29},{... | collective-permute-start | bytes 1671176 | tf_op jit(solution)/shard_map/ppermute | solution.py:255
  51.6 24.9 %all-to-all-start = ((bf16[4,112,2048]{2,1,0:T(8,128)(2,1)}), bf16[4,112,2048]{2,1,0:T(8,128)(2,1)S(1)}, u32[]{:S(2)}, u32[]{:S(2)}) async-start(bf16[4,112,2048]{2,1,0:T(8,128)(2,1)} %copy-done.1), calls=%async_computation | async-start | bytes 3670016 | tf_op jit(solution)/shard_map/all_to_all | solution.py:274
  55.6 15.8 %collective-permute-start.4 = (bf16[128,2176]{1,0:T(8,128)(2,1)}, bf16[128,2176]{1,0:T(8,128)(2,1)S(1)}, u32[]{:S(2)}, u32[]{:S(2)}) collective-permute-start(bf16[128,2176]{1,0:T(8,128)(2,1)} %collective-permute-done.1.refs_1_), channel_id=1, source_target_pairs={{0,4},{4,8},{8,12},{12,16},{16,20},{20,24},{24,28},{28,0},{1,5},{5... | collective-permute-start | bytes 1671176 | tf_op jit(solution)/shard_map/ppermute | solution.py:255
  57.5 14.9 %collective-permute-start.5 = (bf16[128,2176]{1,0:T(8,128)(2,1)}, bf16[128,2176]{1,0:T(8,128)(2,1)S(1)}, u32[]{:S(2)}, u32[]{:S(2)}) collective-permute-start(bf16[128,2176]{1,0:T(8,128)(2,1)} %collective-permute-done.3.refs_2_), channel_id=1, source_target_pairs={{0,28},{4,0},{8,4},{12,8},{16,12},{20,16},{24,20},{28,24},{1,29},{... | collective-permute-start | bytes 1671176 | tf_op jit(solution)/shard_map/ppermute | solution.py:255
  71.4 5.0 %copy-start.15 = (bf16[128,2176]{1,0:T(8,128)(2,1)}, bf16[128,2176]{1,0:T(8,128)(2,1)S(1)}, u32[]{:S(2)}) copy-start(bf16[128,2176]{1,0:T(8,128)(2,1)S(1)} %collective-permute-done.4.refs_1_) | copy-start | bytes 1671172
  72.4 4.0 %copy-start.17 = (bf16[128,2176]{1,0:T(8,128)(2,1)}, bf16[128,2176]{1,0:T(8,128)(2,1)S(1)}, u32[]{:S(2)}) copy-start(bf16[128,2176]{1,0:T(8,128)(2,1)S(1)} %collective-permute-done.5.refs_2_) | copy-start | bytes 1671172
  76.4 21.5 %all-to-all-start.1 = ((bf16[4,72,2048]{2,1,0:T(8,128)(2,1)}), bf16[4,72,2048]{2,1,0:T(8,128)(2,1)S(1)}, u32[]{:S(2)}, u32[]{:S(2)}) async-start(bf16[4,72,2048]{2,1,0:T(8,128)(2,1)} %copy-done.3), calls=%async_computation.1 | async-start | bytes 2359296 | tf_op jit(solution)/shard_map/all_to_all | solution.py:274
  80.9 15.5 %collective-permute-start.6 = (bf16[64,2176]{1,0:T(8,128)(2,1)S(1)}, bf16[64,2176]{1,0:T(8,128)(2,1)S(1)}, u32[]{:S(2)}, u32[]{:S(2)}) collective-permute-start(bf16[64,2176]{1,0:T(8,128)(2,1)S(1)} %slice.30), channel_id=1, source_target_pairs={{0,4},{4,8},{8,12},{12,16},{16,20},{20,24},{24,28},{28,0},{1,5},{5... | collective-permute-start | bytes 835592 | tf_op jit(solution)/shard_map/ppermute | solution.py:255
  83.8 13.4 %collective-permute-start.7 = (bf16[64,2176]{1,0:T(8,128)(2,1)S(1)}, bf16[64,2176]{1,0:T(8,128)(2,1)S(1)}, u32[]{:S(2)}, u32[]{:S(2)}) collective-permute-start(bf16[64,2176]{1,0:T(8,128)(2,1)S(1)} %slice.31), channel_id=1, source_target_pairs={{0,28},{4,0},{8,4},{12,8},{16,12},{20,16},{24,20},{28,24},{1,29},{... | collective-permute-start | bytes 835592 | tf_op jit(solution)/shard_map/ppermute | solution.py:255
  89.3 1.4 copy-start.19
  105.7 23.8 %all-to-all-start.2 = ((bf16[4,112,2048]{2,1,0:T(8,128)(2,1)}), bf16[4,112,2048]{2,1,0:T(8,128)(2,1)}, u32[]{:S(2)}, u32[]{:S(2)}) async-start(bf16[4,112,2048]{2,1,0:T(8,128)(2,1)} %copy-done.2), calls=%async_computation.2 | async-start | bytes 3670016 | tf_op jit(solution)/shard_map/all_to_all | solution.py:274
  129.5 13.3 %all-to-all-start.3 = ((bf16[4,112,1024]{2,1,0:T(8,128)(2,1)}), bf16[4,112,1024]{2,1,0:T(8,128)(2,1)}, u32[]{:S(2)}, u32[]{:S(2)}) async-start(bf16[4,112,1024]{2,1,0:T(8,128)(2,1)} %bitcast.17), calls=%async_computation.3 | async-start | bytes 1835008 | tf_op jit(solution)/shard_map/all_to_all | solution.py:274
  142.8 11.5 %all-to-all-start.4 = ((bf16[4,72,1024]{2,1,0:T(8,128)(2,1)}), bf16[4,72,1024]{2,1,0:T(8,128)(2,1)}, u32[]{:S(2)}, u32[]{:S(2)}) async-start(bf16[4,72,1024]{2,1,0:T(8,128)(2,1)} %bitcast.18), calls=%async_computation.4 | async-start | bytes 1179648 | tf_op jit(solution)/shard_map/all_to_all | solution.py:274
  154.3 20.3 %all-to-all-start.5 = ((bf16[4,112,1024]{2,1,0:T(8,128)(2,1)}), bf16[4,112,1024]{2,1,0:T(8,128)(2,1)}, u32[]{:S(2)}, u32[]{:S(2)}) async-start(bf16[4,112,1024]{2,1,0:T(8,128)(2,1)} %bitcast.16), calls=%async_computation.5 | async-start | bytes 1835008 | tf_op jit(solution)/shard_map/all_to_all | solution.py:274
  158.6 82.9 %reduce-scatter.2.cloned.1.call-start = ((), (), s32[]{:S(2)}) async-start(), calls=%async_computation.7 | async-start | bytes 1327104 | tf_op jit(solution)/shard_map/reduce_scatter | solution.py:344
  174.6 15.2 %copy-start.41 = (bf16[3,4,112,128]{3,2,1,0:T(8,128)(2,1)S(1)}, bf16[3,4,112,128]{3,2,1,0:T(8,128)(2,1)}, u32[]{:S(2)}) copy-start(bf16[3,4,112,128]{3,2,1,0:T(8,128)(2,1)} %copy-done.40) | copy-start | bytes 1032196
  174.6 12.2 %collective-permute-start.16 = (bf16[8,64,1152]{2,1,0:T(8,128)(2,1)}, bf16[8,64,1152]{2,1,0:T(8,128)(2,1)S(1)}, u32[]{:S(2)}, u32[]{:S(2)}) collective-permute-start(bf16[8,64,1152]{2,1,0:T(8,128)(2,1)} %copy-done.22), channel_id=1, source_target_pairs={{0,32},{32,0},{1,33},{33,1},{2,34},{34,2},{3,35},{35,3},{4,36},{36... | collective-permute-start | bytes 3538952 | tf_op jit(solution)/shard_map/ppermute | solution.py:342
  189.8 5.7 %copy-start.33 = (bf16[128,1024]{1,0:T(8,128)(2,1)S(1)}, bf16[128,1024]{1,0:T(8,128)(2,1)}, u32[]{:S(2)}) copy-start(bf16[128,1024]{1,0:T(8,128)(2,1)} %copy-done.32) | copy-start | bytes 786436
  189.8 7.6 %copy-start.31 = (bf16[128,1024]{1,0:T(8,128)(2,1)S(1)}, bf16[128,1024]{1,0:T(8,128)(2,1)}, u32[]{:S(2)}) copy-start(bf16[128,1024]{1,0:T(8,128)(2,1)} %copy-done.30) | copy-start | bytes 786436
  189.8 13.0 %copy-start.37 = (bf16[128,1024]{1,0:T(8,128)(2,1)S(1)}, bf16[128,1024]{1,0:T(8,128)(2,1)}, u32[]{:S(2)}) copy-start(bf16[128,1024]{1,0:T(8,128)(2,1)} %copy-done.36) | copy-start | bytes 786436
  189.8 17.3 %copy-start.35 = (bf16[128,1024]{1,0:T(8,128)(2,1)S(1)}, bf16[128,1024]{1,0:T(8,128)(2,1)}, u32[]{:S(2)}) copy-start(bf16[128,1024]{1,0:T(8,128)(2,1)} %copy-done.34) | copy-start | bytes 786436
  192.1 15.0 %collective-permute-start.12 = (bf16[64,1024]{1,0:T(8,128)(2,1)S(1)}, bf16[64,1024]{1,0:T(8,128)(2,1)S(1)}, u32[]{:S(2)}, u32[]{:S(2)}) collective-permute-start(bf16[64,1024]{1,0:T(8,128)(2,1)S(1)} %get-tuple-element.105), channel_id=1, source_target_pairs={{0,28},{4,0},{8,4},{12,8},{16,12},{20,16},{24,20},{28,24},{1,29},{... | collective-permute-start | bytes 393224 | tf_op jit(solution)/shard_map/ppermute | solution.py:255
  195.5 18.0 %collective-permute-start.8 = (bf16[128,1024]{1,0:T(8,128)(2,1)S(1)}, bf16[128,1024]{1,0:T(8,128)(2,1)S(1)}, u32[]{:S(2)}, u32[]{:S(2)}) collective-permute-start(bf16[128,1024]{1,0:T(8,128)(2,1)S(1)} %copy-done.33), channel_id=1, source_target_pairs={{0,28},{4,0},{8,4},{12,8},{16,12},{20,16},{24,20},{28,24},{1,29},{... | collective-permute-start | bytes 786440 | tf_op jit(solution)/shard_map/ppermute | solution.py:255
  197.4 20.0 %collective-permute-start.9 = (bf16[128,1024]{1,0:T(8,128)(2,1)S(1)}, bf16[128,1024]{1,0:T(8,128)(2,1)S(1)}, u32[]{:S(2)}, u32[]{:S(2)}) collective-permute-start(bf16[128,1024]{1,0:T(8,128)(2,1)S(1)} %copy-done.31), channel_id=1, source_target_pairs={{0,4},{4,8},{8,12},{12,16},{16,20},{20,24},{24,28},{28,0},{1,5},{5... | collective-permute-start | bytes 786440 | tf_op jit(solution)/shard_map/ppermute | solution.py:255
  200.8 9.4 %collective-permute-start.14 = (bf16[64,1024]{1,0:T(8,128)(2,1)S(1)}, bf16[64,1024]{1,0:T(8,128)(2,1)S(1)}, u32[]{:S(2)}, u32[]{:S(2)}) collective-permute-start(bf16[64,1024]{1,0:T(8,128)(2,1)S(1)} %get-tuple-element.106), channel_id=1, source_target_pairs={{0,4},{4,8},{8,12},{12,16},{16,20},{20,24},{24,28},{28,0},{1,5},{5... | collective-permute-start | bytes 393224 | tf_op jit(solution)/shard_map/ppermute | solution.py:255
  202.8 19.0 %collective-permute-start.10 = (bf16[128,1024]{1,0:T(8,128)(2,1)S(1)}, bf16[128,1024]{1,0:T(8,128)(2,1)S(1)}, u32[]{:S(2)}, u32[]{:S(2)}) collective-permute-start(bf16[128,1024]{1,0:T(8,128)(2,1)S(1)} %copy-done.37), channel_id=1, source_target_pairs={{0,24},{4,28},{8,0},{12,4},{16,8},{20,12},{24,16},{28,20},{1,25},{... | collective-permute-start | bytes 786440 | tf_op jit(solution)/shard_map/ppermute | solution.py:255
  207.1 14.6 %collective-permute-start.11 = (bf16[128,1024]{1,0:T(8,128)(2,1)S(1)}, bf16[128,1024]{1,0:T(8,128)(2,1)S(1)}, u32[]{:S(2)}, u32[]{:S(2)}) collective-permute-start(bf16[128,1024]{1,0:T(8,128)(2,1)S(1)} %copy-done.35), channel_id=1, source_target_pairs={{0,8},{4,12},{8,16},{12,20},{16,24},{20,28},{24,0},{28,4},{1,9},{5... | collective-permute-start | bytes 786440 | tf_op jit(solution)/shard_map/ppermute | solution.py:255
  210.2 23.5 %collective-permute-start.13 = (bf16[128,1024]{1,0:T(8,128)(2,1)S(1)}, bf16[128,1024]{1,0:T(8,128)(2,1)S(1)}, u32[]{:S(2)}, u32[]{:S(2)}) collective-permute-start(bf16[128,1024]{1,0:T(8,128)(2,1)S(1)} %pad_maximum_fusion), channel_id=1, source_target_pairs={{0,20},{4,24},{8,28},{12,0},{16,4},{20,8},{24,12},{28,16},{1,21},{... | collective-permute-start | bytes 786440 | tf_op jit(solution)/shard_map/ppermute | solution.py:255
  213.5 27.0 %collective-permute-start.15 = (bf16[128,1024]{1,0:T(8,128)(2,1)S(1)}, bf16[128,1024]{1,0:T(8,128)(2,1)S(1)}, u32[]{:S(2)}, u32[]{:S(2)}) collective-permute-start(bf16[128,1024]{1,0:T(8,128)(2,1)S(1)} %pad_maximum_fusion.1), channel_id=1, source_target_pairs={{0,12},{4,16},{8,20},{12,24},{16,28},{20,0},{24,4},{28,8},{1,13},{... | collective-permute-start | bytes 786440 | tf_op jit(solution)/shard_map/ppermute | solution.py:255
  (34 other events, 33.9 us)
Sparse Core Ops, SparseCore 0:
  189.9 35.0 reduce-scatter.1

commit v2 on v1

v2 whole, which is shorter than its diff:
```python
import functools

import jax
import jax.numpy as jnp
from jax import lax
from jax.experimental import pallas as pl
from jax.experimental.pallas import tpu as pltpu
from jax.sharding import Mesh, PartitionSpec as P

F32 = jnp.float32
BF16 = jnp.bfloat16
LANES = 128
CORES = 2
X_RING = 4
IN_HBM = pl.BlockSpec(memory_space=pltpu.HBM)
IN_SMEM = pl.BlockSpec(memory_space=pltpu.SMEM)
DMA = pltpu.SemaphoreType.DMA


def params(limit=14):
    return pltpu.CompilerParams(vmem_limit_bytes=limit << 20)


def in_hbm(value):
    return pltpu.with_memory_space_constraint(value, pltpu.HBM)


def cost(flops, bytes_accessed):
    return pl.CostEstimate(flops=int(flops), bytes_accessed=int(bytes_accessed), transcendentals=0)


def started(source, target, semaphore):
    copy = pltpu.make_async_copy(source, target, semaphore)
    copy.start()
    return copy


def place(top, part):
    row = lax.broadcasted_iota(jnp.int32, (top, LANES), 0)
    lane = lax.broadcasted_iota(jnp.int32, (top, LANES), 1)
    return (lane == row + part * top).astype(BF16)


def payload_kernel(g_ref, routes_ref, probs_ref, out_ref, routes_in, probs_in, made, sems):
    width = g_ref.shape[1]
    top = routes_ref.shape[1]
    routes_copy = started(routes_ref, routes_in, sems.at[0])
    probs_copy = started(probs_ref, probs_in, sems.at[1])
    g_copy = started(g_ref, made.at[:, pl.ds(0, width)], sems.at[2])
    routes_copy.wait()
    probs_copy.wait()
    routes = routes_in[...].astype(F32).astype(BF16)
    probs = probs_in[...]
    high = probs.astype(BF16)
    rest = probs - high.astype(F32)
    middle = rest.astype(BF16)
    low = (rest - middle.astype(F32)).astype(BF16)
    info = jnp.zeros((g_ref.shape[0], LANES), F32)
    for part, piece in enumerate((routes, high, middle, low)):
        info += jnp.dot(piece, place(top, part), preferred_element_type=F32)
    made[:, width:] = info.astype(BF16)
    g_copy.wait()
    started(made, out_ref, sems.at[3]).wait()


def payload(grad_out, routes, gate_probs):
    tokens, width = grad_out.shape
    top = routes.shape[1]
    return pl.pallas_call(
        payload_kernel,
        out_shape=pltpu.HBM((tokens, width + LANES), BF16),
        in_specs=[IN_HBM] * 3,
        out_specs=IN_HBM,
        scratch_shapes=[
            pltpu.VMEM((tokens, top), jnp.int32),
            pltpu.VMEM((tokens, top), F32),
            pltpu.VMEM((tokens, width + LANES), BF16),
            DMA((4,)),
        ],
        compiler_params=params(8),
        cost_estimate=cost(1e6, 4 * tokens * width),
        name="payload",
    )(in_hbm(grad_out), in_hbm(routes), in_hbm(gate_probs))


def pack_kernel(top, capacity, *refs):
    base_ref, refs = refs[0], refs[1:]
    out_ref, x_in, g_in, pick, made, x_sems, g_sems, out_sems = refs[-8:]
    count = (len(refs) - 8) // 2
    tokens, width = refs[0].shape
    rows = out_ref.shape[1]
    g_copies = [
        started(refs[count + b], g_in.at[pl.ds(b * tokens, tokens)], g_sems.at[b])
        for b in range(count)
    ]
    x_copies = [
        started(refs[b], x_in.at[pl.ds(b * tokens, tokens)], x_sems.at[b]) for b in range(count)
    ]
    before = (
        lax.broadcasted_iota(jnp.int32, (tokens, tokens), 0)
        < lax.broadcasted_iota(jnp.int32, (tokens, tokens), 1)
    ).astype(BF16)
    slots = lax.broadcasted_iota(jnp.int32, (rows, tokens), 0).astype(F32)
    sublanes = lax.broadcasted_iota(jnp.int32, (8, tokens), 0)
    base = base_ref[0].astype(F32)
    weights = [jnp.zeros((rows, 1), F32) for _ in range(X_RING)]
    for b in range(count):
        g_copies[b].wait()
        info = g_in[b * tokens : (b + 1) * tokens, width:].astype(F32).T
        routes = info[:top]
        probs = info[top : 2 * top] + info[2 * top : 3 * top] + info[3 * top : 4 * top]
        masks = []
        chances = []
        stacked = jnp.zeros((8, tokens), F32)
        for expert in range(X_RING):
            same = routes == base + float(expert)
            mask = jnp.sum(jnp.where(same, 1.0, 0.0), axis=0, keepdims=True)
            masks.append(mask)
            chances.append(jnp.sum(jnp.where(same, probs, 0.0), axis=0, keepdims=True))
            stacked = jnp.where(sublanes == expert, mask, stacked)
        rank = jnp.dot(stacked.astype(BF16), before, preferred_element_type=F32)
        for expert in range(X_RING):
            where_to = jnp.where(
                masks[expert] > 0.0, rank[expert : expert + 1] + float(b * capacity), -1.0
            )
            hit = slots == where_to
            weights[expert] += jnp.sum(jnp.where(hit, chances[expert], 0.0), axis=1, keepdims=True)
            pick[expert, :, b * tokens : (b + 1) * tokens] = jnp.where(hit, 1.0, 0.0).astype(BF16)
    for copy in x_copies:
        copy.wait()
    step = 512
    out_copies = []
    for expert in range(X_RING):
        for start in range(0, width, step):
            made[expert, :, start : start + step] = jnp.dot(
                pick[expert], x_in[:, start : start + step], preferred_element_type=F32
            ).astype(BF16)
        for start in range(0, width, step):
            total = jnp.dot(
                pick[expert], g_in[:, start : start + step], preferred_element_type=F32
            )
            made[expert, :, width + start : width + start + step] = (
                total * weights[expert]
            ).astype(BF16)
        out_copies.append(started(made.at[expert], out_ref.at[expert], out_sems.at[expert]))
    for copy in out_copies:
        copy.wait()


def pack(base, x_blocks, g_blocks, top, capacity):
    count = len(x_blocks)
    tokens, width = x_blocks[0].shape
    rows = -(-capacity * count // 8) * 8
    return pl.pallas_call(
        functools.partial(pack_kernel, top, capacity),
        out_shape=pltpu.HBM((X_RING, rows, 2 * width), BF16),
        in_specs=[IN_SMEM] + [pl.BlockSpec(memory_space=pl.ANY)] * (2 * count),
        out_specs=IN_HBM,
        scratch_shapes=[
            pltpu.VMEM((count * tokens, width), BF16),
            pltpu.VMEM((count * tokens, width + LANES), BF16),
            pltpu.VMEM((X_RING, rows, count * tokens), BF16),
            pltpu.VMEM((X_RING, rows, 2 * width), BF16),
            DMA((count,)),
            DMA((count,)),
            DMA((X_RING,)),
        ],
        compiler_params=params(16),
        cost_estimate=cost(
            16 * count * rows * tokens * width, 16 * rows * width + 4 * count * tokens * width
        ),
        name="pack",
    )(base, *x_blocks, *g_blocks)


def expert_kernel(capacity, slot_rows, *refs):
    place_ref, rows_ref, proj_ref, down_ref = refs[:4]
    away_ref, terms_ref = refs[-10:-8]
    rows_in, proj_in, down_in, terms, back, made, in_sems, out_sems = refs[-8:]
    width, hidden_units = down_ref.shape
    count = rows_ref.shape[0]
    per_x = count // X_RING
    blocks = place_ref.shape[0]
    copies = [
        started(rows_ref, rows_in, in_sems.at[0]),
        started(proj_ref, proj_in, in_sems.at[1]),
        started(down_ref, down_in, in_sems.at[2]),
    ]
    for copy in copies:
        copy.wait()
    projected = jnp.dot(rows_in[:, :width], proj_in[...], preferred_element_type=F32)
    grad_hidden = jnp.dot(rows_in[:, width:], down_in[...], preferred_element_type=F32)
    gate_pre = projected[:, :hidden_units]
    up_part = projected[:, hidden_units:]
    sigmoid_v = jax.nn.sigmoid(gate_pre)
    activated = gate_pre * sigmoid_v
    grad_gate = grad_hidden * up_part * sigmoid_v * (1.0 + gate_pre * (1.0 - sigmoid_v))
    terms[:, :hidden_units] = grad_gate.astype(BF16)
    terms[:, hidden_units : 2 * hidden_units] = (grad_hidden * activated).astype(BF16)
    terms[:, 2 * hidden_units :] = (activated * up_part).astype(BF16)
    terms_copy = started(terms, terms_ref, in_sems.at[3])
    back[count:] = jnp.zeros((back.shape[0] - count, width), F32)
    back[:count] = lax.dot_general(
        terms[:, : 2 * hidden_units],
        proj_in[...],
        (((1,), (1,)), ((), ())),
        preferred_element_type=F32,
    )
    out_copies = []
    for column in range(X_RING):
        for b in range(blocks):
            first = column * per_x + b * capacity
            slot = column * blocks + b
            made[slot] = back[first : first + slot_rows].astype(BF16)
            out_copies.append(
                started(made.at[slot], away_ref.at[place_ref[b] + column], out_sems.at[slot])
            )
    terms_copy.wait()
    for copy in out_copies:
        copy.wait()


def expert_rows(places, rows_in, proj_weight, down_weight, capacity, slot_rows, owners, away):
    count = rows_in.shape[0]
    width, hidden_units = down_weight.shape
    blocks = places.shape[0]
    operands = [places, rows_in, proj_weight, down_weight]
    aliases = {}
    if away is not None:
        operands.append(away)
        aliases = {4: 0}
    return pl.pallas_call(
        functools.partial(expert_kernel, capacity, slot_rows),
        out_shape=(
            pltpu.HBM((owners, slot_rows, width), BF16),
            pltpu.HBM((count, 3 * hidden_units), BF16),
        ),
        in_specs=[IN_SMEM] + [IN_HBM] * (len(operands) - 1),
        out_specs=(IN_HBM, IN_HBM),
        scratch_shapes=[
            pltpu.VMEM((count, 2 * width), BF16),
            pltpu.VMEM((width, 2 * hidden_units), BF16),
            pltpu.VMEM((width, hidden_units), BF16),
            pltpu.VMEM((count, 3 * hidden_units), BF16),
            pltpu.VMEM((count + 8, width), F32),
            pltpu.VMEM((X_RING * blocks, slot_rows, width), BF16),
            DMA((4,)),
            DMA((X_RING * blocks,)),
        ],
        input_output_aliases=aliases,
        compiler_params=params(32),
        cost_estimate=cost(
            10 * count * width * hidden_units, 6 * width * hidden_units + 8 * count * width
        ),
        name="expert",
    )(operands[0], *map(in_hbm, operands[1:]))


def weight_kernel(pairs, *refs):
    core_ref, refs = refs[0], refs[1:]
    keep_ref, send_ref, held = refs[-3:]
    share = held.shape[1]
    split = refs[2].shape[1] // 3 * 2
    block = refs[0].shape[1]
    first = jnp.zeros((block, split), F32)
    second = jnp.zeros((block, split // 2), F32)
    dims = (((0,), (0,)), ((), ()))
    for pair in range(pairs):
        x_ref, g_ref, terms_ref = refs[3 * pair : 3 * pair + 3]
        first += lax.dot_general(x_ref[...], terms_ref[:, :split], dims, preferred_element_type=F32)
        second += lax.dot_general(g_ref[...], terms_ref[:, split:], dims, preferred_element_type=F32)
    for part in range(held.shape[0]):
        held[part, :, :split] = first[part * share : (part + 1) * share]
        held[part, :, split:] = second[part * share : (part + 1) * share]
    core = core_ref[0]
    for pair in range(keep_ref.shape[0]):
        keep_ref[pair] = held[CORES * pair + core]
        send_ref[pair] = held[CORES * pair + (CORES - 1) - core].astype(BF16)


def weight_terms(core, row_list, term_list, width, owners):
    columns = term_list[0].shape[1]
    share = width // owners
    block = 256
    steps = width // block
    pieces = block // share
    operands = [core]
    specs = [pl.BlockSpec(memory_space=pltpu.SMEM)]
    total = 0
    for rows, terms in zip(row_list, term_list):
        count = rows.shape[0]
        total += count
        operands += [rows, rows, terms]
        specs += [
            pl.BlockSpec((count, block), lambda i: (0, i)),
            pl.BlockSpec((count, block), lambda i: (0, i + steps)),
            pl.BlockSpec((count, columns), lambda i: (0, 0)),
        ]
    result = pl.BlockSpec((pieces // CORES, share, columns), lambda i: (i, 0, 0))
    shape = (owners // CORES, share, columns)
    return pl.pallas_call(
        functools.partial(weight_kernel, len(row_list)),
        grid=(steps,),
        out_shape=(jax.ShapeDtypeStruct(shape, F32), jax.ShapeDtypeStruct(shape, BF16)),
        in_specs=specs,
        out_specs=(result, result),
        scratch_shapes=[pltpu.VMEM((pieces, share, columns), F32)],
        compiler_params=params(20),
        cost_estimate=cost(
            2 * total * width * columns, 2 * total * (2 * width + columns) + 3 * width * columns
        ),
        name="weight_terms",
    )(*operands)


def combine_kernel(experts, routes_ref, rows_ref, out_ref, routes_in, rows_in, made, sems):
    tokens, top = routes_ref.shape
    total_rows = rows_ref.shape[0]
    slot_rows = total_rows // experts
    routes_copy = started(routes_ref, routes_in, sems.at[0])
    rows_copy = started(rows_ref, rows_in, sems.at[1])
    routes_copy.wait()
    lanes = lax.broadcasted_iota(jnp.int32, (tokens, experts), 1)
    mask = jnp.zeros((tokens, experts), F32)
    for entry in range(top):
        mask += jnp.where(routes_in[:, entry : entry + 1] == lanes, 1.0, 0.0)
    before = (
        lax.broadcasted_iota(jnp.int32, (tokens, tokens), 1)
        < lax.broadcasted_iota(jnp.int32, (tokens, tokens), 0)
    ).astype(BF16)
    rank = jnp.dot(before, mask.astype(BF16), preferred_element_type=F32)
    row = lax.broadcasted_iota(jnp.int32, (experts, total_rows), 0)
    lane = lax.broadcasted_iota(jnp.int32, (experts, total_rows), 1)
    offset = lane - row * slot_rows
    inside = (offset >= 0) & (offset < slot_rows)
    spread = jnp.where(inside, 1.0, 0.0).astype(BF16)
    wanted = jnp.sum(jnp.where(inside, offset.astype(F32), 0.0), axis=0, keepdims=True)
    held = jnp.dot(
        jnp.where(mask > 0.0, rank, -1.0).astype(BF16), spread, preferred_element_type=F32
    )
    pick = jnp.where(held == wanted, 1.0, 0.0).astype(BF16)
    rows_copy.wait()
    made[...] = jnp.dot(pick, rows_in[...], preferred_element_type=F32).astype(BF16)
    started(made, out_ref, sems.at[2]).wait()


def combine(routes, rows_back, experts):
    tokens, top = routes.shape
    total_rows, width = rows_back.shape
    return pl.pallas_call(
        functools.partial(combine_kernel, experts),
        out_shape=pltpu.HBM((tokens, width), BF16),
        in_specs=[IN_HBM] * 2,
        out_specs=IN_HBM,
        scratch_shapes=[
            pltpu.VMEM((tokens, top), jnp.int32),
            pltpu.VMEM((total_rows, width), BF16),
            pltpu.VMEM((tokens, width), BF16),
            DMA((3,)),
        ],
        compiler_params=params(16),
        cost_estimate=cost(2 * tokens * total_rows * width, 2 * (total_rows + tokens) * width),
        name="combine",
    )(in_hbm(routes), in_hbm(rows_back))


def per_device(x_in, grad_out, routes, gate_probs, gate_up, down):
    z_size = lax.axis_size("z")
    experts = z_size * X_RING
    tokens, width = x_in.shape
    top = routes.shape[1]
    capacity = min(tokens, tokens * top * 9 // (8 * experts))
    slot_rows = -(-capacity // 8) * 8
    proj_weight = gate_up[0]
    down_weight = down[0]
    z_index = lax.axis_index("z")
    core = lax.axis_index("c")
    base = (z_index * X_RING).astype(jnp.int32).reshape(1)
    turn = [(i, (i + 1) % z_size) for i in range(z_size)]
    turn += [(z_size + i, z_size + (i - 1) % z_size) for i in range(z_size)]

    def onward(value):
        return lax.ppermute(value, ("c", "z"), turn)

    def crossed(value):
        return lax.all_to_all(value, "x", split_axis=0, concat_axis=0, tiled=True)

    def arrive(packed):
        return crossed(packed).reshape(-1, 2 * width)

    half = z_size // 2
    xs = [x_in]
    gs = [payload(grad_out, routes, gate_probs)]
    for _ in range(half):
        xs.append(onward(xs[-1]))
        gs.append(onward(gs[-1]))
    packed = pack(base, xs[:half], gs[:half], top, capacity)
    xs[half], gs[half], packed = lax.optimization_barrier((xs[half], gs[half], packed))
    rows1 = arrive(packed)
    for _ in range(half + 1, z_size):
        xs.append(onward(xs[-1]))
        gs.append(onward(gs[-1]))
    xs[-1], gs[-1], rows1 = lax.optimization_barrier((xs[-1], gs[-1], rows1))
    rows2 = arrive(pack(base, xs[half:], gs[half:], top, capacity))
    steps = jnp.arange(z_size, dtype=jnp.int32)
    places = jnp.where(core == 0, z_index - steps, z_index + steps) % z_size * X_RING
    places = places.astype(jnp.int32)
    run = functools.partial(
        expert_rows,
        proj_weight=proj_weight,
        down_weight=down_weight,
        capacity=capacity,
        slot_rows=slot_rows,
        owners=experts,
    )
    away, terms1 = run(places[:half], rows1, away=None)
    rows2, away = lax.optimization_barrier((rows2, away))
    away, terms2 = run(places[half:], rows2, away=away)
    away, terms2 = lax.optimization_barrier((away, terms2))
    home = lax.all_to_all(away, ("z", "x"), split_axis=0, concat_axis=0, tiled=True)
    owners = lax.axis_size("y") * CORES
    keep, send = weight_terms(
        core.astype(jnp.int32).reshape(1), (rows1, rows2), (terms1, terms2), width, owners
    )
    other = lax.ppermute(send, "c", [(0, 1), (1, 0)])
    pair = (keep + other.astype(F32)).astype(BF16)
    share = lax.psum_scatter(pair, "y", scatter_dimension=0, tiled=True)
    home, pair = lax.optimization_barrier((home, pair))
    grad_in = combine(routes, home.reshape(-1, width), experts)
    share, grad_in = lax.optimization_barrier((share, grad_in))
    share = share.astype(F32)
    split = share.shape[2] // 3 * 2
    return (grad_in, share[:, :, :split], share[:, :, split:])


def solution(mesh):
    dp, experts = mesh.shape["dp"], mesh.shape["expert"]
    fine = Mesh(
        mesh.devices.reshape(dp // CORES, CORES, experts // X_RING, X_RING), ("y", "c", "z", "x")
    )
    placed = (P(("y", "c", "z", "x"), None),) * 4 + (P(("z", "x"), None, None),) * 2
    return jax.shard_map(
        per_device,
        mesh=fine,
        in_specs=placed,
        out_specs=(
            P(("y", "c", "z", "x"), None),
            P(("z", "x"), ("y", "c"), None),
            P(("z", "x"), ("y", "c"), None),
        ),
        check_vma=False,
    )
```

time: 253 us -> 215 us (0.85); the launches traced: 251 us -> 210 us
  local copies, waits for them, and re-layouts: 41.9 us -> 16.5 us
  starting transfers between devices: 92.7 us -> 80.6 us
  waiting for transfers between devices: 70.4 us -> 62.2 us
  Pallas kernels: 27.6 us -> 35.4 us
  other arithmetic: 4.08 us -> 1.31 us
    ppermute x16 -> x14, waiting for transfers between devices: 47.4 us -> 11.1 us  [onward(): return lax.ppermute(value, ('c', 'z'), turn)]
    all_to_all x0 -> x1, waiting for transfers between devices: none -> 31.7 us  [per_device(): lax.all_to_all(away, ('z', 'x'), split_axis=0, concat_axis=0, tiled=True)]
    unnamed x86 -> x30, local copies, waits for them, and re-layouts: 36.8 us -> 13.4 us
    all_to_all x6 -> x2, starting transfers between devices: 24.6 us -> 8.59 us  [crossed(): return lax.all_to_all(value, 'x', split_axis=0, concat_axis=0, tiled=True)]
    pallas_call x10 -> x6, Pallas kernels: 21 us -> 28.8 us  [the longest x2 15.7 us: expert_rows(): pl.pallas_call(functools.partial(expert_kernel, capacity, slot_rows), out...]
    all_to_all x6 -> x2, waiting for transfers between devices: 20.4 us -> 13.1 us  [crossed(): return lax.all_to_all(value, 'x', split_axis=0, concat_axis=0, tiled=True)]
    all_to_all x0 -> x1, starting transfers between devices: none -> 6.86 us  [per_device(): lax.all_to_all(away, ('z', 'x'), split_axis=0, concat_axis=0, tiled=True)]
    reduce_scatter x1, waiting for transfers between devices: 0.01 us -> 3.89 us  [per_device(): share = lax.psum_scatter(pair, 'y', scatter_dimension=0, tiled=True)]
  transfers between devices with their start and end apart: 24 -> 19, of which waited for: 14 -> 10; matrix products, arithmetic and copies ran while one was open for 1% -> 1% of each run, Pallas kernels for 10% -> 10%
where the time goes in v2:
time: 215 us; the launch traced here: 210 us
  starting transfers between devices  80.6 us (37%)
  waiting for transfers between devices  62.2 us (29%)
  Pallas kernels  35.4 us (16%)
  local copies, waits for them, and re-layouts  16.5 us (8%)
  between operations  14.4 us (7%)
    ppermute x14, starting transfers between devices, onward(): return lax.ppermute(value, ('c', 'z'), turn)  55.8 us
    all_to_all x1, waiting for transfers between devices, per_device(): lax.all_to_all(away, ('z', 'x'), split_axis=0, concat_axis=0, tiled=True)  31.7 us
    pallas_call x2, Pallas kernels, expert_rows(): pl.pallas_call(functools.partial(expert_kernel, capacity, slot_rows), out...  15.7 us
    unnamed x30, local copies, waits for them, and re-layouts  13.4 us
    all_to_all x2, waiting for transfers between devices, crossed(): return lax.all_to_all(value, 'x', split_axis=0, concat_axis=0, tiled=True)  13.1 us
    ppermute x14, waiting for transfers between devices, onward(): return lax.ppermute(value, ('c', 'z'), turn)  11.1 us
    ppermute x1, starting transfers between devices, per_device(): other = lax.ppermute(send, 'c', [(0, 1), (1, 0)])  9.35 us
    all_to_all x2, starting transfers between devices, crossed(): return lax.all_to_all(value, 'x', split_axis=0, concat_axis=0, tiled=True)  8.59 us
  transfers between devices with their start and end apart: 19, of which 10 were waited for; matrix products, arithmetic and copies ran while one was open for 1% of the time, Pallas kernels for 10%

profile of v2, /device:TPU:1, one launch (start us, length us, event | category | flops | bytes accessed | tf_op | source)
XLA Modules:
  0.0 210.5 jit_solution(2496726053461553548)
XLA Ops:
  10.0 1.8 payload.1.refs_5_
  11.8 11.5 %collective-permute-start.4 = (bf16[128,1152]{1,0:T(8,128)(2,1)}, bf16[128,1152]{1,0:T(8,128)(2,1)S(1)}, u32[]{:S(2)}, u32[]{:S(2)}) collective-permute-start(bf16[128,1152]{1,0:T(8,128)(2,1)} %payload.1.refs_5_), channel_id=1, source_target_pairs={{0,4},{4,8},{8,12},{12,16},{16,20},{20,24},{24,28},{28,0},{32,60},... | collective-permute-start | bytes 884744 | tf_op jit(solution)/shard_map/ppermute | solution.py:383
  23.3 2.2 %collective-permute-start = (bf16[128,1024]{1,0:T(8,128)(2,1)}, bf16[128,1024]{1,0:T(8,128)(2,1)S(1)}, u32[]{:S(2)}, u32[]{:S(2)}) collective-permute-start(bf16[128,1024]{1,0:T(8,128)(2,1)} %refs_1_.1), channel_id=1, source_target_pairs={{0,4},{4,8},{8,12},{12,16},{16,20},{20,24},{24,28},{28,0},{32,60},... | collective-permute-start | bytes 786440 | tf_op jit(solution)/shard_map/ppermute | solution.py:383
  25.5 1.8 collective-permute-done.4.refs_6_
  27.3 4.9 %collective-permute-start.5 = (bf16[128,1152]{1,0:T(8,128)(2,1)S(1)}, bf16[128,1152]{1,0:T(8,128)(2,1)S(1)}, u32[]{:S(2)}, u32[]{:S(2)}) collective-permute-start(bf16[128,1152]{1,0:T(8,128)(2,1)S(1)} %collective-permute-done.4.refs_6_), channel_id=1, source_target_pairs={{0,4},{4,8},{8,12},{12,16},{16,20},{20,24},{24,28},{28,0},{32,60},... | collective-permute-start | bytes 884744 | tf_op jit(solution)/shard_map/ppermute | solution.py:383
  32.2 2.8 %collective-permute-start.1 = (bf16[128,1024]{1,0:T(8,128)(2,1)S(1)}, bf16[128,1024]{1,0:T(8,128)(2,1)S(1)}, u32[]{:S(2)}, u32[]{:S(2)}) collective-permute-start(bf16[128,1024]{1,0:T(8,128)(2,1)S(1)} %collective-permute-done.refs_2_), channel_id=1, source_target_pairs={{0,4},{4,8},{8,12},{12,16},{16,20},{20,24},{24,28},{28,0},{32,60},... | collective-permute-start | bytes 786440 | tf_op jit(solution)/shard_map/ppermute | solution.py:383
  35.8 5.0 %collective-permute-start.6 = (bf16[128,1152]{1,0:T(8,128)(2,1)S(1)}, bf16[128,1152]{1,0:T(8,128)(2,1)S(1)}, u32[]{:S(2)}, u32[]{:S(2)}) collective-permute-start(bf16[128,1152]{1,0:T(8,128)(2,1)S(1)} %collective-permute-done.5.refs_7_), channel_id=1, source_target_pairs={{0,4},{4,8},{8,12},{12,16},{16,20},{20,24},{24,28},{28,0},{32,60},... | collective-permute-start | bytes 884744 | tf_op jit(solution)/shard_map/ppermute | solution.py:383
  40.8 2.8 %collective-permute-start.2 = (bf16[128,1024]{1,0:T(8,128)(2,1)S(1)}, bf16[128,1024]{1,0:T(8,128)(2,1)S(1)}, u32[]{:S(2)}, u32[]{:S(2)}) collective-permute-start(bf16[128,1024]{1,0:T(8,128)(2,1)S(1)} %collective-permute-done.1.refs_3_), channel_id=1, source_target_pairs={{0,4},{4,8},{8,12},{12,16},{16,20},{20,24},{24,28},{28,0},{32,60},... | collective-permute-start | bytes 786440 | tf_op jit(solution)/shard_map/ppermute | solution.py:383
  44.5 5.0 %collective-permute-start.7 = (bf16[128,1152]{1,0:T(8,128)(2,1)S(1)}, bf16[128,1152]{1,0:T(8,128)(2,1)S(1)}, u32[]{:S(2)}, u32[]{:S(2)}) collective-permute-start(bf16[128,1152]{1,0:T(8,128)(2,1)S(1)} %collective-permute-done.6.refs_8_), channel_id=1, source_target_pairs={{0,4},{4,8},{8,12},{12,16},{16,20},{20,24},{24,28},{28,0},{32,60},... | collective-permute-start | bytes 884744 | tf_op jit(solution)/shard_map/ppermute | solution.py:383
  49.5 2.8 %collective-permute-start.3 = (bf16[128,1024]{1,0:T(8,128)(2,1)S(1)}, bf16[128,1024]{1,0:T(8,128)(2,1)S(1)}, u32[]{:S(2)}, u32[]{:S(2)}) collective-permute-start(bf16[128,1024]{1,0:T(8,128)(2,1)S(1)} %collective-permute-done.2.refs_4_), channel_id=1, source_target_pairs={{0,4},{4,8},{8,12},{12,16},{16,20},{20,24},{24,28},{28,0},{32,60},... | collective-permute-start | bytes 786440 | tf_op jit(solution)/shard_map/ppermute | solution.py:383
  54.2 4.1 %pack.2 = bf16[4,144,2048]{2,1,0:T(8,128)(2,1)} custom-call(s32[1]{0:T(128)} %bitcast.1.refs_0_, bf16[128,1024]{1,0:T(8,128)(2,1)S(1)} %copy-done.5, bf16[128,1024]{1,0:T(8,128)(2,1)S(1)} %collective-permute-done.refs_2_, bf16[128,1024]{1,0:T(8,128)(2,1)S(1)} %collective-permute-done.1.refs_3_, bf16[128,1024]{1,0:T(8,128)(2,1)S(1)} %collective-permute-done.2.refs_4_, ...), custom_call_target="tpu_custom_call" | custom-call | flops 1207959552 | bytes 4456448 | tf_op jit(solution)/shard_map/pack/pallas_call | solution.py:154
  58.4 4.0 %all-to-all-start = ((bf16[4,144,2048]{2,1,0:T(8,128)(2,1)}), bf16[4,144,2048]{2,1,0:T(8,128)(2,1)S(1)}, u32[]{:S(2)}, u32[]{:S(2)}) async-start(bf16[4,144,2048]{2,1,0:T(8,128)(2,1)} %pack.2), calls=%async_computation | async-start | bytes 4718592 | tf_op jit(solution)/shard_map/all_to_all | solution.py:386
  62.4 2.6 %collective-permute-start.11 = (bf16[128,1152]{1,0:T(8,128)(2,1)S(1)}, bf16[128,1152]{1,0:T(8,128)(2,1)S(1)}, u32[]{:S(2)}, u32[]{:S(2)}) collective-permute-start(bf16[128,1152]{1,0:T(8,128)(2,1)S(1)} %collective-permute-done.7.refs_5_), channel_id=1, source_target_pairs={{0,4},{4,8},{8,12},{12,16},{16,20},{20,24},{24,28},{28,0},{32,60},... | collective-permute-start | bytes 884744 | tf_op jit(solution)/shard_map/ppermute | solution.py:383
  65.0 1.9 collective-permute-start.8
  66.9 3.2 %collective-permute-done.11.refs_6_ = bf16[128,1152]{1,0:T(8,128)(2,1)S(1)} collective-permute-done((bf16[128,1152]{1,0:T(8,128)(2,1)S(1)}, bf16[128,1152]{1,0:T(8,128)(2,1)S(1)}, u32[]{:S(2)}, u32[]{:S(2)}) %collective-permute-start.11) | collective-permute-done | bytes 294944 | tf_op jit(solution)/shard_map/ppermute | solution.py:383
  70.2 3.8 %collective-permute-start.12 = (bf16[128,1152]{1,0:T(8,128)(2,1)S(1)}, bf16[128,1152]{1,0:T(8,128)(2,1)S(1)}, u32[]{:S(2)}, u32[]{:S(2)}) collective-permute-start(bf16[128,1152]{1,0:T(8,128)(2,1)S(1)} %collective-permute-done.11.refs_6_), channel_id=1, source_target_pairs={{0,4},{4,8},{8,12},{12,16},{16,20},{20,24},{24,28},{28,0},{32,60},... | collective-permute-start | bytes 884744 | tf_op jit(solution)/shard_map/ppermute | solution.py:383
  74.0 2.8 %collective-permute-start.9 = (bf16[128,1024]{1,0:T(8,128)(2,1)S(1)}, bf16[128,1024]{1,0:T(8,128)(2,1)S(1)}, u32[]{:S(2)}, u32[]{:S(2)}) collective-permute-start(bf16[128,1024]{1,0:T(8,128)(2,1)S(1)} %collective-permute-done.8.refs_2_), channel_id=1, source_target_pairs={{0,4},{4,8},{8,12},{12,16},{16,20},{20,24},{24,28},{28,0},{32,60},... | collective-permute-start | bytes 786440 | tf_op jit(solution)/shard_map/ppermute | solution.py:383
  77.9 5.0 %collective-permute-start.13 = (bf16[128,1152]{1,0:T(8,128)(2,1)S(1)}, bf16[128,1152]{1,0:T(8,128)(2,1)S(1)}, u32[]{:S(2)}, u32[]{:S(2)}) collective-permute-start(bf16[128,1152]{1,0:T(8,128)(2,1)S(1)} %collective-permute-done.12.refs_7_), channel_id=1, source_target_pairs={{0,4},{4,8},{8,12},{12,16},{16,20},{20,24},{24,28},{28,0},{32,60},... | collective-permute-start | bytes 884744 | tf_op jit(solution)/shard_map/ppermute | solution.py:383
  82.9 2.8 %collective-permute-start.10 = (bf16[128,1024]{1,0:T(8,128)(2,1)S(1)}, bf16[128,1024]{1,0:T(8,128)(2,1)S(1)}, u32[]{:S(2)}, u32[]{:S(2)}) collective-permute-start(bf16[128,1024]{1,0:T(8,128)(2,1)S(1)} %collective-permute-done.9.refs_3_), channel_id=1, source_target_pairs={{0,4},{4,8},{8,12},{12,16},{16,20},{20,24},{24,28},{28,0},{32,60},... | collective-permute-start | bytes 786440 | tf_op jit(solution)/shard_map/ppermute | solution.py:383
  86.4 3.9 %collective-permute-done.10.refs_4_ = bf16[128,1024]{1,0:T(8,128)(2,1)S(1)} collective-permute-done((bf16[128,1024]{1,0:T(8,128)(2,1)S(1)}, bf16[128,1024]{1,0:T(8,128)(2,1)S(1)}, u32[]{:S(2)}, u32[]{:S(2)}) %collective-permute-start.10) | collective-permute-done | bytes 262176 | tf_op jit(solution)/shard_map/ppermute | solution.py:383
  95.0 4.1 %pack.3 = bf16[4,144,2048]{2,1,0:T(8,128)(2,1)} custom-call(s32[1]{0:T(128)} %bitcast.1.refs_0_, bf16[128,1024]{1,0:T(8,128)(2,1)S(1)} %copy-done.7, bf16[128,1024]{1,0:T(8,128)(2,1)S(1)} %copy-done.9, bf16[128,1024]{1,0:T(8,128)(2,1)S(1)} %copy-done.11, bf16[128,1024]{1,0:T(8,128)(2,1)S(1)} %copy-done.13, ...), custom_call_target="tpu_custom_call" | custom-call | flops 1207959552 | bytes 4456448 | tf_op jit(solution)/shard_map/pack/pallas_call | solution.py:154
  99.2 4.6 %all-to-all-start.1 = ((bf16[4,144,2048]{2,1,0:T(8,128)(2,1)}), bf16[4,144,2048]{2,1,0:T(8,128)(2,1)}, u32[]{:S(2)}, u32[]{:S(2)}) async-start(bf16[4,144,2048]{2,1,0:T(8,128)(2,1)} %pack.3), calls=%async_computation.1 | async-start | bytes 4718592 | tf_op jit(solution)/shard_map/all_to_all | solution.py:386
  103.8 7.8 %expert.2 = (bf16[32,40,1024]{2,1,0:T(8,128)(2,1)}, bf16[576,1152]{1,0:T(8,128)(2,1)}) custom-call(s32[4]{0:T(128)S(1)} %get-tuple-element.38.refs_0_, bf16[576,2048]{1,0:T(8,128)(2,1)} %bitcast.7, bf16[1024,768]{1,0:T(8,128)(2,1)} %bitcast.10, bf16[1024,384]{1,0:T(8,128)(2,1)} %bitcast.12), custom_call_target="tpu_custom_call" | custom-call | flops 2264924160 | bytes 7077888 | tf_op jit(solution)/shard_map/expert/pallas_call | solution.py:232
  111.7 13.1 %all-to-all-done.1 = bf16[4,144,2048]{2,1,0:T(8,128)(2,1)} async-done(((bf16[4,144,2048]{2,1,0:T(8,128)(2,1)}), bf16[4,144,2048]{2,1,0:T(8,128)(2,1)}, u32[]{:S(2)}, u32[]{:S(2)}) %all-to-all-start.1) | async-done | bytes 2359328 | tf_op jit(solution)/shard_map/all_to_all | solution.py:386
  124.8 7.9 %expert.3 = (bf16[32,40,1024]{2,1,0:T(8,128)(2,1)}, bf16[576,1152]{1,0:T(8,128)(2,1)}) custom-call(s32[4]{0:T(128)S(1)} %get-tuple-element.37.refs_0_, bf16[576,2048]{1,0:T(8,128)(2,1)} %bitcast.5.refs_1_.refs_4_.refs_5_, bf16[1024,768]{1,0:T(8,128)(2,1)} %bitcast.11, bf16[1024,384]{1,0:T(8,128)(2,1)} %bitcast.13, ...), custom_call_target="tpu_custom_call", output_to_operand_aliasing={{0}: (4, {})} | custom-call | flops 2264924160 | bytes 7077888 | tf_op jit(solution)/shard_map/expert/pallas_call | solution.py:232
  132.7 6.9 %all-to-all-start.2 = ((bf16[32,40,1024]{2,1,0:T(8,128)(2,1)}), bf16[32,40,1024]{2,1,0:T(8,128)(2,1)}, u32[]{:S(2)}, u32[]{:S(2)}) async-start(bf16[32,40,1024]{2,1,0:T(8,128)(2,1)} %get-tuple-element.33), calls=%async_computation.3 | async-start | bytes 5242880 | tf_op jit(solution)/shard_map/all_to_all | solution.py:420
  142.2 6.6 %weight_terms.1 = (f32[8,64,1152]{2,1,0:T(8,128)S(1)}, bf16[8,64,1152]{2,1,0:T(8,128)(2,1)S(1)}) custom-call(s32[1]{0:T(128)} %bitcast.refs_0_, bf16[576,2048]{1,0:T(8,128)(2,1)S(1)} %bitcast.8, bf16[576,2048]{1,0:T(8,128)(2,1)S(1)} %bitcast.9, bf16[576,1152]{1,0:T(8,128)(2,1)S(1)} %copy-done.2, bf16[576,2048]{1,0:T(8,128)(2,1)} %bitcast.5.refs_1_.refs_4_.refs_5_, ...), custom_call_target="tpu_custom_call" | custom-call | flops 2717908992 | bytes 10911744 | tf_op jit(solution)/shard_map/weight_terms/pallas_call | solution.py:301
  148.8 9.4 %collective-permute-start.14 = (bf16[8,64,1152]{2,1,0:T(8,128)(2,1)S(1)}, bf16[8,64,1152]{2,1,0:T(8,128)(2,1)S(1)}, u32[]{:S(2)}, u32[]{:S(2)}) collective-permute-start(bf16[8,64,1152]{2,1,0:T(8,128)(2,1)S(1)} %get-tuple-element.32), channel_id=1, source_target_pairs={{0,32},{32,0},{1,33},{33,1},{2,34},{34,2},{3,35},{35,3},{4,36},{36... | collective-permute-start | bytes 3538952 | tf_op jit(solution)/shard_map/ppermute | solution.py:425
  158.2 2.5 %collective-permute-done.14 = bf16[8,64,1152]{2,1,0:T(8,128)(2,1)S(1)} collective-permute-done((bf16[8,64,1152]{2,1,0:T(8,128)(2,1)S(1)}, bf16[8,64,1152]{2,1,0:T(8,128)(2,1)S(1)}, u32[]{:S(2)}, u32[]{:S(2)}) %collective-permute-start.14) | collective-permute-done | bytes 1179680 | tf_op jit(solution)/shard_map/ppermute | solution.py:425
  162.0 31.7 %all-to-all-done.2 = bf16[32,40,1024]{2,1,0:T(8,128)(2,1)} async-done(((bf16[32,40,1024]{2,1,0:T(8,128)(2,1)}), bf16[32,40,1024]{2,1,0:T(8,128)(2,1)}, u32[]{:S(2)}, u32[]{:S(2)}) %all-to-all-start.2) | async-done | bytes 2621472 | tf_op jit(solution)/shard_map/all_to_all | solution.py:420
  193.7 3.0 %combine.1 = bf16[128,1024]{1,0:T(8,128)(2,1)} custom-call(s32[128,8]{1,0:T(8,128)} %copy.10.routes_ref, bf16[1280,1024]{1,0:T(8,128)(2,1)} %bitcast.6.rows_ref), custom_call_target="tpu_custom_call" | custom-call | flops 335544320 | bytes 2883584 | tf_op jit(solution)/shard_map/combine/pallas_call | solution.py:350
  196.7 3.9 %reduce-scatter.2.cloned.1.call-done = bf16[1,64,1152]{2,1,0:T(8,128)(2,1)} async-done(((bf16[8,64,1152]{2,1,0:T(8,128)(2,1)}), bf16[1,64,1152]{2,1,0:T(8,128)(2,1)}) %reduce-scatter.2.cloned.1.call-update) | async-done | bytes 147472 | tf_op jit(solution)/shard_map/reduce_scatter | solution.py:427
  (49 shorter events, 20.0 us)
Async XLA Ops:
  11.8 15.5 %collective-permute-start.4 = (bf16[128,1152]{1,0:T(8,128)(2,1)}, bf16[128,1152]{1,0:T(8,128)(2,1)S(1)}, u32[]{:S(2)}, u32[]{:S(2)}) collective-permute-start(bf16[128,1152]{1,0:T(8,128)(2,1)} %payload.1.refs_5_), channel_id=1, source_target_pairs={{0,4},{4,8},{8,12},{12,16},{16,20},{20,24},{24,28},{28,0},{32,60},... | collective-permute-start | bytes 884744 | tf_op jit(solution)/shard_map/ppermute | solution.py:383
  23.3 8.9 %collective-permute-start = (bf16[128,1024]{1,0:T(8,128)(2,1)}, bf16[128,1024]{1,0:T(8,128)(2,1)S(1)}, u32[]{:S(2)}, u32[]{:S(2)}) collective-permute-start(bf16[128,1024]{1,0:T(8,128)(2,1)} %refs_1_.1), channel_id=1, source_target_pairs={{0,4},{4,8},{8,12},{12,16},{16,20},{20,24},{24,28},{28,0},{32,60},... | collective-permute-start | bytes 786440 | tf_op jit(solution)/shard_map/ppermute | solution.py:383
  27.3 8.6 %collective-permute-start.5 = (bf16[128,1152]{1,0:T(8,128)(2,1)S(1)}, bf16[128,1152]{1,0:T(8,128)(2,1)S(1)}, u32[]{:S(2)}, u32[]{:S(2)}) collective-permute-start(bf16[128,1152]{1,0:T(8,128)(2,1)S(1)} %collective-permute-done.4.refs_6_), channel_id=1, source_target_pairs={{0,4},{4,8},{8,12},{12,16},{16,20},{20,24},{24,28},{28,0},{32,60},... | collective-permute-start | bytes 884744 | tf_op jit(solution)/shard_map/ppermute | solution.py:383
  32.2 8.7 %collective-permute-start.1 = (bf16[128,1024]{1,0:T(8,128)(2,1)S(1)}, bf16[128,1024]{1,0:T(8,128)(2,1)S(1)}, u32[]{:S(2)}, u32[]{:S(2)}) collective-permute-start(bf16[128,1024]{1,0:T(8,128)(2,1)S(1)} %collective-permute-done.refs_2_), channel_id=1, source_target_pairs={{0,4},{4,8},{8,12},{12,16},{16,20},{20,24},{24,28},{28,0},{32,60},... | collective-permute-start | bytes 786440 | tf_op jit(solution)/shard_map/ppermute | solution.py:383
  35.8 8.7 %collective-permute-start.6 = (bf16[128,1152]{1,0:T(8,128)(2,1)S(1)}, bf16[128,1152]{1,0:T(8,128)(2,1)S(1)}, u32[]{:S(2)}, u32[]{:S(2)}) collective-permute-start(bf16[128,1152]{1,0:T(8,128)(2,1)S(1)} %collective-permute-done.5.refs_7_), channel_id=1, source_target_pairs={{0,4},{4,8},{8,12},{12,16},{16,20},{20,24},{24,28},{28,0},{32,60},... | collective-permute-start | bytes 884744 | tf_op jit(solution)/shard_map/ppermute | solution.py:383
  40.8 8.7 %collective-permute-start.2 = (bf16[128,1024]{1,0:T(8,128)(2,1)S(1)}, bf16[128,1024]{1,0:T(8,128)(2,1)S(1)}, u32[]{:S(2)}, u32[]{:S(2)}) collective-permute-start(bf16[128,1024]{1,0:T(8,128)(2,1)S(1)} %collective-permute-done.1.refs_3_), channel_id=1, source_target_pairs={{0,4},{4,8},{8,12},{12,16},{16,20},{20,24},{24,28},{28,0},{32,60},... | collective-permute-start | bytes 786440 | tf_op jit(solution)/shard_map/ppermute | solution.py:383
  44.5 13.9 %collective-permute-start.7 = (bf16[128,1152]{1,0:T(8,128)(2,1)S(1)}, bf16[128,1152]{1,0:T(8,128)(2,1)S(1)}, u32[]{:S(2)}, u32[]{:S(2)}) collective-permute-start(bf16[128,1152]{1,0:T(8,128)(2,1)S(1)} %collective-permute-done.6.refs_8_), channel_id=1, source_target_pairs={{0,4},{4,8},{8,12},{12,16},{16,20},{20,24},{24,28},{28,0},{32,60},... | collective-permute-start | bytes 884744 | tf_op jit(solution)/shard_map/ppermute | solution.py:383
  49.5 8.9 %collective-permute-start.3 = (bf16[128,1024]{1,0:T(8,128)(2,1)S(1)}, bf16[128,1024]{1,0:T(8,128)(2,1)S(1)}, u32[]{:S(2)}, u32[]{:S(2)}) collective-permute-start(bf16[128,1024]{1,0:T(8,128)(2,1)S(1)} %collective-permute-done.2.refs_4_), channel_id=1, source_target_pairs={{0,4},{4,8},{8,12},{12,16},{16,20},{20,24},{24,28},{28,0},{32,60},... | collective-permute-start | bytes 786440 | tf_op jit(solution)/shard_map/ppermute | solution.py:383
  52.3 1.0 copy-start.4
  53.3 0.9 copy-start.5
  58.4 6.6 %copy-start.6 = (bf16[128,1024]{1,0:T(8,128)(2,1)}, bf16[128,1024]{1,0:T(8,128)(2,1)S(1)}, u32[]{:S(2)}) copy-start(bf16[128,1024]{1,0:T(8,128)(2,1)S(1)} %collective-permute-done.3.refs_1_) | copy-start | bytes 786436
  58.4 32.6 %all-to-all-start = ((bf16[4,144,2048]{2,1,0:T(8,128)(2,1)}), bf16[4,144,2048]{2,1,0:T(8,128)(2,1)S(1)}, u32[]{:S(2)}, u32[]{:S(2)}) async-start(bf16[4,144,2048]{2,1,0:T(8,128)(2,1)} %pack.2), calls=%async_computation | async-start | bytes 4718592 | tf_op jit(solution)/shard_map/all_to_all | solution.py:386
  62.4 7.8 %collective-permute-start.11 = (bf16[128,1152]{1,0:T(8,128)(2,1)S(1)}, bf16[128,1152]{1,0:T(8,128)(2,1)S(1)}, u32[]{:S(2)}, u32[]{:S(2)}) collective-permute-start(bf16[128,1152]{1,0:T(8,128)(2,1)S(1)} %collective-permute-done.7.refs_5_), channel_id=1, source_target_pairs={{0,4},{4,8},{8,12},{12,16},{16,20},{20,24},{24,28},{28,0},{32,60},... | collective-permute-start | bytes 884744 | tf_op jit(solution)/shard_map/ppermute | solution.py:383
  65.0 9.0 %collective-permute-start.8 = (bf16[128,1024]{1,0:T(8,128)(2,1)S(1)}, bf16[128,1024]{1,0:T(8,128)(2,1)S(1)}, u32[]{:S(2)}, u32[]{:S(2)}) collective-permute-start(bf16[128,1024]{1,0:T(8,128)(2,1)S(1)} %collective-permute-done.3.refs_1_), channel_id=1, source_target_pairs={{0,4},{4,8},{8,12},{12,16},{16,20},{20,24},{24,28},{28,0},{32,60},... | collective-permute-start | bytes 786440 | tf_op jit(solution)/shard_map/ppermute | solution.py:383
  70.2 7.8 %collective-permute-start.12 = (bf16[128,1152]{1,0:T(8,128)(2,1)S(1)}, bf16[128,1152]{1,0:T(8,128)(2,1)S(1)}, u32[]{:S(2)}, u32[]{:S(2)}) collective-permute-start(bf16[128,1152]{1,0:T(8,128)(2,1)S(1)} %collective-permute-done.11.refs_6_), channel_id=1, source_target_pairs={{0,4},{4,8},{8,12},{12,16},{16,20},{20,24},{24,28},{28,0},{32,60},... | collective-permute-start | bytes 884744 | tf_op jit(solution)/shard_map/ppermute | solution.py:383
  74.0 9.0 %collective-permute-start.9 = (bf16[128,1024]{1,0:T(8,128)(2,1)S(1)}, bf16[128,1024]{1,0:T(8,128)(2,1)S(1)}, u32[]{:S(2)}, u32[]{:S(2)}) collective-permute-start(bf16[128,1024]{1,0:T(8,128)(2,1)S(1)} %collective-permute-done.8.refs_2_), channel_id=1, source_target_pairs={{0,4},{4,8},{8,12},{12,16},{16,20},{20,24},{24,28},{28,0},{32,60},... | collective-permute-start | bytes 786440 | tf_op jit(solution)/shard_map/ppermute | solution.py:383
  76.8 0.7 copy-start.8
  77.9 13.1 %collective-permute-start.13 = (bf16[128,1152]{1,0:T(8,128)(2,1)S(1)}, bf16[128,1152]{1,0:T(8,128)(2,1)S(1)}, u32[]{:S(2)}, u32[]{:S(2)}) collective-permute-start(bf16[128,1152]{1,0:T(8,128)(2,1)S(1)} %collective-permute-done.12.refs_7_), channel_id=1, source_target_pairs={{0,4},{4,8},{8,12},{12,16},{16,20},{20,24},{24,28},{28,0},{32,60},... | collective-permute-start | bytes 884744 | tf_op jit(solution)/shard_map/ppermute | solution.py:383
  82.9 7.4 %collective-permute-start.10 = (bf16[128,1024]{1,0:T(8,128)(2,1)S(1)}, bf16[128,1024]{1,0:T(8,128)(2,1)S(1)}, u32[]{:S(2)}, u32[]{:S(2)}) collective-permute-start(bf16[128,1024]{1,0:T(8,128)(2,1)S(1)} %collective-permute-done.9.refs_3_), channel_id=1, source_target_pairs={{0,4},{4,8},{8,12},{12,16},{16,20},{20,24},{24,28},{28,0},{32,60},... | collective-permute-start | bytes 786440 | tf_op jit(solution)/shard_map/ppermute | solution.py:383
  85.7 0.7 copy-start.10
  91.0 8.1 %copy-start = (bf16[4,144,2048]{2,1,0:T(8,128)(2,1)}, bf16[4,144,2048]{2,1,0:T(8,128)(2,1)S(1)}, u32[]{:S(2)}) copy-start(bf16[4,144,2048]{2,1,0:T(8,128)(2,1)S(1)} %all-to-all-done) | copy-start | bytes 7077892
  91.0 1.1 copy-start.7
  92.2 0.9 copy-start.9
  93.1 0.9 copy-start.11
  94.1 0.9 copy-start.13
  99.2 25.6 %all-to-all-start.1 = ((bf16[4,144,2048]{2,1,0:T(8,128)(2,1)}), bf16[4,144,2048]{2,1,0:T(8,128)(2,1)}, u32[]{:S(2)}, u32[]{:S(2)}) async-start(bf16[4,144,2048]{2,1,0:T(8,128)(2,1)} %pack.3), calls=%async_computation.1 | async-start | bytes 4718592 | tf_op jit(solution)/shard_map/all_to_all | solution.py:386
  132.7 6.9 %copy-start.1 = (bf16[4,144,2048]{2,1,0:T(8,128)(2,1)S(1)}, bf16[4,144,2048]{2,1,0:T(8,128)(2,1)}, u32[]{:S(2)}) copy-start(bf16[4,144,2048]{2,1,0:T(8,128)(2,1)} %copy-done) | copy-start | bytes 7077892
  132.7 61.0 %all-to-all-start.2 = ((bf16[32,40,1024]{2,1,0:T(8,128)(2,1)}), bf16[32,40,1024]{2,1,0:T(8,128)(2,1)}, u32[]{:S(2)}, u32[]{:S(2)}) async-start(bf16[32,40,1024]{2,1,0:T(8,128)(2,1)} %get-tuple-element.33), calls=%async_computation.3 | async-start | bytes 5242880 | tf_op jit(solution)/shard_map/all_to_all | solution.py:420
  139.5 61.1 %reduce-scatter.2.cloned.1.call-start = ((), (), s32[]{:S(2)}) async-start(), calls=%async_computation.4 | async-start | bytes 1327104 | tf_op jit(solution)/shard_map/reduce_scatter | solution.py:427
  139.6 1.3 copy-start.2
  140.9 1.3 copy-start.3
  148.8 11.8 %collective-permute-start.14 = (bf16[8,64,1152]{2,1,0:T(8,128)(2,1)S(1)}, bf16[8,64,1152]{2,1,0:T(8,128)(2,1)S(1)}, u32[]{:S(2)}, u32[]{:S(2)}) collective-permute-start(bf16[8,64,1152]{2,1,0:T(8,128)(2,1)S(1)} %get-tuple-element.32), channel_id=1, source_target_pairs={{0,32},{32,0},{1,33},{33,1},{2,34},{34,2},{3,35},{35,3},{4,36},{36... | collective-permute-start | bytes 3538952 | tf_op jit(solution)/shard_map/ppermute | solution.py:425
  (1 other events, 0.7 us)
Sparse Core Ops, SparseCore 0:
  162.1 38.4 reduce-scatter.1

commit v3 on v2

--- a/solution.py
+++ b/solution.py
@@ -13,6 +13,7 @@
 CORES = 2
 X_RING = 4
 IN_HBM = pl.BlockSpec(memory_space=pltpu.HBM)
+ANYWHERE = pl.BlockSpec(memory_space=pl.ANY)
 IN_SMEM = pl.BlockSpec(memory_space=pltpu.SMEM)
 DMA = pltpu.SemaphoreType.DMA
 
@@ -35,67 +36,64 @@
     return copy
 
 
-def place(top, part):
-    row = lax.broadcasted_iota(jnp.int32, (top, LANES), 0)
-    lane = lax.broadcasted_iota(jnp.int32, (top, LANES), 1)
-    return (lane == row + part * top).astype(BF16)
-
-
-def payload_kernel(g_ref, routes_ref, probs_ref, out_ref, routes_in, probs_in, made, sems):
+def payload_kernel(x_ref, g_ref, routes_ref, probs_ref, out_ref, routes_in, probs_in, made, sems):
     width = g_ref.shape[1]
-    top = routes_ref.shape[1]
+    top = routes_ref.shape[0]
     routes_copy = started(routes_ref, routes_in, sems.at[0])
     probs_copy = started(probs_ref, probs_in, sems.at[1])
-    g_copy = started(g_ref, made.at[:, pl.ds(0, width)], sems.at[2])
+    x_copy = started(x_ref, out_ref.at[:, pl.ds(0, width)], sems.at[2])
+    g_copy = started(g_ref, out_ref.at[:, pl.ds(width, width)], sems.at[3])
     routes_copy.wait()
     probs_copy.wait()
-    routes = routes_in[...].astype(F32).astype(BF16)
     probs = probs_in[...]
-    high = probs.astype(BF16)
-    rest = probs - high.astype(F32)
-    middle = rest.astype(BF16)
-    low = (rest - middle.astype(F32)).astype(BF16)
-    info = jnp.zeros((g_ref.shape[0], LANES), F32)
-    for part, piece in enumerate((routes, high, middle, low)):
-        info += jnp.dot(piece, place(top, part), preferred_element_type=F32)
-    made[:, width:] = info.astype(BF16)
+    high = probs.astype(BF16).astype(F32)
+    middle = (probs - high).astype(BF16).astype(F32)
+    low = probs - high - middle
+    rest = jnp.zeros((LANES - 4 * top, LANES), F32)
+    info = jnp.concatenate([routes_in[...].astype(F32), high, middle, low, rest], axis=0)
+    made[...] = info.T.astype(BF16)
+    info_copy = started(made, out_ref.at[:, pl.ds(2 * width, LANES)], sems.at[4])
+    x_copy.wait()
     g_copy.wait()
-    started(made, out_ref, sems.at[3]).wait()
-
-
-def payload(grad_out, routes, gate_probs):
+    info_copy.wait()
+
+
+def payload(x_in, grad_out, routes, gate_probs):
     tokens, width = grad_out.shape
-    top = routes.shape[1]
+    top = routes.shape[0]
     return pl.pallas_call(
         payload_kernel,
-        out_shape=pltpu.HBM((tokens, width + LANES), BF16),
-        in_specs=[IN_HBM] * 3,
-        out_specs=IN_HBM,
+        out_shape=jax.ShapeDtypeStruct((tokens, 2 * width + LANES), BF16),
+        in_specs=[IN_HBM] * 4,
+        out_specs=ANYWHERE,
         scratch_shapes=[
-            pltpu.VMEM((tokens, top), jnp.int32),
-            pltpu.VMEM((tokens, top), F32),
-            pltpu.VMEM((tokens, width + LANES), BF16),
-            DMA((4,)),
+            pltpu.VMEM((top, tokens), jnp.int32),
+            pltpu.VMEM((top, tokens), F32),
+            pltpu.VMEM((tokens, LANES), BF16),
+            DMA((5,)),
         ],
         compiler_params=params(8),
-        cost_estimate=cost(1e6, 4 * tokens * width),
+        cost_estimate=cost(1e6, 8 * tokens * width),
         name="payload",
-    )(in_hbm(grad_out), in_hbm(routes), in_hbm(gate_probs))
-
-
-def pack_kernel(top, capacity, *refs):
+    )(in_hbm(x_in), in_hbm(grad_out), in_hbm(routes), in_hbm(gate_probs))
+
+
+def pack_kernel(top, capacity, width, tokens, *refs):
     base_ref, refs = refs[0], refs[1:]
-    out_ref, x_in, g_in, pick, made, x_sems, g_sems, out_sems = refs[-8:]
-    count = (len(refs) - 8) // 2
-    tokens, width = refs[0].shape
+    out_ref, held, pick, made, in_sems, out_sems = refs[-6:]
+    pieces = refs[:-6]
     rows = out_ref.shape[1]
-    g_copies = [
-        started(refs[count + b], g_in.at[pl.ds(b * tokens, tokens)], g_sems.at[b])
-        for b in range(count)
-    ]
-    x_copies = [
-        started(refs[b], x_in.at[pl.ds(b * tokens, tokens)], x_sems.at[b]) for b in range(count)
-    ]
+    count = held.shape[0] // tokens
+    copies = []
+    ends = []
+    filled = 0
+    for piece in range(len(pieces)):
+        size = pieces[piece].shape[0]
+        copies.append(
+            started(pieces[piece], held.at[pl.ds(filled, size)], in_sems.at[piece])
+        )
+        filled += size
+        ends.append(filled)
     before = (
         lax.broadcasted_iota(jnp.int32, (tokens, tokens), 0)
         < lax.broadcasted_iota(jnp.int32, (tokens, tokens), 1)
@@ -105,8 +103,10 @@
     base = base_ref[0].astype(F32)
     weights = [jnp.zeros((rows, 1), F32) for _ in range(X_RING)]
     for b in range(count):
-        g_copies[b].wait()
-        info = g_in[b * tokens : (b + 1) * tokens, width:].astype(F32).T
+        for copy, end in zip(copies, ends):
+            if b * tokens < end <= (b + 1) * tokens:
+                copy.wait()
+        info = held[b * tokens : (b + 1) * tokens, 2 * width :].astype(F32).T
         routes = info[:top]
         probs = info[top : 2 * top] + info[2 * top : 3 * top] + info[3 * top : 4 * top]
         masks = []
@@ -126,57 +126,47 @@
             hit = slots == where_to
             weights[expert] += jnp.sum(jnp.where(hit, chances[expert], 0.0), axis=1, keepdims=True)
             pick[expert, :, b * tokens : (b + 1) * tokens] = jnp.where(hit, 1.0, 0.0).astype(BF16)
-    for copy in x_copies:
-        copy.wait()
     step = 512
     out_copies = []
     for expert in range(X_RING):
-        for start in range(0, width, step):
-            made[expert, :, start : start + step] = jnp.dot(
-                pick[expert], x_in[:, start : start + step], preferred_element_type=F32
-            ).astype(BF16)
-        for start in range(0, width, step):
+        for start in range(0, 2 * width, step):
             total = jnp.dot(
-                pick[expert], g_in[:, start : start + step], preferred_element_type=F32
+                pick[expert], held[:, start : start + step], preferred_element_type=F32
             )
-            made[expert, :, width + start : width + start + step] = (
-                total * weights[expert]
-            ).astype(BF16)
+            if start >= width:
+                total = total * weights[expert]
+            made[expert, :, start : start + step] = total.astype(BF16)
         out_copies.append(started(made.at[expert], out_ref.at[expert], out_sems.at[expert]))
     for copy in out_copies:
         copy.wait()
 
 
-def pack(base, x_blocks, g_blocks, top, capacity):
-    count = len(x_blocks)
-    tokens, width = x_blocks[0].shape
+def pack(base, pieces, top, capacity, width, tokens):
+    total = sum(piece.shape[0] for piece in pieces)
+    count = total // tokens
     rows = -(-capacity * count // 8) * 8
     return pl.pallas_call(
-        functools.partial(pack_kernel, top, capacity),
+        functools.partial(pack_kernel, top, capacity, width, tokens),
         out_shape=pltpu.HBM((X_RING, rows, 2 * width), BF16),
-        in_specs=[IN_SMEM] + [pl.BlockSpec(memory_space=pl.ANY)] * (2 * count),
+        in_specs=[IN_SMEM] + [ANYWHERE] * len(pieces),
         out_specs=IN_HBM,
         scratch_shapes=[
-            pltpu.VMEM((count * tokens, width), BF16),
-            pltpu.VMEM((count * tokens, width + LANES), BF16),
-            pltpu.VMEM((X_RING, rows, count * tokens), BF16),
+            pltpu.VMEM((total, 2 * width + LANES), BF16),
+            pltpu.VMEM((X_RING, rows, total), BF16),
             pltpu.VMEM((X_RING, rows, 2 * width), BF16),
-            DMA((count,)),
-            DMA((count,)),
+            DMA((len(pieces),)),
             DMA((X_RING,)),
         ],
-        compiler_params=params(16),
-        cost_estimate=cost(
-            16 * count * rows * tokens * width, 16 * rows * width + 4 * count * tokens * width
-        ),
+        compiler_params=params(12),
+        cost_estimate=cost(16 * rows * total * width, 16 * rows * width + 4 * total * width),
         name="pack",
-    )(base, *x_blocks, *g_blocks)
+    )(base, *pieces)
 
 
 def expert_kernel(capacity, slot_rows, *refs):
-    place_ref, rows_ref, proj_ref, down_ref = refs[:4]
-    away_ref, terms_ref = refs[-10:-8]
-    rows_in, proj_in, down_in, terms, back, made, in_sems, out_sems = refs[-8:]
+    place_ref, rows_ref, proj_ref, down_ref, turned_ref = refs[:5]
+    away_ref, terms_ref = refs[-11:-9]
+    rows_in, proj_in, down_in, turned_in, terms, back, made, in_sems, out_sems = refs[-9:]
     width, hidden_units = down_ref.shape
     count = rows_ref.shape[0]
     per_x = count // X_RING
@@ -185,6 +175,7 @@
         started(rows_ref, rows_in, in_sems.at[0]),
         started(proj_ref, proj_in, in_sems.at[1]),
         started(down_ref, down_in, in_sems.at[2]),
+        started(turned_ref, turned_in, in_sems.at[4]),
     ]
     for copy in copies:
         copy.wait()
@@ -200,11 +191,8 @@
     terms[:, 2 * hidden_units :] = (activated * up_part).astype(BF16)
     terms_copy = started(terms, terms_ref, in_sems.at[3])
     back[count:] = jnp.zeros((back.shape[0] - count, width), F32)
-    back[:count] = lax.dot_general(
-        terms[:, : 2 * hidden_units],
-        proj_in[...],
-        (((1,), (1,)), ((), ())),
-        preferred_element_type=F32,
+    back[:count] = jnp.dot(
+        terms[:, : 2 * hidden_units], turned_in[...], preferred_element_type=F32
     )
     out_copies = []
     for column in range(X_RING):
@@ -220,31 +208,32 @@
         copy.wait()
 
 
-def expert_rows(places, rows_in, proj_weight, down_weight, capacity, slot_rows, owners, away):
+def expert_rows(places, rows_in, away, proj_weight, down_weight, turned, capacity, slot_rows, owners):
     count = rows_in.shape[0]
     width, hidden_units = down_weight.shape
     blocks = places.shape[0]
-    operands = [places, rows_in, proj_weight, down_weight]
+    operands = [places, rows_in, proj_weight, down_weight, turned]
     aliases = {}
     if away is not None:
         operands.append(away)
-        aliases = {4: 0}
+        aliases = {5: 0}
     return pl.pallas_call(
         functools.partial(expert_kernel, capacity, slot_rows),
         out_shape=(
             pltpu.HBM((owners, slot_rows, width), BF16),
             pltpu.HBM((count, 3 * hidden_units), BF16),
         ),
-        in_specs=[IN_SMEM] + [IN_HBM] * (len(operands) - 1),
+        in_specs=[IN_SMEM, ANYWHERE] + [IN_HBM] * (len(operands) - 2),
         out_specs=(IN_HBM, IN_HBM),
         scratch_shapes=[
             pltpu.VMEM((count, 2 * width), BF16),
             pltpu.VMEM((width, 2 * hidden_units), BF16),
             pltpu.VMEM((width, hidden_units), BF16),
+            pltpu.VMEM((2 * hidden_units, width), BF16),
             pltpu.VMEM((count, 3 * hidden_units), BF16),
             pltpu.VMEM((count + 8, width), F32),
             pltpu.VMEM((X_RING * blocks, slot_rows, width), BF16),
-            DMA((4,)),
+            DMA((5,)),
             DMA((X_RING * blocks,)),
         ],
         input_output_aliases=aliases,
@@ -253,7 +242,7 @@
             10 * count * width * hidden_units, 6 * width * hidden_units + 8 * count * width
         ),
         name="expert",
-    )(operands[0], *map(in_hbm, operands[1:]))
+    )(*operands[:2], *map(in_hbm, operands[2:]))
 
 
 def weight_kernel(pairs, *refs):
@@ -290,7 +279,7 @@
     for rows, terms in zip(row_list, term_list):
         count = rows.shape[0]
         total += count
-        operands += [rows, rows, terms]
+        operands += [rows, rows, in_hbm(terms)]
         specs += [
             pl.BlockSpec((count, block), lambda i: (0, i)),
             pl.BlockSpec((count, block), lambda i: (0, i + steps)),
@@ -314,16 +303,17 @@
 
 
 def combine_kernel(experts, routes_ref, rows_ref, out_ref, routes_in, rows_in, made, sems):
-    tokens, top = routes_ref.shape
+    top, tokens = routes_ref.shape
     total_rows = rows_ref.shape[0]
     slot_rows = total_rows // experts
     routes_copy = started(routes_ref, routes_in, sems.at[0])
     rows_copy = started(rows_ref, rows_in, sems.at[1])
     routes_copy.wait()
-    lanes = lax.broadcasted_iota(jnp.int32, (tokens, experts), 1)
-    mask = jnp.zeros((tokens, experts), F32)
+    labels = lax.broadcasted_iota(jnp.int32, (LANES, tokens), 0)
+    mask = jnp.zeros((LANES, tokens), F32)
     for entry in range(top):
-        mask += jnp.where(routes_in[:, entry : entry + 1] == lanes, 1.0, 0.0)
+        mask += jnp.where(routes_in[entry : entry + 1] == labels, 1.0, 0.0)
+    mask = mask.T[:, :experts]
     before = (
         lax.broadcasted_iota(jnp.int32, (tokens, tokens), 1)
         < lax.broadcasted_iota(jnp.int32, (tokens, tokens), 0)
@@ -345,7 +335,7 @@
 
 
 def combine(routes, rows_back, experts):
-    tokens, top = routes.shape
+    top, tokens = routes.shape
     total_rows, width = rows_back.shape
     return pl.pallas_call(
         functools.partial(combine_kernel, experts),
@@ -353,7 +343,7 @@
         in_specs=[IN_HBM] * 2,
         out_specs=IN_HBM,
         scratch_shapes=[
-            pltpu.VMEM((tokens, top), jnp.int32),
+            pltpu.VMEM((top, tokens), jnp.int32),
             pltpu.VMEM((total_rows, width), BF16),
             pltpu.VMEM((tokens, width), BF16),
             DMA((3,)),
@@ -374,53 +364,63 @@
     proj_weight = gate_up[0]
     down_weight = down[0]
     z_index = lax.axis_index("z")
-    core = lax.axis_index("c")
+    core = lax.axis_index("c").astype(jnp.int32).reshape(1)
     base = (z_index * X_RING).astype(jnp.int32).reshape(1)
-    turn = [(i, (i + 1) % z_size) for i in range(z_size)]
-    turn += [(z_size + i, z_size + (i - 1) % z_size) for i in range(z_size)]
-
-    def onward(value):
-        return lax.ppermute(value, ("c", "z"), turn)
+    routes = routes.T
+    turned = proj_weight.T
+
+    def shift(value, by):
+        return lax.ppermute(value, "z", [(i, (i + by) % z_size) for i in range(z_size)])
+
+    def packed(*pieces):
+        return pack(base, pieces, top, capacity, width, tokens)
 
     def crossed(value):
         return lax.all_to_all(value, "x", split_axis=0, concat_axis=0, tiled=True)
 
-    def arrive(packed):
-        return crossed(packed).reshape(-1, 2 * width)
-
-    half = z_size // 2
-    xs = [x_in]
-    gs = [payload(grad_out, routes, gate_probs)]
-    for _ in range(half):
-        xs.append(onward(xs[-1]))
-        gs.append(onward(gs[-1]))
-    packed = pack(base, xs[:half], gs[:half], top, capacity)
-    xs[half], gs[half], packed = lax.optimization_barrier((xs[half], gs[half], packed))
-    rows1 = arrive(packed)
-    for _ in range(half + 1, z_size):
-        xs.append(onward(xs[-1]))
-        gs.append(onward(gs[-1]))
-    xs[-1], gs[-1], rows1 = lax.optimization_barrier((xs[-1], gs[-1], rows1))
-    rows2 = arrive(pack(base, xs[half:], gs[half:], top, capacity))
-    steps = jnp.arange(z_size, dtype=jnp.int32)
-    places = jnp.where(core == 0, z_index - steps, z_index + steps) % z_size * X_RING
-    places = places.astype(jnp.int32)
+    def flat(value):
+        return value.reshape(-1, 2 * width)
+
     run = functools.partial(
         expert_rows,
         proj_weight=proj_weight,
         down_weight=down_weight,
+        turned=turned,
         capacity=capacity,
         slot_rows=slot_rows,
         owners=experts,
     )
-    away, terms1 = run(places[:half], rows1, away=None)
-    rows2, away = lax.optimization_barrier((rows2, away))
-    away, terms2 = run(places[half:], rows2, away=away)
-    away, terms2 = lax.optimization_barrier((away, terms2))
+
+    def places(*offsets):
+        steps = jnp.array(offsets, jnp.int32)
+        return ((z_index + steps) % z_size * X_RING).astype(jnp.int32)
+
+    half = tokens // 2
+    own = payload(x_in, grad_out, routes, gate_probs.T)
+    fore1, back1 = shift(own, 1), shift(own, -1)
+    fore2, back2 = shift(fore1, 1), shift(back1, -1)
+    packed1 = packed(own, fore1, back1)
+    fore2, back2, packed1 = lax.optimization_barrier((fore2, back2, packed1))
+    fore3, back3 = shift(fore2, 1), shift(back2, -1)
+    rows1 = crossed(packed1)
+    packed2 = packed(fore2, back2)
+    fore3, back3, packed2, rows1 = lax.optimization_barrier((fore3, back3, packed2, rows1))
+    fore4, back4 = shift(fore3[:half], 1), shift(back3[half:], -1)
+    rows1 = flat(rows1)
+    away, terms1 = run(places(0, -1, 1), rows1, None)
+    rows2 = crossed(packed2)
+    fore4, back4, rows2, away = lax.optimization_barrier((fore4, back4, rows2, away))
+    packed3 = packed(fore3, back3, fore4, back4)
+    rows2 = flat(rows2)
+    away, terms2 = run(places(-2, 2), rows2, away)
+    rows3, away = lax.optimization_barrier((crossed(packed3), away))
+    rows3 = flat(rows3)
+    away, terms3 = run(places(-3, 3, 4), rows3, away)
+    away, terms3 = lax.optimization_barrier((away, terms3))
     home = lax.all_to_all(away, ("z", "x"), split_axis=0, concat_axis=0, tiled=True)
     owners = lax.axis_size("y") * CORES
     keep, send = weight_terms(
-        core.astype(jnp.int32).reshape(1), (rows1, rows2), (terms1, terms2), width, owners
+        core, (rows1, rows2, rows3), (terms1, terms2, terms3), width, owners
     )
     other = lax.ppermute(send, "c", [(0, 1), (1, 0)])
     pair = (keep + other.astype(F32)).astype(BF16)

time: 215 us -> 213 us (level)
  the two profiles are of different devices: /device:TPU:1 before, /device:TPU:2 now
where the time goes in v3:
time: 213 us; the launch traced here: 212 us
  waiting for transfers between devices  86.5 us (41%)
  starting transfers between devices  55.9 us (26%)
  Pallas kernels  39.5 us (19%)
  local copies, waits for them, and re-layouts  14.5 us (7%)
  between operations  14.3 us (7%)
    all_to_all x1, waiting for transfers between devices, per_device(): lax.all_to_all(away, ('z', 'x'), split_axis=0, concat_axis=0, tiled=True)  41.4 us
    ppermute x8, starting transfers between devices, shift(): lax.ppermute(value, 'z', [(i, (i + by) % z_size) for i in range(z_size)])  33.3 us
    ppermute x8, waiting for transfers between devices, shift(): lax.ppermute(value, 'z', [(i, (i + by) % z_size) for i in range(z_size)])  25.9 us
    pallas_call x3, Pallas kernels, expert_rows(): pl.pallas_call(functools.partial(expert_kernel, capacity, slot_rows), out...  18.7 us
    all_to_all x3, waiting for transfers between devices, crossed(): return lax.all_to_all(value, 'x', split_axis=0, concat_axis=0, tiled=True)  16.2 us
    all_to_all x3, starting transfers between devices, crossed(): return lax.all_to_all(value, 'x', split_axis=0, concat_axis=0, tiled=True)  14.6 us
    unnamed x23, local copies, waits for them, and re-layouts  9.56 us
    pallas_call x3, Pallas kernels, pack(): pl.pallas_call(functools.partial(pack_kernel, top, capacity, width, token...  9.14 us
  transfers between devices with their start and end apart: 14, of which 9 were waited for; matrix products, arithmetic and copies ran while one was open for 3% of the time, Pallas kernels for 13%

profile of v3, /device:TPU:2, one launch (start us, length us, event | category | flops | bytes accessed | tf_op | source)
XLA Modules:
  0.0 212.0 jit_solution(14516788890476725827)
XLA Ops:
  8.3 10.9 %collective-permute-start.2 = (bf16[128,2176]{1,0:T(8,128)(2,1)S(1)}, bf16[128,2176]{1,0:T(8,128)(2,1)S(1)}, u32[]{:S(2)}, u32[]{:S(2)}) collective-permute-start(bf16[128,2176]{1,0:T(8,128)(2,1)S(1)} %payload.1.refs_1_), channel_id=1, source_target_pairs={{0,28},{4,0},{8,4},{12,8},{16,12},{20,16},{24,20},{28,24},{1,29},{... | collective-permute-start | bytes 1671176 | tf_op jit(solution)/shard_map/ppermute | solution.py:373
  19.2 1.9 collective-permute-start
  21.2 9.9 %collective-permute-done.2.refs_3_ = bf16[128,2176]{1,0:T(8,128)(2,1)S(1)} collective-permute-done((bf16[128,2176]{1,0:T(8,128)(2,1)S(1)}, bf16[128,2176]{1,0:T(8,128)(2,1)S(1)}, u32[]{:S(2)}, u32[]{:S(2)}) %collective-permute-start.2) | collective-permute-done | bytes 557088 | tf_op jit(solution)/shard_map/ppermute | solution.py:373
  31.1 5.6 %collective-permute-start.3 = (bf16[128,2176]{1,0:T(8,128)(2,1)S(1)}, bf16[128,2176]{1,0:T(8,128)(2,1)S(1)}, u32[]{:S(2)}, u32[]{:S(2)}) collective-permute-start(bf16[128,2176]{1,0:T(8,128)(2,1)S(1)} %collective-permute-done.2.refs_3_), channel_id=1, source_target_pairs={{0,28},{4,0},{8,4},{12,8},{16,12},{20,16},{24,20},{28,24},{1,29},{... | collective-permute-start | bytes 1671176 | tf_op jit(solution)/shard_map/ppermute | solution.py:373
  36.7 1.9 collective-permute-start.1
  38.6 3.2 %pack.3 = bf16[4,112,2048]{2,1,0:T(8,128)(2,1)} custom-call(s32[1]{0:T(128)} %bitcast.3.refs_0_, bf16[128,2176]{1,0:T(8,128)(2,1)S(1)} %payload.1.refs_1_, bf16[128,2176]{1,0:T(8,128)(2,1)S(1)} %collective-permute-done.refs_2_, bf16[128,2176]{1,0:T(8,128)(2,1)S(1)} %collective-permute-done.2.refs_3_), custom_call_target="tpu_custom_call" | custom-call | flops 704643072 | bytes 3407872 | tf_op jit(solution)/shard_map/pack/pallas_call | solution.py:148
  41.8 5.9 %collective-permute-done.3.refs_2_ = bf16[128,2176]{1,0:T(8,128)(2,1)S(1)} collective-permute-done((bf16[128,2176]{1,0:T(8,128)(2,1)S(1)}, bf16[128,2176]{1,0:T(8,128)(2,1)S(1)}, u32[]{:S(2)}, u32[]{:S(2)}) %collective-permute-start.3) | collective-permute-done | bytes 557088 | tf_op jit(solution)/shard_map/ppermute | solution.py:373
  47.7 5.3 %collective-permute-done.1.refs_1_ = bf16[128,2176]{1,0:T(8,128)(2,1)S(1)} collective-permute-done((bf16[128,2176]{1,0:T(8,128)(2,1)S(1)}, bf16[128,2176]{1,0:T(8,128)(2,1)S(1)}, u32[]{:S(2)}, u32[]{:S(2)}) %collective-permute-start.1) | collective-permute-done | bytes 557088 | tf_op jit(solution)/shard_map/ppermute | solution.py:373
  53.8 4.8 %all-to-all-start = ((bf16[4,112,2048]{2,1,0:T(8,128)(2,1)}), bf16[4,112,2048]{2,1,0:T(8,128)(2,1)S(1)}, u32[]{:S(2)}, u32[]{:S(2)}) async-start(bf16[4,112,2048]{2,1,0:T(8,128)(2,1)} %pack.3), calls=%async_computation | async-start | bytes 3670016 | tf_op jit(solution)/shard_map/all_to_all | solution.py:379
  58.7 1.9 collective-permute-start.4
  60.6 5.1 %collective-permute-start.5 = (bf16[128,2176]{1,0:T(8,128)(2,1)S(1)}, bf16[128,2176]{1,0:T(8,128)(2,1)}, u32[]{:S(2)}, u32[]{:S(2)}) collective-permute-start(bf16[128,2176]{1,0:T(8,128)(2,1)S(1)} %collective-permute-done.3.refs_2_), channel_id=1, source_target_pairs={{0,28},{4,0},{8,4},{12,8},{16,12},{20,16},{24,20},{28,24},{1,29},{... | collective-permute-start | bytes 1671176 | tf_op jit(solution)/shard_map/ppermute | solution.py:373
  66.8 2.3 %pack.4 = bf16[4,72,2048]{2,1,0:T(8,128)(2,1)} custom-call(s32[1]{0:T(128)} %bitcast.3.refs_0_, bf16[128,2176]{1,0:T(8,128)(2,1)S(1)} %copy-done.5, bf16[128,2176]{1,0:T(8,128)(2,1)S(1)} %collective-permute-done.3.refs_2_), custom_call_target="tpu_custom_call" | custom-call | flops 301989888 | bytes 2228224 | tf_op jit(solution)/shard_map/pack/pallas_call | solution.py:148
  69.1 4.6 %collective-permute-done.4.refs_1_ = bf16[128,2176]{1,0:T(8,128)(2,1)S(1)} collective-permute-done((bf16[128,2176]{1,0:T(8,128)(2,1)}, bf16[128,2176]{1,0:T(8,128)(2,1)S(1)}, u32[]{:S(2)}, u32[]{:S(2)}) %collective-permute-start.4) | collective-permute-done | bytes 557088 | tf_op jit(solution)/shard_map/ppermute | solution.py:373
  74.7 4.0 %all-to-all-done = bf16[4,112,2048]{2,1,0:T(8,128)(2,1)S(1)} async-done(((bf16[4,112,2048]{2,1,0:T(8,128)(2,1)}), bf16[4,112,2048]{2,1,0:T(8,128)(2,1)S(1)}, u32[]{:S(2)}, u32[]{:S(2)}) %all-to-all-start) | async-done | bytes 1835040 | tf_op jit(solution)/shard_map/all_to_all | solution.py:379
  78.7 5.0 %all-to-all-start.1 = ((bf16[4,72,2048]{2,1,0:T(8,128)(2,1)}), bf16[4,72,2048]{2,1,0:T(8,128)(2,1)S(1)}, u32[]{:S(2)}, u32[]{:S(2)}) async-start(bf16[4,72,2048]{2,1,0:T(8,128)(2,1)} %pack.4), calls=%async_computation.1 | async-start | bytes 2359296 | tf_op jit(solution)/shard_map/all_to_all | solution.py:379
  83.6 2.7 %copy.14 = bf16[1,1024,768]{1,2,0:T(8,128)(2,1)} copy(bf16[1,1024,768]{2,1,0:T(8,128)(2,1)} %param.13) | data formatting | bytes 3145728 | tf_op args[4]
  88.2 1.9 collective-permute-start.7
  90.2 3.9 %collective-permute-start.6 = (bf16[64,2176]{1,0:T(8,128)(2,1)S(1)}, bf16[64,2176]{1,0:T(8,128)(2,1)S(1)}, u32[]{:S(2)}, u32[]{:S(2)}) collective-permute-start(bf16[64,2176]{1,0:T(8,128)(2,1)S(1)} %slice.12), channel_id=1, source_target_pairs={{0,4},{4,8},{8,12},{12,16},{16,20},{20,24},{24,28},{28,0},{1,5},{5... | collective-permute-start | bytes 835592 | tf_op jit(solution)/shard_map/ppermute | solution.py:373
  94.2 6.5 %expert.3 = (bf16[32,40,1024]{2,1,0:T(8,128)(2,1)}, bf16[448,1152]{1,0:T(8,128)(2,1)}) custom-call(s32[3]{0:T(128)S(1)} %get-tuple-element.51.refs_0_, bf16[448,2048]{1,0:T(8,128)(2,1)S(1)} %bitcast.19, bf16[1024,768]{1,0:T(8,128)(2,1)} %bitcast.22, bf16[1024,384]{1,0:T(8,128)(2,1)} %bitcast.28, bf16[768,1024]{1,0:T(8,128)(2,1)} %bitcast.25), custom_call_target="tpu_custom_call" | custom-call | flops 1761607680 | bytes 6029312 | tf_op jit(solution)/shard_map/expert/pallas_call | solution.py:220
  103.4 3.7 %pack.5 = bf16[4,112,2048]{2,1,0:T(8,128)(2,1)} custom-call(s32[1]{0:T(128)} %bitcast.3.refs_0_, bf16[128,2176]{1,0:T(8,128)(2,1)S(1)} %copy-done.3, bf16[128,2176]{1,0:T(8,128)(2,1)} %collective-permute-done.5.refs_2_, bf16[64,2176]{1,0:T(8,128)(2,1)S(1)} %copy-done.7, bf16[64,2176]{1,0:T(8,128)(2,1)S(1)} %collective-permute-done.7.refs_4_), custom_call_target="tpu_custom_call" | custom-call | flops 704643072 | bytes 3407872 | tf_op jit(solution)/shard_map/pack/pallas_call | solution.py:148
  107.1 4.8 %all-to-all-start.2 = ((bf16[4,112,2048]{2,1,0:T(8,128)(2,1)}), bf16[4,112,2048]{2,1,0:T(8,128)(2,1)S(1)}, u32[]{:S(2)}, u32[]{:S(2)}) async-start(bf16[4,112,2048]{2,1,0:T(8,128)(2,1)} %pack.5), calls=%async_computation.2 | async-start | bytes 3670016 | tf_op jit(solution)/shard_map/all_to_all | solution.py:379
  112.0 5.7 %expert.4 = (bf16[32,40,1024]{2,1,0:T(8,128)(2,1)}, bf16[288,1152]{1,0:T(8,128)(2,1)}) custom-call(s32[2]{0:T(128)S(1)} %fusion.3.refs_0_, bf16[288,2048]{1,0:T(8,128)(2,1)S(1)} %bitcast.16, bf16[1024,768]{1,0:T(8,128)(2,1)} %bitcast.23, bf16[1024,384]{1,0:T(8,128)(2,1)} %bitcast.29, bf16[768,1024]{1,0:T(8,128)(2,1)} %bitcast.26, ...), custom_call_target="tpu_custom_call", output_to_operand_aliasing={{0}: (5, {})} | custom-call | flops 1132462080 | bytes 4718592 | tf_op jit(solution)/shard_map/expert/pallas_call | solution.py:220
  117.6 12.2 %all-to-all-done.2 = bf16[4,112,2048]{2,1,0:T(8,128)(2,1)S(1)} async-done(((bf16[4,112,2048]{2,1,0:T(8,128)(2,1)}), bf16[4,112,2048]{2,1,0:T(8,128)(2,1)S(1)}, u32[]{:S(2)}, u32[]{:S(2)}) %all-to-all-start.2) | async-done | bytes 1835040 | tf_op jit(solution)/shard_map/all_to_all | solution.py:379
  129.9 6.5 %expert.5 = (bf16[32,40,1024]{2,1,0:T(8,128)(2,1)}, bf16[448,1152]{1,0:T(8,128)(2,1)}) custom-call(s32[3]{0:T(128)S(1)} %get-tuple-element.52.refs_0_, bf16[448,2048]{1,0:T(8,128)(2,1)S(1)} %bitcast.13, bf16[1024,768]{1,0:T(8,128)(2,1)} %bitcast.24, bf16[1024,384]{1,0:T(8,128)(2,1)} %bitcast.30, ...), custom_call_target="tpu_custom_call", output_to_operand_aliasing={{0}: (5, {})} | custom-call | flops 1761607680 | bytes 6029312 | tf_op jit(solution)/shard_map/expert/pallas_call | solution.py:220
  136.4 5.9 %all-to-all-start.3 = ((bf16[32,40,1024]{2,1,0:T(8,128)(2,1)}), bf16[32,40,1024]{2,1,0:T(8,128)(2,1)}, u32[]{:S(2)}, u32[]{:S(2)}) async-start(bf16[32,40,1024]{2,1,0:T(8,128)(2,1)} %get-tuple-element.47), calls=%async_computation.4 | async-start | bytes 5242880 | tf_op jit(solution)/shard_map/all_to_all | solution.py:420
  142.6 1.5 copy-done.1
  144.1 7.4 %weight_terms.1 = (f32[8,64,1152]{2,1,0:T(8,128)S(1)}, bf16[8,64,1152]{2,1,0:T(8,128)(2,1)S(1)}) custom-call(s32[1]{0:T(128)} %bitcast.refs_0_, bf16[448,2048]{1,0:T(8,128)(2,1)S(1)} %bitcast.20, bf16[448,2048]{1,0:T(8,128)(2,1)S(1)} %bitcast.21, bf16[448,1152]{1,0:T(8,128)(2,1)} %get-tuple-element.31.refs_3_, bf16[288,2048]{1,0:T(8,128)(2,1)S(1)} %bitcast.17, ...), custom_call_target="tpu_custom_call" | custom-call | flops 2793406464 | bytes 11116544 | tf_op jit(solution)/shard_map/weight_terms/pallas_call | solution.py:290
  151.5 1.9 collective-permute-start.8
  153.4 2.8 %collective-permute-done.8 = bf16[8,64,1152]{2,1,0:T(8,128)(2,1)S(1)} collective-permute-done((bf16[8,64,1152]{2,1,0:T(8,128)(2,1)S(1)}, bf16[8,64,1152]{2,1,0:T(8,128)(2,1)S(1)}, u32[]{:S(2)}, u32[]{:S(2)}) %collective-permute-start.8) | collective-permute-done | bytes 1179680 | tf_op jit(solution)/shard_map/ppermute | solution.py:425
  157.6 41.4 %all-to-all-done.3 = bf16[32,40,1024]{2,1,0:T(8,128)(2,1)} async-done(((bf16[32,40,1024]{2,1,0:T(8,128)(2,1)}), bf16[32,40,1024]{2,1,0:T(8,128)(2,1)}, u32[]{:S(2)}, u32[]{:S(2)}) %all-to-all-start.3) | async-done | bytes 2621472 | tf_op jit(solution)/shard_map/all_to_all | solution.py:420
  199.0 3.0 %combine.1 = bf16[128,1024]{1,0:T(8,128)(2,1)} custom-call(s32[8,128]{1,0:T(8,128)} %bitcast.32, bf16[1280,1024]{1,0:T(8,128)(2,1)} %bitcast.12.rows_ref), custom_call_target="tpu_custom_call" | custom-call | flops 335544320 | bytes 2883584 | tf_op jit(solution)/shard_map/combine/pallas_call | solution.py:340
  203.5 1.6 slice.16
  (36 shorter events, 11.7 us)
Async XLA Ops:
  8.3 22.8 %collective-permute-start.2 = (bf16[128,2176]{1,0:T(8,128)(2,1)S(1)}, bf16[128,2176]{1,0:T(8,128)(2,1)S(1)}, u32[]{:S(2)}, u32[]{:S(2)}) collective-permute-start(bf16[128,2176]{1,0:T(8,128)(2,1)S(1)} %payload.1.refs_1_), channel_id=1, source_target_pairs={{0,28},{4,0},{8,4},{12,8},{16,12},{20,16},{24,20},{28,24},{1,29},{... | collective-permute-start | bytes 1671176 | tf_op jit(solution)/shard_map/ppermute | solution.py:373
  19.2 17.5 %collective-permute-start = (bf16[128,2176]{1,0:T(8,128)(2,1)S(1)}, bf16[128,2176]{1,0:T(8,128)(2,1)S(1)}, u32[]{:S(2)}, u32[]{:S(2)}) collective-permute-start(bf16[128,2176]{1,0:T(8,128)(2,1)S(1)} %payload.1.refs_1_), channel_id=1, source_target_pairs={{0,4},{4,8},{8,12},{12,16},{16,20},{20,24},{24,28},{28,0},{1,5},{5... | collective-permute-start | bytes 1671176 | tf_op jit(solution)/shard_map/ppermute | solution.py:373
  31.1 16.6 %collective-permute-start.3 = (bf16[128,2176]{1,0:T(8,128)(2,1)S(1)}, bf16[128,2176]{1,0:T(8,128)(2,1)S(1)}, u32[]{:S(2)}, u32[]{:S(2)}) collective-permute-start(bf16[128,2176]{1,0:T(8,128)(2,1)S(1)} %collective-permute-done.2.refs_3_), channel_id=1, source_target_pairs={{0,28},{4,0},{8,4},{12,8},{16,12},{20,16},{24,20},{28,24},{1,29},{... | collective-permute-start | bytes 1671176 | tf_op jit(solution)/shard_map/ppermute | solution.py:373
  36.7 16.3 %collective-permute-start.1 = (bf16[128,2176]{1,0:T(8,128)(2,1)S(1)}, bf16[128,2176]{1,0:T(8,128)(2,1)S(1)}, u32[]{:S(2)}, u32[]{:S(2)}) collective-permute-start(bf16[128,2176]{1,0:T(8,128)(2,1)S(1)} %collective-permute-done.refs_2_), channel_id=1, source_target_pairs={{0,4},{4,8},{8,12},{12,16},{16,20},{20,24},{24,28},{28,0},{1,5},{5... | collective-permute-start | bytes 1671176 | tf_op jit(solution)/shard_map/ppermute | solution.py:373
  53.0 0.8 copy-start.4
  53.8 24.8 %all-to-all-start = ((bf16[4,112,2048]{2,1,0:T(8,128)(2,1)}), bf16[4,112,2048]{2,1,0:T(8,128)(2,1)S(1)}, u32[]{:S(2)}, u32[]{:S(2)}) async-start(bf16[4,112,2048]{2,1,0:T(8,128)(2,1)} %pack.3), calls=%async_computation | async-start | bytes 3670016 | tf_op jit(solution)/shard_map/all_to_all | solution.py:379
  58.7 15.0 %collective-permute-start.4 = (bf16[128,2176]{1,0:T(8,128)(2,1)}, bf16[128,2176]{1,0:T(8,128)(2,1)S(1)}, u32[]{:S(2)}, u32[]{:S(2)}) collective-permute-start(bf16[128,2176]{1,0:T(8,128)(2,1)} %copy-done.4), channel_id=1, source_target_pairs={{0,4},{4,8},{8,12},{12,16},{16,20},{20,24},{24,28},{28,0},{1,5},{5... | collective-permute-start | bytes 1671176 | tf_op jit(solution)/shard_map/ppermute | solution.py:373
  60.6 14.1 %collective-permute-start.5 = (bf16[128,2176]{1,0:T(8,128)(2,1)S(1)}, bf16[128,2176]{1,0:T(8,128)(2,1)}, u32[]{:S(2)}, u32[]{:S(2)}) collective-permute-start(bf16[128,2176]{1,0:T(8,128)(2,1)S(1)} %collective-permute-done.3.refs_2_), channel_id=1, source_target_pairs={{0,28},{4,0},{8,4},{12,8},{16,12},{20,16},{24,20},{28,24},{1,29},{... | collective-permute-start | bytes 1671176 | tf_op jit(solution)/shard_map/ppermute | solution.py:373
  65.7 1.1 copy-start.5
  73.7 0.8 copy-start.2
  78.7 15.5 %copy-start = (bf16[4,112,2048]{2,1,0:T(8,128)(2,1)}, bf16[4,112,2048]{2,1,0:T(8,128)(2,1)S(1)}, u32[]{:S(2)}) copy-start(bf16[4,112,2048]{2,1,0:T(8,128)(2,1)S(1)} %all-to-all-done) | copy-start | bytes 5505028
  78.7 22.8 %all-to-all-start.1 = ((bf16[4,72,2048]{2,1,0:T(8,128)(2,1)}), bf16[4,72,2048]{2,1,0:T(8,128)(2,1)S(1)}, u32[]{:S(2)}, u32[]{:S(2)}) async-start(bf16[4,72,2048]{2,1,0:T(8,128)(2,1)} %pack.4), calls=%async_computation.1 | async-start | bytes 2359296 | tf_op jit(solution)/shard_map/all_to_all | solution.py:379
  83.6 10.5 %copy-start.8 = (s32[3]{0:T(128)S(1)}, s32[3]{0:T(128)}, u32[]{:S(2)}) copy-start(s32[3]{0:T(128)} %constant.52.clone) | copy-start | bytes 40
  83.6 10.5 %copy-start.9 = (s32[3]{0:T(128)S(1)}, s32[3]{0:T(128)}, u32[]{:S(2)}) copy-start(s32[3]{0:T(128)} %constant.50.clone) | copy-start | bytes 40
  88.2 12.4 %collective-permute-start.7 = (bf16[64,2176]{1,0:T(8,128)(2,1)S(1)}, bf16[64,2176]{1,0:T(8,128)(2,1)S(1)}, u32[]{:S(2)}, u32[]{:S(2)}) collective-permute-start(bf16[64,2176]{1,0:T(8,128)(2,1)S(1)} %slice.13), channel_id=1, source_target_pairs={{0,28},{4,0},{8,4},{12,8},{16,12},{20,16},{24,20},{28,24},{1,29},{... | collective-permute-start | bytes 835592 | tf_op jit(solution)/shard_map/ppermute | solution.py:373
  90.2 10.5 %collective-permute-start.6 = (bf16[64,2176]{1,0:T(8,128)(2,1)S(1)}, bf16[64,2176]{1,0:T(8,128)(2,1)S(1)}, u32[]{:S(2)}, u32[]{:S(2)}) collective-permute-start(bf16[64,2176]{1,0:T(8,128)(2,1)S(1)} %slice.12), channel_id=1, source_target_pairs={{0,4},{4,8},{8,12},{12,16},{16,20},{20,24},{24,28},{28,0},{1,5},{5... | collective-permute-start | bytes 835592 | tf_op jit(solution)/shard_map/ppermute | solution.py:373
  100.7 0.7 copy-start.6
  101.4 1.1 copy-start.3
  102.5 1.0 copy-start.7
  107.1 4.8 %copy-start.10 = (s32[2]{0:T(128)S(1)}, s32[2]{0:T(128)}, u32[]{:S(2)}) copy-start(s32[2]{0:T(128)} %constant.51.clone) | copy-start | bytes 28
  107.1 22.8 %all-to-all-start.2 = ((bf16[4,112,2048]{2,1,0:T(8,128)(2,1)}), bf16[4,112,2048]{2,1,0:T(8,128)(2,1)S(1)}, u32[]{:S(2)}, u32[]{:S(2)}) async-start(bf16[4,112,2048]{2,1,0:T(8,128)(2,1)} %pack.5), calls=%async_computation.2 | async-start | bytes 3670016 | tf_op jit(solution)/shard_map/all_to_all | solution.py:379
  136.4 62.6 %all-to-all-start.3 = ((bf16[32,40,1024]{2,1,0:T(8,128)(2,1)}), bf16[32,40,1024]{2,1,0:T(8,128)(2,1)}, u32[]{:S(2)}, u32[]{:S(2)}) async-start(bf16[32,40,1024]{2,1,0:T(8,128)(2,1)} %get-tuple-element.47), calls=%async_computation.4 | async-start | bytes 5242880 | tf_op jit(solution)/shard_map/all_to_all | solution.py:420
  142.3 59.8 %reduce-scatter.2.cloned.1.call-start = ((), (), s32[]{:S(2)}) async-start(), calls=%async_computation.5 | async-start | bytes 1327104 | tf_op jit(solution)/shard_map/reduce_scatter | solution.py:427
  142.6 1.5 copy-start.1
  151.5 4.7 %collective-permute-start.8 = (bf16[8,64,1152]{2,1,0:T(8,128)(2,1)S(1)}, bf16[8,64,1152]{2,1,0:T(8,128)(2,1)S(1)}, u32[]{:S(2)}, u32[]{:S(2)}) collective-permute-start(bf16[8,64,1152]{2,1,0:T(8,128)(2,1)S(1)} %get-tuple-element.46), channel_id=1, source_target_pairs={{0,32},{32,0},{1,33},{33,1},{2,34},{34,2},{3,35},{35,3},{4,36},{36... | collective-permute-start | bytes 3538952 | tf_op jit(solution)/shard_map/ppermute | solution.py:425
Sparse Core Ops, SparseCore 0:
  157.7 42.3 reduce-scatter.1

commit v4 on v3

--- a/solution.py
+++ b/solution.py
@@ -302,6 +302,25 @@
     )(*operands)
 
 
+def merge_kernel(y_ref, keep_ref, other_ref, *out_refs):
+    count = len(out_refs)
+    for by in range(count):
+        block = (y_ref[0] + by) % count
+        out_refs[by][...] = (keep_ref[block] + other_ref[block].astype(F32)).astype(BF16)
+
+
+def merge(y_index, keep, other):
+    count, share, columns = keep.shape
+    return pl.pallas_call(
+        merge_kernel,
+        out_shape=tuple(jax.ShapeDtypeStruct((share, columns), BF16) for _ in range(count)),
+        in_specs=[IN_SMEM] + [pl.BlockSpec(memory_space=pltpu.VMEM)] * 2,
+        compiler_params=params(8),
+        cost_estimate=cost(keep.size, 8 * keep.size),
+        name="merge",
+    )(y_index, keep, other)
+
+
 def combine_kernel(experts, routes_ref, rows_ref, out_ref, routes_in, rows_in, made, sems):
     top, tokens = routes_ref.shape
     total_rows = rows_ref.shape[0]
@@ -400,37 +419,43 @@
     fore1, back1 = shift(own, 1), shift(own, -1)
     fore2, back2 = shift(fore1, 1), shift(back1, -1)
     packed1 = packed(own, fore1, back1)
-    fore2, back2, packed1 = lax.optimization_barrier((fore2, back2, packed1))
-    fore3, back3 = shift(fore2, 1), shift(back2, -1)
     rows1 = crossed(packed1)
+    onward_f, onward_b, _ = lax.optimization_barrier((fore2, back2, packed1))
+    fore3, back3 = shift(onward_f, 1), shift(onward_b, -1)
     packed2 = packed(fore2, back2)
-    fore3, back3, packed2, rows1 = lax.optimization_barrier((fore3, back3, packed2, rows1))
-    fore4, back4 = shift(fore3[:half], 1), shift(back3[half:], -1)
+    onward_f, onward_b, _ = lax.optimization_barrier((fore3, back3, packed2))
+    fore4, back4 = shift(onward_f[:half], 1), shift(onward_b[half:], -1)
+    packed2, rows1 = lax.optimization_barrier((packed2, rows1))
+    rows2 = crossed(packed2)
     rows1 = flat(rows1)
     away, terms1 = run(places(0, -1, 1), rows1, None)
-    rows2 = crossed(packed2)
-    fore4, back4, rows2, away = lax.optimization_barrier((fore4, back4, rows2, away))
     packed3 = packed(fore3, back3, fore4, back4)
+    packed3, rows2, away = lax.optimization_barrier((packed3, rows2, away))
+    rows3 = crossed(packed3)
     rows2 = flat(rows2)
     away, terms2 = run(places(-2, 2), rows2, away)
-    rows3, away = lax.optimization_barrier((crossed(packed3), away))
+    rows3, away = lax.optimization_barrier((rows3, away))
     rows3 = flat(rows3)
     away, terms3 = run(places(-3, 3, 4), rows3, away)
     away, terms3 = lax.optimization_barrier((away, terms3))
     home = lax.all_to_all(away, ("z", "x"), split_axis=0, concat_axis=0, tiled=True)
-    owners = lax.axis_size("y") * CORES
+    y_size = lax.axis_size("y")
     keep, send = weight_terms(
-        core, (rows1, rows2, rows3), (terms1, terms2, terms3), width, owners
+        core, (rows1, rows2, rows3), (terms1, terms2, terms3), width, y_size * CORES
     )
     other = lax.ppermute(send, "c", [(0, 1), (1, 0)])
-    pair = (keep + other.astype(F32)).astype(BF16)
-    share = lax.psum_scatter(pair, "y", scatter_dimension=0, tiled=True)
-    home, pair = lax.optimization_barrier((home, pair))
+    y_index = lax.axis_index("y").astype(jnp.int32).reshape(1)
+    shares = merge(y_index, keep, other)
+    total = shares[0].astype(F32)
+    for by in range(1, y_size):
+        total = total + lax.ppermute(
+            shares[by], "y", [(i, (i + by) % y_size) for i in range(y_size)]
+        ).astype(F32)
+    split = total.shape[1] // 3 * 2
+    grads = (total[None, :, :split], total[None, :, split:])
+    home, grads = lax.optimization_barrier((home, grads))
     grad_in = combine(routes, home.reshape(-1, width), experts)
-    share, grad_in = lax.optimization_barrier((share, grad_in))
-    share = share.astype(F32)
-    split = share.shape[2] // 3 * 2
-    return (grad_in, share[:, :, :split], share[:, :, split:])
+    return (grad_in, *grads)
 
 
 def solution(mesh):

time: 213 us -> 192 us (0.901)
  the two profiles are of different devices: /device:TPU:2 before, /device:TPU:1 now
where the time goes in v4:
time: 192 us; the launch traced here: 189 us
  starting transfers between devices  88 us (46%)
  waiting for transfers between devices  47.8 us (25%)
  Pallas kernels  41.6 us (22%)
  local copies, waits for them, and re-layouts  10.5 us (5%)
    ppermute x8, starting transfers between devices, shift(): lax.ppermute(value, 'z', [(i, (i + by) % z_size) for i in range(z_size)])  34.8 us
    ppermute x7, starting transfers between devices, per_device(): lax.ppermute(shares[by], 'y', [(i, (i + by) % y_size) for i in range(y_si...  28.4 us
    ppermute x8, waiting for transfers between devices, shift(): lax.ppermute(value, 'z', [(i, (i + by) % z_size) for i in range(z_size)])  21.3 us
    pallas_call x3, Pallas kernels, expert_rows(): pl.pallas_call(functools.partial(expert_kernel, capacity, slot_rows), out...  18.8 us
    all_to_all x3, waiting for transfers between devices, crossed(): return lax.all_to_all(value, 'x', split_axis=0, concat_axis=0, tiled=True)  12.8 us
    all_to_all x3, starting transfers between devices, crossed(): return lax.all_to_all(value, 'x', split_axis=0, concat_axis=0, tiled=True)  11.9 us
    ppermute x7, waiting for transfers between devices, per_device(): lax.ppermute(shares[by], 'y', [(i, (i + by) % y_size) for i in range(y_si...  11 us
    pallas_call x3, Pallas kernels, pack(): pl.pallas_call(functools.partial(pack_kernel, top, capacity, width, token...  10.3 us
  transfers between devices with their start and end apart: 20, of which 8 were waited for; matrix products, arithmetic and copies ran while one was open for 3% of the time, Pallas kernels for 15%

profile of v4, /device:TPU:1, one launch (start us, length us, event | category | flops | bytes accessed | tf_op | source)
XLA Modules:
  0.0 189.2 jit_solution(8265472477219677307)
XLA Ops:
  1.7 4.8 %collective-permute-start = (bf16[128,2176]{1,0:T(8,128)(2,1)S(1)}, bf16[128,2176]{1,0:T(8,128)(2,1)S(1)}, u32[]{:S(2)}, u32[]{:S(2)}) collective-permute-start(bf16[128,2176]{1,0:T(8,128)(2,1)S(1)} %payload.1.refs_1_), channel_id=1, source_target_pairs={{0,4},{4,8},{8,12},{12,16},{16,20},{20,24},{24,28},{28,0},{1,5},{5... | collective-permute-start | bytes 1671176 | tf_op jit(solution)/shard_map/ppermute | solution.py:392
  6.6 8.6 %collective-permute-start.2 = (bf16[128,2176]{1,0:T(8,128)(2,1)S(1)}, bf16[128,2176]{1,0:T(8,128)(2,1)S(1)}, u32[]{:S(2)}, u32[]{:S(2)}) collective-permute-start(bf16[128,2176]{1,0:T(8,128)(2,1)S(1)} %payload.1.refs_1_), channel_id=1, source_target_pairs={{0,28},{4,0},{8,4},{12,8},{16,12},{20,16},{24,20},{28,24},{1,29},{... | collective-permute-start | bytes 1671176 | tf_op jit(solution)/shard_map/ppermute | solution.py:392
  15.2 10.4 %collective-permute-done.refs_2_ = bf16[128,2176]{1,0:T(8,128)(2,1)S(1)} collective-permute-done((bf16[128,2176]{1,0:T(8,128)(2,1)S(1)}, bf16[128,2176]{1,0:T(8,128)(2,1)S(1)}, u32[]{:S(2)}, u32[]{:S(2)}) %collective-permute-start) | collective-permute-done | bytes 557088 | tf_op jit(solution)/shard_map/ppermute | solution.py:392
  26.5 3.1 %pack.3 = bf16[4,112,2048]{2,1,0:T(8,128)(2,1)} custom-call(s32[1]{0:T(128)} %bitcast.1.refs_0_, bf16[128,2176]{1,0:T(8,128)(2,1)S(1)} %payload.1.refs_1_, bf16[128,2176]{1,0:T(8,128)(2,1)S(1)} %collective-permute-done.refs_2_, bf16[128,2176]{1,0:T(8,128)(2,1)S(1)} %collective-permute-done.2.refs_3_), custom_call_target="tpu_custom_call" | custom-call | flops 704643072 | bytes 3407872 | tf_op jit(solution)/shard_map/pack/pallas_call | solution.py:148
  29.6 4.0 %all-to-all-start = ((bf16[4,112,2048]{2,1,0:T(8,128)(2,1)}), bf16[4,112,2048]{2,1,0:T(8,128)(2,1)S(1)}, u32[]{:S(2)}, u32[]{:S(2)}) async-start(bf16[4,112,2048]{2,1,0:T(8,128)(2,1)} %pack.3), calls=%async_computation | async-start | bytes 3670016 | tf_op jit(solution)/shard_map/all_to_all | solution.py:398
  35.5 5.3 %collective-permute-start.3 = (bf16[128,2176]{1,0:T(8,128)(2,1)S(1)}, bf16[128,2176]{1,0:T(8,128)(2,1)}, u32[]{:S(2)}, u32[]{:S(2)}) collective-permute-start(bf16[128,2176]{1,0:T(8,128)(2,1)S(1)} %collective-permute-done.2.refs_3_), channel_id=1, source_target_pairs={{0,28},{4,0},{8,4},{12,8},{16,12},{20,16},{24,20},{28,24},{1,29},{... | collective-permute-start | bytes 1671176 | tf_op jit(solution)/shard_map/ppermute | solution.py:392
  40.9 9.3 %collective-permute-done.1.refs_1_ = bf16[128,2176]{1,0:T(8,128)(2,1)} collective-permute-done((bf16[128,2176]{1,0:T(8,128)(2,1)S(1)}, bf16[128,2176]{1,0:T(8,128)(2,1)}, u32[]{:S(2)}, u32[]{:S(2)}) %collective-permute-start.1) | collective-permute-done | bytes 557088 | tf_op jit(solution)/shard_map/ppermute | solution.py:392
  50.9 2.9 %collective-permute-start.4 = (bf16[128,2176]{1,0:T(8,128)(2,1)}, bf16[128,2176]{1,0:T(8,128)(2,1)}, u32[]{:S(2)}, u32[]{:S(2)}) collective-permute-start(bf16[128,2176]{1,0:T(8,128)(2,1)} %collective-permute-done.1.refs_1_), channel_id=1, source_target_pairs={{0,4},{4,8},{8,12},{12,16},{16,20},{20,24},{24,28},{28,0},{1,5},{5... | collective-permute-start | bytes 1671176 | tf_op jit(solution)/shard_map/ppermute | solution.py:392
  53.9 4.4 %collective-permute-start.5 = (bf16[128,2176]{1,0:T(8,128)(2,1)}, bf16[128,2176]{1,0:T(8,128)(2,1)}, u32[]{:S(2)}, u32[]{:S(2)}) collective-permute-start(bf16[128,2176]{1,0:T(8,128)(2,1)} %collective-permute-done.3.refs_2_), channel_id=1, source_target_pairs={{0,28},{4,0},{8,4},{12,8},{16,12},{20,16},{24,20},{28,24},{1,29},{... | collective-permute-start | bytes 1671176 | tf_op jit(solution)/shard_map/ppermute | solution.py:392
  58.3 3.2 %pack.4 = bf16[4,72,2048]{2,1,0:T(8,128)(2,1)} custom-call(s32[1]{0:T(128)} %bitcast.1.refs_0_, bf16[128,2176]{1,0:T(8,128)(2,1)} %collective-permute-done.1.refs_1_, bf16[128,2176]{1,0:T(8,128)(2,1)} %collective-permute-done.3.refs_2_), custom_call_target="tpu_custom_call" | custom-call | flops 301989888 | bytes 2228224 | tf_op jit(solution)/shard_map/pack/pallas_call | solution.py:148
  61.5 4.0 %all-to-all-start.1 = ((bf16[4,72,2048]{2,1,0:T(8,128)(2,1)}), bf16[4,72,2048]{2,1,0:T(8,128)(2,1)S(1)}, u32[]{:S(2)}, u32[]{:S(2)}) async-start(bf16[4,72,2048]{2,1,0:T(8,128)(2,1)} %pack.4), calls=%async_computation.1 | async-start | bytes 2359296 | tf_op jit(solution)/shard_map/all_to_all | solution.py:398
  65.5 2.6 %copy.14 = bf16[1,1024,768]{1,2,0:T(8,128)(2,1)} copy(bf16[1,1024,768]{2,1,0:T(8,128)(2,1)} %param.13) | data formatting | bytes 3145728 | tf_op args[4]
  72.0 4.9 %collective-permute-start.7 = (bf16[64,2176]{1,0:T(8,128)(2,1)S(1)}, bf16[64,2176]{1,0:T(8,128)(2,1)S(1)}, u32[]{:S(2)}, u32[]{:S(2)}) collective-permute-start(bf16[64,2176]{1,0:T(8,128)(2,1)S(1)} %slice.13), channel_id=1, source_target_pairs={{0,28},{4,0},{8,4},{12,8},{16,12},{20,16},{24,20},{28,24},{1,29},{... | collective-permute-start | bytes 835592 | tf_op jit(solution)/shard_map/ppermute | solution.py:392
  77.0 6.5 %expert.3 = (bf16[32,40,1024]{2,1,0:T(8,128)(2,1)}, bf16[448,1152]{1,0:T(8,128)(2,1)}) custom-call(s32[3]{0:T(128)S(1)} %get-tuple-element.64.refs_0_, bf16[448,2048]{1,0:T(8,128)(2,1)S(1)} %bitcast.24, bf16[1024,768]{1,0:T(8,128)(2,1)} %bitcast.27, bf16[1024,384]{1,0:T(8,128)(2,1)} %bitcast.33, bf16[768,1024]{1,0:T(8,128)(2,1)} %bitcast.30), custom_call_target="tpu_custom_call" | custom-call | flops 1761607680 | bytes 6029312 | tf_op jit(solution)/shard_map/expert/pallas_call | solution.py:220
  83.6 4.0 %pack.5 = bf16[4,112,2048]{2,1,0:T(8,128)(2,1)} custom-call(s32[1]{0:T(128)} %bitcast.1.refs_0_, bf16[128,2176]{1,0:T(8,128)(2,1)} %collective-permute-done.4.refs_1_, bf16[128,2176]{1,0:T(8,128)(2,1)} %collective-permute-done.5.refs_2_, bf16[64,2176]{1,0:T(8,128)(2,1)S(1)} %collective-permute-done.6.refs_3_, bf16[64,2176]{1,0:T(8,128)(2,1)S(1)} %collective-permute-done.7.refs_4_), custom_call_target="tpu_custom_call" | custom-call | flops 704643072 | bytes 3407872 | tf_op jit(solution)/shard_map/pack/pallas_call | solution.py:148
  87.6 3.9 %all-to-all-start.2 = ((bf16[4,112,2048]{2,1,0:T(8,128)(2,1)}), bf16[4,112,2048]{2,1,0:T(8,128)(2,1)S(1)}, u32[]{:S(2)}, u32[]{:S(2)}) async-start(bf16[4,112,2048]{2,1,0:T(8,128)(2,1)} %pack.5), calls=%async_computation.2 | async-start | bytes 3670016 | tf_op jit(solution)/shard_map/all_to_all | solution.py:398
  91.5 5.7 %expert.4 = (bf16[32,40,1024]{2,1,0:T(8,128)(2,1)}, bf16[288,1152]{1,0:T(8,128)(2,1)}) custom-call(s32[2]{0:T(128)S(1)} %fusion.5.refs_0_, bf16[288,2048]{1,0:T(8,128)(2,1)S(1)} %bitcast.21, bf16[1024,768]{1,0:T(8,128)(2,1)} %bitcast.28, bf16[1024,384]{1,0:T(8,128)(2,1)} %bitcast.34, bf16[768,1024]{1,0:T(8,128)(2,1)} %bitcast.31, ...), custom_call_target="tpu_custom_call", output_to_operand_aliasing={{0}: (5, {})} | custom-call | flops 1132462080 | bytes 4718592 | tf_op jit(solution)/shard_map/expert/pallas_call | solution.py:220
  97.2 12.8 %all-to-all-done.2 = bf16[4,112,2048]{2,1,0:T(8,128)(2,1)S(1)} async-done(((bf16[4,112,2048]{2,1,0:T(8,128)(2,1)}), bf16[4,112,2048]{2,1,0:T(8,128)(2,1)S(1)}, u32[]{:S(2)}, u32[]{:S(2)}) %all-to-all-start.2) | async-done | bytes 1835040 | tf_op jit(solution)/shard_map/all_to_all | solution.py:398
  110.0 6.5 %expert.5 = (bf16[32,40,1024]{2,1,0:T(8,128)(2,1)}, bf16[448,1152]{1,0:T(8,128)(2,1)}) custom-call(s32[3]{0:T(128)S(1)} %get-tuple-element.63.refs_0_, bf16[448,2048]{1,0:T(8,128)(2,1)S(1)} %bitcast.18, bf16[1024,768]{1,0:T(8,128)(2,1)} %bitcast.29, bf16[1024,384]{1,0:T(8,128)(2,1)} %bitcast.35, ...), custom_call_target="tpu_custom_call", output_to_operand_aliasing={{0}: (5, {})} | custom-call | flops 1761607680 | bytes 6029312 | tf_op jit(solution)/shard_map/expert/pallas_call | solution.py:220
  116.6 5.0 %all-to-all-start.3 = ((bf16[32,40,1024]{2,1,0:T(8,128)(2,1)}), bf16[32,40,1024]{2,1,0:T(8,128)(2,1)}, u32[]{:S(2)}, u32[]{:S(2)}) async-start(bf16[32,40,1024]{2,1,0:T(8,128)(2,1)} %get-tuple-element.46), calls=%async_computation.3 | async-start | bytes 5242880 | tf_op jit(solution)/shard_map/all_to_all | solution.py:441
  123.1 8.2 %weight_terms.1 = (f32[8,64,1152]{2,1,0:T(8,128)S(1)}, bf16[8,64,1152]{2,1,0:T(8,128)(2,1)}) custom-call(s32[1]{0:T(128)} %bitcast.12.refs_0_, bf16[448,2048]{1,0:T(8,128)(2,1)S(1)} %bitcast.25, bf16[448,2048]{1,0:T(8,128)(2,1)S(1)} %bitcast.26, bf16[448,1152]{1,0:T(8,128)(2,1)} %get-tuple-element.47.refs_3_, bf16[288,2048]{1,0:T(8,128)(2,1)S(1)} %bitcast.22, ...), custom_call_target="tpu_custom_call" | custom-call | flops 2793406464 | bytes 11116544 | tf_op jit(solution)/shard_map/weight_terms/pallas_call | solution.py:290
  132.7 7.8 %collective-permute-start.8 = (bf16[8,64,1152]{2,1,0:T(8,128)(2,1)}, bf16[8,64,1152]{2,1,0:T(8,128)(2,1)S(1)}, u32[]{:S(2)}, u32[]{:S(2)}) collective-permute-start(bf16[8,64,1152]{2,1,0:T(8,128)(2,1)} %get-tuple-element.51), channel_id=1, source_target_pairs={{0,32},{32,0},{1,33},{33,1},{2,34},{34,2},{3,35},{35,3},{4,36},{36... | collective-permute-start | bytes 3538952 | tf_op jit(solution)/shard_map/ppermute | solution.py:446
  140.5 2.7 %collective-permute-done.8.other_ref = bf16[8,64,1152]{2,1,0:T(8,128)(2,1)S(1)} collective-permute-done((bf16[8,64,1152]{2,1,0:T(8,128)(2,1)}, bf16[8,64,1152]{2,1,0:T(8,128)(2,1)S(1)}, u32[]{:S(2)}, u32[]{:S(2)}) %collective-permute-start.8) | collective-permute-done | bytes 1179680 | tf_op jit(solution)/shard_map/ppermute | solution.py:446
  145.1 4.2 %collective-permute-start.10 = (bf16[64,1152]{1,0:T(8,128)(2,1)S(1)}, bf16[64,1152]{1,0:T(8,128)(2,1)S(1)}, u32[]{:S(2)}, u32[]{:S(2)}) collective-permute-start(bf16[64,1152]{1,0:T(8,128)(2,1)S(1)} %get-tuple-element.54), channel_id=1, source_target_pairs={{0,128},{64,192},{128,256},{192,320},{256,384},{320,448},{384,0},{... | collective-permute-start | bytes 442376 | tf_op jit(solution)/shard_map/ppermute | solution.py:451
  149.3 5.5 %collective-permute-start.11 = (bf16[64,1152]{1,0:T(8,128)(2,1)S(1)}, bf16[64,1152]{1,0:T(8,128)(2,1)S(1)}, u32[]{:S(2)}, u32[]{:S(2)}) collective-permute-start(bf16[64,1152]{1,0:T(8,128)(2,1)S(1)} %get-tuple-element.55), channel_id=1, source_target_pairs={{0,192},{64,256},{128,320},{192,384},{256,448},{320,0},{384,64},{4... | collective-permute-start | bytes 442376 | tf_op jit(solution)/shard_map/ppermute | solution.py:451
  154.8 2.6 %collective-permute-start.12 = (bf16[64,1152]{1,0:T(8,128)(2,1)S(1)}, bf16[64,1152]{1,0:T(8,128)(2,1)S(1)}, u32[]{:S(2)}, u32[]{:S(2)}) collective-permute-start(bf16[64,1152]{1,0:T(8,128)(2,1)S(1)} %get-tuple-element.56), channel_id=1, source_target_pairs={{0,256},{64,320},{128,384},{192,448},{256,0},{320,64},{384,128},{4... | collective-permute-start | bytes 442376 | tf_op jit(solution)/shard_map/ppermute | solution.py:451
  157.5 5.8 %collective-permute-start.13 = (bf16[64,1152]{1,0:T(8,128)(2,1)S(1)}, bf16[64,1152]{1,0:T(8,128)(2,1)S(1)}, u32[]{:S(2)}, u32[]{:S(2)}) collective-permute-start(bf16[64,1152]{1,0:T(8,128)(2,1)S(1)} %get-tuple-element.57), channel_id=1, source_target_pairs={{0,320},{64,384},{128,448},{192,0},{256,64},{320,128},{384,192},{4... | collective-permute-start | bytes 442376 | tf_op jit(solution)/shard_map/ppermute | solution.py:451
  163.3 5.0 %collective-permute-start.14 = (bf16[64,1152]{1,0:T(8,128)(2,1)S(1)}, bf16[64,1152]{1,0:T(8,128)(2,1)S(1)}, u32[]{:S(2)}, u32[]{:S(2)}) collective-permute-start(bf16[64,1152]{1,0:T(8,128)(2,1)S(1)} %get-tuple-element.58), channel_id=1, source_target_pairs={{0,384},{64,448},{128,0},{192,64},{256,128},{320,192},{384,256},{4... | collective-permute-start | bytes 442376 | tf_op jit(solution)/shard_map/ppermute | solution.py:451
  170.2 3.4 %collective-permute-start.9 = (bf16[64,1152]{1,0:T(8,128)(2,1)S(1)}, bf16[64,1152]{1,0:T(8,128)(2,1)S(1)}, u32[]{:S(2)}, u32[]{:S(2)}) collective-permute-start(bf16[64,1152]{1,0:T(8,128)(2,1)S(1)} %get-tuple-element.53), channel_id=1, source_target_pairs={{0,64},{64,128},{128,192},{192,256},{256,320},{320,384},{384,448},... | collective-permute-start | bytes 442376 | tf_op jit(solution)/shard_map/ppermute | solution.py:451
  173.6 2.3 %collective-permute-done.13 = bf16[64,1152]{1,0:T(8,128)(2,1)S(1)} collective-permute-done((bf16[64,1152]{1,0:T(8,128)(2,1)S(1)}, bf16[64,1152]{1,0:T(8,128)(2,1)S(1)}, u32[]{:S(2)}, u32[]{:S(2)}) %collective-permute-start.13) | collective-permute-done | bytes 147488 | tf_op jit(solution)/shard_map/ppermute | solution.py:451
  175.9 8.6 %collective-permute-done.14 = bf16[64,1152]{1,0:T(8,128)(2,1)S(1)} collective-permute-done((bf16[64,1152]{1,0:T(8,128)(2,1)S(1)}, bf16[64,1152]{1,0:T(8,128)(2,1)S(1)}, u32[]{:S(2)}, u32[]{:S(2)}) %collective-permute-start.14) | collective-permute-done | bytes 147488 | tf_op jit(solution)/shard_map/ppermute | solution.py:451
  186.0 3.0 %combine.1 = bf16[128,1024]{1,0:T(8,128)(2,1)} custom-call(s32[8,128]{1,0:T(8,128)} %bitcast.37, bf16[1280,1024]{1,0:T(8,128)(2,1)} %bitcast.15.rows_ref), custom_call_target="tpu_custom_call" | custom-call | flops 335544320 | bytes 2883584 | tf_op jit(solution)/shard_map/combine/pallas_call | solution.py:359
  (40 shorter events, 16.8 us)
Async XLA Ops:
  1.7 23.8 %collective-permute-start = (bf16[128,2176]{1,0:T(8,128)(2,1)S(1)}, bf16[128,2176]{1,0:T(8,128)(2,1)S(1)}, u32[]{:S(2)}, u32[]{:S(2)}) collective-permute-start(bf16[128,2176]{1,0:T(8,128)(2,1)S(1)} %payload.1.refs_1_), channel_id=1, source_target_pairs={{0,4},{4,8},{8,12},{12,16},{16,20},{20,24},{24,28},{28,0},{1,5},{5... | collective-permute-start | bytes 1671176 | tf_op jit(solution)/shard_map/ppermute | solution.py:392
  6.6 19.9 %collective-permute-start.2 = (bf16[128,2176]{1,0:T(8,128)(2,1)S(1)}, bf16[128,2176]{1,0:T(8,128)(2,1)S(1)}, u32[]{:S(2)}, u32[]{:S(2)}) collective-permute-start(bf16[128,2176]{1,0:T(8,128)(2,1)S(1)} %payload.1.refs_1_), channel_id=1, source_target_pairs={{0,28},{4,0},{8,4},{12,8},{16,12},{20,16},{24,20},{28,24},{1,29},{... | collective-permute-start | bytes 1671176 | tf_op jit(solution)/shard_map/ppermute | solution.py:392
  29.6 31.9 %all-to-all-start = ((bf16[4,112,2048]{2,1,0:T(8,128)(2,1)}), bf16[4,112,2048]{2,1,0:T(8,128)(2,1)S(1)}, u32[]{:S(2)}, u32[]{:S(2)}) async-start(bf16[4,112,2048]{2,1,0:T(8,128)(2,1)} %pack.3), calls=%async_computation | async-start | bytes 3670016 | tf_op jit(solution)/shard_map/all_to_all | solution.py:398
  33.6 16.5 %collective-permute-start.1 = (bf16[128,2176]{1,0:T(8,128)(2,1)S(1)}, bf16[128,2176]{1,0:T(8,128)(2,1)}, u32[]{:S(2)}, u32[]{:S(2)}) collective-permute-start(bf16[128,2176]{1,0:T(8,128)(2,1)S(1)} %collective-permute-done.refs_2_), channel_id=1, source_target_pairs={{0,4},{4,8},{8,12},{12,16},{16,20},{20,24},{24,28},{28,0},{1,5},{5... | collective-permute-start | bytes 1671176 | tf_op jit(solution)/shard_map/ppermute | solution.py:392
  35.5 15.4 %collective-permute-start.3 = (bf16[128,2176]{1,0:T(8,128)(2,1)S(1)}, bf16[128,2176]{1,0:T(8,128)(2,1)}, u32[]{:S(2)}, u32[]{:S(2)}) collective-permute-start(bf16[128,2176]{1,0:T(8,128)(2,1)S(1)} %collective-permute-done.2.refs_3_), channel_id=1, source_target_pairs={{0,28},{4,0},{8,4},{12,8},{16,12},{20,16},{24,20},{28,24},{1,29},{... | collective-permute-start | bytes 1671176 | tf_op jit(solution)/shard_map/ppermute | solution.py:392
  50.9 17.2 %collective-permute-start.4 = (bf16[128,2176]{1,0:T(8,128)(2,1)}, bf16[128,2176]{1,0:T(8,128)(2,1)}, u32[]{:S(2)}, u32[]{:S(2)}) collective-permute-start(bf16[128,2176]{1,0:T(8,128)(2,1)} %collective-permute-done.1.refs_1_), channel_id=1, source_target_pairs={{0,4},{4,8},{8,12},{12,16},{16,20},{20,24},{24,28},{28,0},{1,5},{5... | collective-permute-start | bytes 1671176 | tf_op jit(solution)/shard_map/ppermute | solution.py:392
  53.9 14.3 %collective-permute-start.5 = (bf16[128,2176]{1,0:T(8,128)(2,1)}, bf16[128,2176]{1,0:T(8,128)(2,1)}, u32[]{:S(2)}, u32[]{:S(2)}) collective-permute-start(bf16[128,2176]{1,0:T(8,128)(2,1)} %collective-permute-done.3.refs_2_), channel_id=1, source_target_pairs={{0,28},{4,0},{8,4},{12,8},{16,12},{20,16},{24,20},{28,24},{1,29},{... | collective-permute-start | bytes 1671176 | tf_op jit(solution)/shard_map/ppermute | solution.py:392
  61.5 15.5 %copy-start = (bf16[4,112,2048]{2,1,0:T(8,128)(2,1)}, bf16[4,112,2048]{2,1,0:T(8,128)(2,1)S(1)}, u32[]{:S(2)}) copy-start(bf16[4,112,2048]{2,1,0:T(8,128)(2,1)S(1)} %all-to-all-done) | copy-start | bytes 5505028
  61.5 26.0 %all-to-all-start.1 = ((bf16[4,72,2048]{2,1,0:T(8,128)(2,1)}), bf16[4,72,2048]{2,1,0:T(8,128)(2,1)S(1)}, u32[]{:S(2)}, u32[]{:S(2)}) async-start(bf16[4,72,2048]{2,1,0:T(8,128)(2,1)} %pack.4), calls=%async_computation.1 | async-start | bytes 2359296 | tf_op jit(solution)/shard_map/all_to_all | solution.py:398
  65.5 11.5 %copy-start.4 = (s32[3]{0:T(128)S(1)}, s32[3]{0:T(128)}, u32[]{:S(2)}) copy-start(s32[3]{0:T(128)} %constant.54.clone) | copy-start | bytes 40
  65.5 11.5 %copy-start.5 = (s32[3]{0:T(128)S(1)}, s32[3]{0:T(128)}, u32[]{:S(2)}) copy-start(s32[3]{0:T(128)} %constant.56.clone) | copy-start | bytes 40
  69.1 14.4 %collective-permute-start.6 = (bf16[64,2176]{1,0:T(8,128)(2,1)S(1)}, bf16[64,2176]{1,0:T(8,128)(2,1)S(1)}, u32[]{:S(2)}, u32[]{:S(2)}) collective-permute-start(bf16[64,2176]{1,0:T(8,128)(2,1)S(1)} %slice.12), channel_id=1, source_target_pairs={{0,4},{4,8},{8,12},{12,16},{16,20},{20,24},{24,28},{28,0},{1,5},{5... | collective-permute-start | bytes 835592 | tf_op jit(solution)/shard_map/ppermute | solution.py:392
  72.0 11.5 %collective-permute-start.7 = (bf16[64,2176]{1,0:T(8,128)(2,1)S(1)}, bf16[64,2176]{1,0:T(8,128)(2,1)S(1)}, u32[]{:S(2)}, u32[]{:S(2)}) collective-permute-start(bf16[64,2176]{1,0:T(8,128)(2,1)S(1)} %slice.13), channel_id=1, source_target_pairs={{0,28},{4,0},{8,4},{12,8},{16,12},{20,16},{24,20},{28,24},{1,29},{... | collective-permute-start | bytes 835592 | tf_op jit(solution)/shard_map/ppermute | solution.py:392
  87.6 3.9 %copy-start.6 = (s32[2]{0:T(128)S(1)}, s32[2]{0:T(128)}, u32[]{:S(2)}) copy-start(s32[2]{0:T(128)} %constant.55.clone) | copy-start | bytes 28
  87.6 22.5 %all-to-all-start.2 = ((bf16[4,112,2048]{2,1,0:T(8,128)(2,1)}), bf16[4,112,2048]{2,1,0:T(8,128)(2,1)S(1)}, u32[]{:S(2)}, u32[]{:S(2)}) async-start(bf16[4,112,2048]{2,1,0:T(8,128)(2,1)} %pack.5), calls=%async_computation.2 | async-start | bytes 3670016 | tf_op jit(solution)/shard_map/all_to_all | solution.py:398
  116.6 69.5 %all-to-all-start.3 = ((bf16[32,40,1024]{2,1,0:T(8,128)(2,1)}), bf16[32,40,1024]{2,1,0:T(8,128)(2,1)}, u32[]{:S(2)}, u32[]{:S(2)}) async-start(bf16[32,40,1024]{2,1,0:T(8,128)(2,1)} %get-tuple-element.46), calls=%async_computation.3 | async-start | bytes 5242880 | tf_op jit(solution)/shard_map/all_to_all | solution.py:441
  121.6 1.5 copy-start.1
  131.3 1.4 copy-start.2
  132.7 10.5 %collective-permute-start.8 = (bf16[8,64,1152]{2,1,0:T(8,128)(2,1)}, bf16[8,64,1152]{2,1,0:T(8,128)(2,1)S(1)}, u32[]{:S(2)}, u32[]{:S(2)}) collective-permute-start(bf16[8,64,1152]{2,1,0:T(8,128)(2,1)} %get-tuple-element.51), channel_id=1, source_target_pairs={{0,32},{32,0},{1,33},{33,1},{2,34},{34,2},{3,35},{35,3},{4,36},{36... | collective-permute-start | bytes 3538952 | tf_op jit(solution)/shard_map/ppermute | solution.py:446
  143.2 1.7 copy-start.3
  145.1 23.2 %collective-permute-start.10 = (bf16[64,1152]{1,0:T(8,128)(2,1)S(1)}, bf16[64,1152]{1,0:T(8,128)(2,1)S(1)}, u32[]{:S(2)}, u32[]{:S(2)}) collective-permute-start(bf16[64,1152]{1,0:T(8,128)(2,1)S(1)} %get-tuple-element.54), channel_id=1, source_target_pairs={{0,128},{64,192},{128,256},{192,320},{256,384},{320,448},{384,0},{... | collective-permute-start | bytes 442376 | tf_op jit(solution)/shard_map/ppermute | solution.py:451
  149.3 20.9 %collective-permute-start.11 = (bf16[64,1152]{1,0:T(8,128)(2,1)S(1)}, bf16[64,1152]{1,0:T(8,128)(2,1)S(1)}, u32[]{:S(2)}, u32[]{:S(2)}) collective-permute-start(bf16[64,1152]{1,0:T(8,128)(2,1)S(1)} %get-tuple-element.55), channel_id=1, source_target_pairs={{0,192},{64,256},{128,320},{192,384},{256,448},{320,0},{384,64},{4... | collective-permute-start | bytes 442376 | tf_op jit(solution)/shard_map/ppermute | solution.py:451
  154.8 18.7 %collective-permute-start.12 = (bf16[64,1152]{1,0:T(8,128)(2,1)S(1)}, bf16[64,1152]{1,0:T(8,128)(2,1)S(1)}, u32[]{:S(2)}, u32[]{:S(2)}) collective-permute-start(bf16[64,1152]{1,0:T(8,128)(2,1)S(1)} %get-tuple-element.56), channel_id=1, source_target_pairs={{0,256},{64,320},{128,384},{192,448},{256,0},{320,64},{384,128},{4... | collective-permute-start | bytes 442376 | tf_op jit(solution)/shard_map/ppermute | solution.py:451
  157.5 18.4 %collective-permute-start.13 = (bf16[64,1152]{1,0:T(8,128)(2,1)S(1)}, bf16[64,1152]{1,0:T(8,128)(2,1)S(1)}, u32[]{:S(2)}, u32[]{:S(2)}) collective-permute-start(bf16[64,1152]{1,0:T(8,128)(2,1)S(1)} %get-tuple-element.57), channel_id=1, source_target_pairs={{0,320},{64,384},{128,448},{192,0},{256,64},{320,128},{384,192},{4... | collective-permute-start | bytes 442376 | tf_op jit(solution)/shard_map/ppermute | solution.py:451
  163.3 21.3 %collective-permute-start.14 = (bf16[64,1152]{1,0:T(8,128)(2,1)S(1)}, bf16[64,1152]{1,0:T(8,128)(2,1)S(1)}, u32[]{:S(2)}, u32[]{:S(2)}) collective-permute-start(bf16[64,1152]{1,0:T(8,128)(2,1)S(1)} %get-tuple-element.58), channel_id=1, source_target_pairs={{0,384},{64,448},{128,0},{192,64},{256,128},{320,192},{384,256},{4... | collective-permute-start | bytes 442376 | tf_op jit(solution)/shard_map/ppermute | solution.py:451
  168.2 16.3 %collective-permute-start.15 = (bf16[64,1152]{1,0:T(8,128)(2,1)S(1)}, bf16[64,1152]{1,0:T(8,128)(2,1)S(1)}, u32[]{:S(2)}, u32[]{:S(2)}) collective-permute-start(bf16[64,1152]{1,0:T(8,128)(2,1)S(1)} %get-tuple-element.59), channel_id=1, source_target_pairs={{0,448},{64,0},{128,64},{192,128},{256,192},{320,256},{384,320},{4... | collective-permute-start | bytes 442376 | tf_op jit(solution)/shard_map/ppermute | solution.py:451
  170.2 14.4 %collective-permute-start.9 = (bf16[64,1152]{1,0:T(8,128)(2,1)S(1)}, bf16[64,1152]{1,0:T(8,128)(2,1)S(1)}, u32[]{:S(2)}, u32[]{:S(2)}) collective-permute-start(bf16[64,1152]{1,0:T(8,128)(2,1)S(1)} %get-tuple-element.53), channel_id=1, source_target_pairs={{0,64},{64,128},{128,192},{192,256},{256,320},{320,384},{384,448},... | collective-permute-start | bytes 442376 | tf_op jit(solution)/shard_map/ppermute | solution.py:451

commit v5 on v4

--- a/solution.py
+++ b/solution.py
@@ -12,6 +12,7 @@
 LANES = 128
 CORES = 2
 X_RING = 4
+HINT = 60
 IN_HBM = pl.BlockSpec(memory_space=pltpu.HBM)
 ANYWHERE = pl.BlockSpec(memory_space=pl.ANY)
 IN_SMEM = pl.BlockSpec(memory_space=pltpu.SMEM)
@@ -27,7 +28,9 @@
 
 
 def cost(flops, bytes_accessed):
-    return pl.CostEstimate(flops=int(flops), bytes_accessed=int(bytes_accessed), transcendentals=0)
+    return pl.CostEstimate(
+        flops=int(HINT * flops), bytes_accessed=int(HINT * bytes_accessed), transcendentals=0
+    )
 
 
 def started(source, target, semaphore):
@@ -290,7 +293,7 @@
     return pl.pallas_call(
         functools.partial(weight_kernel, len(row_list)),
         grid=(steps,),
-        out_shape=(jax.ShapeDtypeStruct(shape, F32), jax.ShapeDtypeStruct(shape, BF16)),
+        out_shape=(pltpu.HBM(shape, F32), pltpu.HBM(shape, BF16)),
         in_specs=specs,
         out_specs=(result, result),
         scratch_shapes=[pltpu.VMEM((pieces, share, columns), F32)],
@@ -302,11 +305,17 @@
     )(*operands)
 
 
-def merge_kernel(y_ref, keep_ref, other_ref, *out_refs):
+def merge_kernel(y_ref, keep_ref, other_ref, *refs):
+    keep, other, sems = refs[-3:]
+    out_refs = refs[:-3]
     count = len(out_refs)
+    keep_copy = started(keep_ref, keep, sems.at[0])
+    other_copy = started(other_ref, other, sems.at[1])
+    keep_copy.wait()
+    other_copy.wait()
     for by in range(count):
         block = (y_ref[0] + by) % count
-        out_refs[by][...] = (keep_ref[block] + other_ref[block].astype(F32)).astype(BF16)
+        out_refs[by][...] = (keep[block] + other[block].astype(F32)).astype(BF16)
 
 
 def merge(y_index, keep, other):
@@ -314,11 +323,12 @@
     return pl.pallas_call(
         merge_kernel,
         out_shape=tuple(jax.ShapeDtypeStruct((share, columns), BF16) for _ in range(count)),
-        in_specs=[IN_SMEM] + [pl.BlockSpec(memory_space=pltpu.VMEM)] * 2,
+        in_specs=[IN_SMEM, IN_HBM, ANYWHERE],
+        scratch_shapes=[pltpu.VMEM(keep.shape, F32), pltpu.VMEM(other.shape, BF16), DMA((2,))],
         compiler_params=params(8),
         cost_estimate=cost(keep.size, 8 * keep.size),
         name="merge",
-    )(y_index, keep, other)
+    )(y_index, in_hbm(keep), other)
 
 
 def combine_kernel(experts, routes_ref, rows_ref, out_ref, routes_in, rows_in, made, sems):
@@ -418,44 +428,47 @@
     own = payload(x_in, grad_out, routes, gate_probs.T)
     fore1, back1 = shift(own, 1), shift(own, -1)
     fore2, back2 = shift(fore1, 1), shift(back1, -1)
-    packed1 = packed(own, fore1, back1)
+    packed0 = packed(own)
+    rows0 = crossed(packed0)
+    fore3, back3 = shift(fore2, 1), shift(back2, -1)
+    packed1, rows0 = lax.optimization_barrier((packed(fore1, back1, fore2, back2), rows0))
     rows1 = crossed(packed1)
-    onward_f, onward_b, _ = lax.optimization_barrier((fore2, back2, packed1))
-    fore3, back3 = shift(onward_f, 1), shift(onward_b, -1)
-    packed2 = packed(fore2, back2)
-    onward_f, onward_b, _ = lax.optimization_barrier((fore3, back3, packed2))
+    onward_f, onward_b, _ = lax.optimization_barrier((fore3, back3, packed1))
     fore4, back4 = shift(onward_f[:half], 1), shift(onward_b[half:], -1)
-    packed2, rows1 = lax.optimization_barrier((packed2, rows1))
+    rows0 = flat(rows0)
+    away, terms0 = run(places(0), rows0, None)
+    packed2 = packed(fore3, back3, fore4, back4)
+    packed2, rows1, away = lax.optimization_barrier((packed2, rows1, away))
     rows2 = crossed(packed2)
     rows1 = flat(rows1)
-    away, terms1 = run(places(0, -1, 1), rows1, None)
-    packed3 = packed(fore3, back3, fore4, back4)
-    packed3, rows2, away = lax.optimization_barrier((packed3, rows2, away))
-    rows3 = crossed(packed3)
+    away, terms1 = run(places(-1, 1, -2, 2), rows1, away)
+    rows2, away = lax.optimization_barrier((rows2, away))
     rows2 = flat(rows2)
-    away, terms2 = run(places(-2, 2), rows2, away)
-    rows3, away = lax.optimization_barrier((rows3, away))
-    rows3 = flat(rows3)
-    away, terms3 = run(places(-3, 3, 4), rows3, away)
-    away, terms3 = lax.optimization_barrier((away, terms3))
+    away, terms2 = run(places(-3, 3, 4), rows2, away)
+    away, terms2 = lax.optimization_barrier((away, terms2))
     home = lax.all_to_all(away, ("z", "x"), split_axis=0, concat_axis=0, tiled=True)
     y_size = lax.axis_size("y")
     keep, send = weight_terms(
-        core, (rows1, rows2, rows3), (terms1, terms2, terms3), width, y_size * CORES
+        core,
+        (in_hbm(rows0), in_hbm(rows1), rows2),
+        (terms0, terms1, terms2),
+        width,
+        y_size * CORES,
     )
     other = lax.ppermute(send, "c", [(0, 1), (1, 0)])
     y_index = lax.axis_index("y").astype(jnp.int32).reshape(1)
     shares = merge(y_index, keep, other)
+    moved = [
+        lax.ppermute(shares[by], "y", [(i, (i + by) % y_size) for i in range(y_size)])
+        for by in range(1, y_size)
+    ]
+    grad_in = combine(routes, home.reshape(-1, width), experts)
+    grad_in, *moved = lax.optimization_barrier((grad_in, *moved))
     total = shares[0].astype(F32)
-    for by in range(1, y_size):
-        total = total + lax.ppermute(
-            shares[by], "y", [(i, (i + by) % y_size) for i in range(y_size)]
-        ).astype(F32)
+    for share in moved:
+        total = total + share.astype(F32)
     split = total.shape[1] // 3 * 2
-    grads = (total[None, :, :split], total[None, :, split:])
-    home, grads = lax.optimization_barrier((home, grads))
-    grad_in = combine(routes, home.reshape(-1, width), experts)
-    return (grad_in, *grads)
+    return (grad_in, total[None, :, :split], total[None, :, split:])
 
 
 def solution(mesh):

time: 192 us -> 186 us (0.969)
  the two profiles are of different devices: /device:TPU:1 before, /device:TPU:48 now
where the time goes in v5:
time: 186 us; the launch traced here: 185 us
  starting transfers between devices  80.5 us (43%)
  waiting for transfers between devices  53.9 us (29%)
  Pallas kernels  42.9 us (23%)
  local copies, waits for them, and re-layouts  5.96 us (3%)
    ppermute x8, starting transfers between devices, shift(): lax.ppermute(value, 'z', [(i, (i + by) % z_size) for i in range(z_size)])  34.5 us
    ppermute x7, starting transfers between devices, per_device(): lax.ppermute(shares[by], 'y', [(i, (i + by) % y_size) for i in range(y_si...  26.1 us
    all_to_all x3, waiting for transfers between devices, crossed(): return lax.all_to_all(value, 'x', split_axis=0, concat_axis=0, tiled=True)  20.3 us
    pallas_call x3, Pallas kernels, expert_rows(): pl.pallas_call(functools.partial(expert_kernel, capacity, slot_rows), out...  18.8 us
    all_to_all x1, waiting for transfers between devices, per_device(): lax.all_to_all(away, ('z', 'x'), split_axis=0, concat_axis=0, tiled=True)  16.4 us
    ppermute x8, waiting for transfers between devices, shift(): lax.ppermute(value, 'z', [(i, (i + by) % z_size) for i in range(z_size)])  14.2 us
    all_to_all x3, starting transfers between devices, crossed(): return lax.all_to_all(value, 'x', split_axis=0, concat_axis=0, tiled=True)  13 us
    pallas_call x3, Pallas kernels, pack(): pl.pallas_call(functools.partial(pack_kernel, top, capacity, width, token...  9.43 us
  transfers between devices with their start and end apart: 20, of which 8 were waited for; matrix products, arithmetic and copies ran while one was open for 3% of the time, Pallas kernels for 19%

profile of v5, /device:TPU:48, one launch (start us, length us, event | category | flops | bytes accessed | tf_op | source)
XLA Modules:
  0.0 184.6 jit_solution(6597026277360915230)
XLA Ops:
  1.7 4.3 %collective-permute-start = (bf16[128,2176]{1,0:T(8,128)(2,1)S(1)}, bf16[128,2176]{1,0:T(8,128)(2,1)S(1)}, u32[]{:S(2)}, u32[]{:S(2)}) collective-permute-start(bf16[128,2176]{1,0:T(8,128)(2,1)S(1)} %payload.1.refs_1_), channel_id=1, source_target_pairs={{0,4},{4,8},{8,12},{12,16},{16,20},{20,24},{24,28},{28,0},{1,5},{5... | collective-permute-start | bytes 1671176 | tf_op jit(solution)/shard_map/ppermute | solution.py:402
  6.0 8.6 %collective-permute-start.3 = (bf16[128,2176]{1,0:T(8,128)(2,1)S(1)}, bf16[128,2176]{1,0:T(8,128)(2,1)S(1)}, u32[]{:S(2)}, u32[]{:S(2)}) collective-permute-start(bf16[128,2176]{1,0:T(8,128)(2,1)S(1)} %payload.1.refs_1_), channel_id=1, source_target_pairs={{0,28},{4,0},{8,4},{12,8},{16,12},{20,16},{24,20},{28,24},{1,29},{... | collective-permute-start | bytes 1671176 | tf_op jit(solution)/shard_map/ppermute | solution.py:402
  14.6 10.7 %collective-permute-done.refs_1_ = bf16[128,2176]{1,0:T(8,128)(2,1)S(1)} collective-permute-done((bf16[128,2176]{1,0:T(8,128)(2,1)S(1)}, bf16[128,2176]{1,0:T(8,128)(2,1)S(1)}, u32[]{:S(2)}, u32[]{:S(2)}) %collective-permute-start) | collective-permute-done | bytes 557088 | tf_op jit(solution)/shard_map/ppermute | solution.py:402
  25.3 1.9 %collective-permute-start.1 = (bf16[128,2176]{1,0:T(8,128)(2,1)S(1)}, bf16[128,2176]{1,0:T(8,128)(2,1)}, u32[]{:S(2)}, u32[]{:S(2)}) collective-permute-start(bf16[128,2176]{1,0:T(8,128)(2,1)S(1)} %collective-permute-done.refs_1_), channel_id=1, source_target_pairs={{0,4},{4,8},{8,12},{12,16},{16,20},{20,24},{24,28},{28,0},{1,5},{5... | collective-permute-start | bytes 1671176 | tf_op jit(solution)/shard_map/ppermute | solution.py:402
  27.2 5.1 %collective-permute-start.4 = (bf16[128,2176]{1,0:T(8,128)(2,1)S(1)}, bf16[128,2176]{1,0:T(8,128)(2,1)}, u32[]{:S(2)}, u32[]{:S(2)}) collective-permute-start(bf16[128,2176]{1,0:T(8,128)(2,1)S(1)} %collective-permute-done.3.refs_2_), channel_id=1, source_target_pairs={{0,28},{4,0},{8,4},{12,8},{16,12},{20,16},{24,20},{28,24},{1,29},{... | collective-permute-start | bytes 1671176 | tf_op jit(solution)/shard_map/ppermute | solution.py:402
  33.8 4.3 %all-to-all-start = ((bf16[4,40,2048]{2,1,0:T(8,128)(2,1)}), bf16[4,40,2048]{2,1,0:T(8,128)(2,1)S(1)}, u32[]{:S(2)}, u32[]{:S(2)}) async-start(bf16[4,40,2048]{2,1,0:T(8,128)(2,1)} %pack.4), calls=%async_computation | async-start | bytes 1310720 | tf_op jit(solution)/shard_map/all_to_all | solution.py:408
  38.2 2.6 %copy.14 = bf16[1,1024,768]{1,2,0:T(8,128)(2,1)} copy(bf16[1,1024,768]{2,1,0:T(8,128)(2,1)} %param.13) | data formatting | bytes 3145728 | tf_op args[4]
  42.3 1.9 %collective-permute-start.2 = (bf16[128,2176]{1,0:T(8,128)(2,1)}, bf16[128,2176]{1,0:T(8,128)(2,1)}, u32[]{:S(2)}, u32[]{:S(2)}) collective-permute-start(bf16[128,2176]{1,0:T(8,128)(2,1)} %collective-permute-done.1.refs_3_), channel_id=1, source_target_pairs={{0,4},{4,8},{8,12},{12,16},{16,20},{20,24},{24,28},{28,0},{1,5},{5... | collective-permute-start | bytes 1671176 | tf_op jit(solution)/shard_map/ppermute | solution.py:402
  44.3 5.1 %collective-permute-start.5 = (bf16[128,2176]{1,0:T(8,128)(2,1)}, bf16[128,2176]{1,0:T(8,128)(2,1)}, u32[]{:S(2)}, u32[]{:S(2)}) collective-permute-start(bf16[128,2176]{1,0:T(8,128)(2,1)} %collective-permute-done.4.refs_4_), channel_id=1, source_target_pairs={{0,28},{4,0},{8,4},{12,8},{16,12},{20,16},{24,20},{28,24},{1,29},{... | collective-permute-start | bytes 1671176 | tf_op jit(solution)/shard_map/ppermute | solution.py:402
  49.4 4.0 %pack.3 = bf16[4,144,2048]{2,1,0:T(8,128)(2,1)} custom-call(s32[1]{0:T(128)} %bitcast.1.refs_0_, bf16[128,2176]{1,0:T(8,128)(2,1)S(1)} %collective-permute-done.refs_1_, bf16[128,2176]{1,0:T(8,128)(2,1)S(1)} %collective-permute-done.3.refs_2_, bf16[128,2176]{1,0:T(8,128)(2,1)} %collective-permute-done.1.refs_3_, bf16[128,2176]{1,0:T(8,128)(2,1)} %collective-permute-done.4.refs_4_), custom_call_target="tpu_custom_call" | custom-call | flops 72477573120 | bytes 267386880 | tf_op jit(solution)/shard_map/pack/pallas_call | solution.py:151
  53.5 4.3 %all-to-all-start.1 = ((bf16[4,144,2048]{2,1,0:T(8,128)(2,1)}), bf16[4,144,2048]{2,1,0:T(8,128)(2,1)S(1)}, u32[]{:S(2)}, u32[]{:S(2)}) async-start(bf16[4,144,2048]{2,1,0:T(8,128)(2,1)} %pack.3), calls=%async_computation.1 | async-start | bytes 4718592 | tf_op jit(solution)/shard_map/all_to_all | solution.py:408
  60.8 1.9 %collective-permute-start.6 = (bf16[64,2176]{1,0:T(8,128)(2,1)S(1)}, bf16[64,2176]{1,0:T(8,128)(2,1)S(1)}, u32[]{:S(2)}, u32[]{:S(2)}) collective-permute-start(bf16[64,2176]{1,0:T(8,128)(2,1)S(1)} %slice.12), channel_id=1, source_target_pairs={{0,4},{4,8},{8,12},{12,16},{16,20},{20,24},{24,28},{28,0},{1,5},{5... | collective-permute-start | bytes 835592 | tf_op jit(solution)/shard_map/ppermute | solution.py:402
  63.7 5.6 %collective-permute-start.7 = (bf16[64,2176]{1,0:T(8,128)(2,1)S(1)}, bf16[64,2176]{1,0:T(8,128)(2,1)S(1)}, u32[]{:S(2)}, u32[]{:S(2)}) collective-permute-start(bf16[64,2176]{1,0:T(8,128)(2,1)S(1)} %slice.13), channel_id=1, source_target_pairs={{0,28},{4,0},{8,4},{12,8},{16,12},{20,16},{24,20},{28,24},{1,29},{... | collective-permute-start | bytes 835592 | tf_op jit(solution)/shard_map/ppermute | solution.py:402
  69.3 4.0 %expert.3 = (bf16[32,40,1024]{2,1,0:T(8,128)(2,1)}, bf16[160,1152]{1,0:T(8,128)(2,1)}) custom-call(s32[1]{0:T(128)S(6)} %mul.14.refs_0_, bf16[160,2048]{1,0:T(8,128)(2,1)S(1)} %bitcast.22, bf16[1024,768]{1,0:T(8,128)(2,1)} %bitcast.25, bf16[1024,384]{1,0:T(8,128)(2,1)} %bitcast.34, bf16[768,1024]{1,0:T(8,128)(2,1)} %bitcast.28), custom_call_target="tpu_custom_call" | custom-call | flops 37748736000 | bytes 220200960 | tf_op jit(solution)/shard_map/expert/pallas_call | solution.py:223
  73.4 4.0 %pack.5 = bf16[4,112,2048]{2,1,0:T(8,128)(2,1)} custom-call(s32[1]{0:T(128)} %bitcast.1.refs_0_, bf16[128,2176]{1,0:T(8,128)(2,1)} %collective-permute-done.2.refs_1_, bf16[128,2176]{1,0:T(8,128)(2,1)} %collective-permute-done.5.refs_2_, bf16[64,2176]{1,0:T(8,128)(2,1)S(1)} %collective-permute-done.6.refs_3_, bf16[64,2176]{1,0:T(8,128)(2,1)S(1)} %collective-permute-done.7.refs_4_), custom_call_target="tpu_custom_call" | custom-call | flops 42278584320 | bytes 204472320 | tf_op jit(solution)/shard_map/pack/pallas_call | solution.py:151
  77.3 7.5 %all-to-all-done.1 = bf16[4,144,2048]{2,1,0:T(8,128)(2,1)S(1)} async-done(((bf16[4,144,2048]{2,1,0:T(8,128)(2,1)}), bf16[4,144,2048]{2,1,0:T(8,128)(2,1)S(1)}, u32[]{:S(2)}, u32[]{:S(2)}) %all-to-all-start.1) | async-done | bytes 2359328 | tf_op jit(solution)/shard_map/all_to_all | solution.py:408
  84.9 4.4 %all-to-all-start.2 = ((bf16[4,112,2048]{2,1,0:T(8,128)(2,1)}), bf16[4,112,2048]{2,1,0:T(8,128)(2,1)}, u32[]{:S(2)}, u32[]{:S(2)}) async-start(bf16[4,112,2048]{2,1,0:T(8,128)(2,1)} %pack.5), calls=%async_computation.2 | async-start | bytes 3670016 | tf_op jit(solution)/shard_map/all_to_all | solution.py:408
  89.3 7.8 %expert.4 = (bf16[32,40,1024]{2,1,0:T(8,128)(2,1)}, bf16[576,1152]{1,0:T(8,128)(2,1)}) custom-call(s32[4]{0:T(128)S(1)} %fusion.3.refs_0_, bf16[576,2048]{1,0:T(8,128)(2,1)S(1)} %bitcast.19, bf16[1024,768]{1,0:T(8,128)(2,1)} %bitcast.26, bf16[1024,384]{1,0:T(8,128)(2,1)} %bitcast.35, bf16[768,1024]{1,0:T(8,128)(2,1)} %bitcast.29, ...), custom_call_target="tpu_custom_call", output_to_operand_aliasing={{0}: (5, {})} | custom-call | flops 135895449600 | bytes 424673280 | tf_op jit(solution)/shard_map/expert/pallas_call | solution.py:223
  97.2 12.8 %all-to-all-done.2 = bf16[4,112,2048]{2,1,0:T(8,128)(2,1)} async-done(((bf16[4,112,2048]{2,1,0:T(8,128)(2,1)}), bf16[4,112,2048]{2,1,0:T(8,128)(2,1)}, u32[]{:S(2)}, u32[]{:S(2)}) %all-to-all-start.2) | async-done | bytes 1835040 | tf_op jit(solution)/shard_map/all_to_all | solution.py:408
  109.9 7.0 %expert.5 = (bf16[32,40,1024]{2,1,0:T(8,128)(2,1)}, bf16[448,1152]{1,0:T(8,128)(2,1)}) custom-call(s32[3]{0:T(128)S(1)} %fusion.1.refs_0_, bf16[448,2048]{1,0:T(8,128)(2,1)} %bitcast.11.refs_1_.refs_7_.refs_8_, bf16[1024,768]{1,0:T(8,128)(2,1)} %bitcast.27, bf16[1024,384]{1,0:T(8,128)(2,1)} %bitcast.36, ...), custom_call_target="tpu_custom_call", output_to_operand_aliasing={{0}: (5, {})} | custom-call | flops 105696460800 | bytes 361758720 | tf_op jit(solution)/shard_map/expert/pallas_call | solution.py:223
  116.9 5.0 %all-to-all-start.3 = ((bf16[32,40,1024]{2,1,0:T(8,128)(2,1)}), bf16[32,40,1024]{2,1,0:T(8,128)(2,1)}, u32[]{:S(2)}, u32[]{:S(2)}) async-start(bf16[32,40,1024]{2,1,0:T(8,128)(2,1)} %get-tuple-element.47), calls=%async_computation.3 | async-start | bytes 5242880 | tf_op jit(solution)/shard_map/all_to_all | solution.py:449
  121.9 8.7 %weight_terms.1 = (f32[8,64,1152]{2,1,0:T(8,128)}, bf16[8,64,1152]{2,1,0:T(8,128)(2,1)}) custom-call(s32[1]{0:T(128)} %bitcast.14.refs_0_, bf16[160,2048]{1,0:T(8,128)(2,1)} %bitcast.23, bf16[160,2048]{1,0:T(8,128)(2,1)} %bitcast.24, bf16[160,1152]{1,0:T(8,128)(2,1)} %get-tuple-element.48.refs_3_, bf16[576,2048]{1,0:T(8,128)(2,1)} %bitcast.20, ...), custom_call_target="tpu_custom_call" | custom-call | flops 167604387840 | bytes 666992640 | tf_op jit(solution)/shard_map/weight_terms/pallas_call | solution.py:293
  132.5 3.0 %collective-permute-done.8.other_ref = bf16[8,64,1152]{2,1,0:T(8,128)(2,1)S(1)} collective-permute-done((bf16[8,64,1152]{2,1,0:T(8,128)(2,1)}, bf16[8,64,1152]{2,1,0:T(8,128)(2,1)S(1)}, u32[]{:S(2)}, u32[]{:S(2)}) %collective-permute-start.8) | collective-permute-done | bytes 1179680 | tf_op jit(solution)/shard_map/ppermute | solution.py:458
  137.4 1.9 %collective-permute-start.10 = (bf16[64,1152]{1,0:T(8,128)(2,1)S(1)}, bf16[64,1152]{1,0:T(8,128)(2,1)S(1)}, u32[]{:S(2)}, u32[]{:S(2)}) collective-permute-start(bf16[64,1152]{1,0:T(8,128)(2,1)S(1)} %get-tuple-element.54), channel_id=1, source_target_pairs={{0,128},{64,192},{128,256},{192,320},{256,384},{320,448},{384,0},{... | collective-permute-start | bytes 442376 | tf_op jit(solution)/shard_map/ppermute | solution.py:462
  139.4 5.4 %collective-permute-start.11 = (bf16[64,1152]{1,0:T(8,128)(2,1)S(1)}, bf16[64,1152]{1,0:T(8,128)(2,1)S(1)}, u32[]{:S(2)}, u32[]{:S(2)}) collective-permute-start(bf16[64,1152]{1,0:T(8,128)(2,1)S(1)} %get-tuple-element.55), channel_id=1, source_target_pairs={{0,192},{64,256},{128,320},{192,384},{256,448},{320,0},{384,64},{4... | collective-permute-start | bytes 442376 | tf_op jit(solution)/shard_map/ppermute | solution.py:462
  144.7 5.0 %collective-permute-start.12 = (bf16[64,1152]{1,0:T(8,128)(2,1)S(1)}, bf16[64,1152]{1,0:T(8,128)(2,1)S(1)}, u32[]{:S(2)}, u32[]{:S(2)}) collective-permute-start(bf16[64,1152]{1,0:T(8,128)(2,1)S(1)} %get-tuple-element.56), channel_id=1, source_target_pairs={{0,256},{64,320},{128,384},{192,448},{256,0},{320,64},{384,128},{4... | collective-permute-start | bytes 442376 | tf_op jit(solution)/shard_map/ppermute | solution.py:462
  149.8 6.0 %collective-permute-start.13 = (bf16[64,1152]{1,0:T(8,128)(2,1)S(1)}, bf16[64,1152]{1,0:T(8,128)(2,1)S(1)}, u32[]{:S(2)}, u32[]{:S(2)}) collective-permute-start(bf16[64,1152]{1,0:T(8,128)(2,1)S(1)} %get-tuple-element.57), channel_id=1, source_target_pairs={{0,320},{64,384},{128,448},{192,0},{256,64},{320,128},{384,192},{4... | collective-permute-start | bytes 442376 | tf_op jit(solution)/shard_map/ppermute | solution.py:462
  155.8 1.9 %collective-permute-start.14 = (bf16[64,1152]{1,0:T(8,128)(2,1)S(1)}, bf16[64,1152]{1,0:T(8,128)(2,1)S(1)}, u32[]{:S(2)}, u32[]{:S(2)}) collective-permute-start(bf16[64,1152]{1,0:T(8,128)(2,1)S(1)} %get-tuple-element.58), channel_id=1, source_target_pairs={{0,384},{64,448},{128,0},{192,64},{256,128},{320,192},{384,256},{4... | collective-permute-start | bytes 442376 | tf_op jit(solution)/shard_map/ppermute | solution.py:462
  157.8 2.5 %collective-permute-start.15 = (bf16[64,1152]{1,0:T(8,128)(2,1)S(1)}, bf16[64,1152]{1,0:T(8,128)(2,1)S(1)}, u32[]{:S(2)}, u32[]{:S(2)}) collective-permute-start(bf16[64,1152]{1,0:T(8,128)(2,1)S(1)} %get-tuple-element.59), channel_id=1, source_target_pairs={{0,448},{64,0},{128,64},{192,128},{256,192},{320,256},{384,320},{4... | collective-permute-start | bytes 442376 | tf_op jit(solution)/shard_map/ppermute | solution.py:462
  160.3 3.4 %collective-permute-start.9 = (bf16[64,1152]{1,0:T(8,128)(2,1)S(1)}, bf16[64,1152]{1,0:T(8,128)(2,1)S(1)}, u32[]{:S(2)}, u32[]{:S(2)}) collective-permute-start(bf16[64,1152]{1,0:T(8,128)(2,1)S(1)} %get-tuple-element.53), channel_id=1, source_target_pairs={{0,64},{64,128},{128,192},{192,256},{256,320},{320,384},{384,448},... | collective-permute-start | bytes 442376 | tf_op jit(solution)/shard_map/ppermute | solution.py:462
  163.6 16.4 %all-to-all-done.3 = bf16[32,40,1024]{2,1,0:T(8,128)(2,1)} async-done(((bf16[32,40,1024]{2,1,0:T(8,128)(2,1)}), bf16[32,40,1024]{2,1,0:T(8,128)(2,1)}, u32[]{:S(2)}, u32[]{:S(2)}) %all-to-all-start.3) | async-done | bytes 2621472 | tf_op jit(solution)/shard_map/all_to_all | solution.py:449
  180.0 3.0 %combine.1 = bf16[128,1024]{1,0:T(8,128)(2,1)} custom-call(s32[8,128]{1,0:T(8,128)} %bitcast.33, bf16[1280,1024]{1,0:T(8,128)(2,1)} %bitcast.12.rows_ref), custom_call_target="tpu_custom_call" | custom-call | flops 20132659200 | bytes 173015040 | tf_op jit(solution)/shard_map/combine/pallas_call | solution.py:369
  (34 shorter events, 13.4 us)
Async XLA Ops:
  1.7 23.6 %collective-permute-start = (bf16[128,2176]{1,0:T(8,128)(2,1)S(1)}, bf16[128,2176]{1,0:T(8,128)(2,1)S(1)}, u32[]{:S(2)}, u32[]{:S(2)}) collective-permute-start(bf16[128,2176]{1,0:T(8,128)(2,1)S(1)} %payload.1.refs_1_), channel_id=1, source_target_pairs={{0,4},{4,8},{8,12},{12,16},{16,20},{20,24},{24,28},{28,0},{1,5},{5... | collective-permute-start | bytes 1671176 | tf_op jit(solution)/shard_map/ppermute | solution.py:402
  6.0 21.2 %collective-permute-start.3 = (bf16[128,2176]{1,0:T(8,128)(2,1)S(1)}, bf16[128,2176]{1,0:T(8,128)(2,1)S(1)}, u32[]{:S(2)}, u32[]{:S(2)}) collective-permute-start(bf16[128,2176]{1,0:T(8,128)(2,1)S(1)} %payload.1.refs_1_), channel_id=1, source_target_pairs={{0,28},{4,0},{8,4},{12,8},{16,12},{20,16},{24,20},{28,24},{1,29},{... | collective-permute-start | bytes 1671176 | tf_op jit(solution)/shard_map/ppermute | solution.py:402
  25.3 17.0 %collective-permute-start.1 = (bf16[128,2176]{1,0:T(8,128)(2,1)S(1)}, bf16[128,2176]{1,0:T(8,128)(2,1)}, u32[]{:S(2)}, u32[]{:S(2)}) collective-permute-start(bf16[128,2176]{1,0:T(8,128)(2,1)S(1)} %collective-permute-done.refs_1_), channel_id=1, source_target_pairs={{0,4},{4,8},{8,12},{12,16},{16,20},{20,24},{24,28},{28,0},{1,5},{5... | collective-permute-start | bytes 1671176 | tf_op jit(solution)/shard_map/ppermute | solution.py:402
  27.2 17.0 %collective-permute-start.4 = (bf16[128,2176]{1,0:T(8,128)(2,1)S(1)}, bf16[128,2176]{1,0:T(8,128)(2,1)}, u32[]{:S(2)}, u32[]{:S(2)}) collective-permute-start(bf16[128,2176]{1,0:T(8,128)(2,1)S(1)} %collective-permute-done.3.refs_2_), channel_id=1, source_target_pairs={{0,28},{4,0},{8,4},{12,8},{16,12},{20,16},{24,20},{28,24},{1,29},{... | collective-permute-start | bytes 1671176 | tf_op jit(solution)/shard_map/ppermute | solution.py:402
  33.8 7.0 %copy-start.3 = (s32[4]{0:T(128)S(1)}, s32[4]{0:T(128)}, u32[]{:S(2)}) copy-start(s32[4]{0:T(128)} %constant.67.clone) | copy-start | bytes 52
  33.8 7.0 %copy-start.2 = (s32[3]{0:T(128)S(1)}, s32[3]{0:T(128)}, u32[]{:S(2)}) copy-start(s32[3]{0:T(128)} %constant.68.clone) | copy-start | bytes 40
  33.8 19.6 %all-to-all-start = ((bf16[4,40,2048]{2,1,0:T(8,128)(2,1)}), bf16[4,40,2048]{2,1,0:T(8,128)(2,1)S(1)}, u32[]{:S(2)}, u32[]{:S(2)}) async-start(bf16[4,40,2048]{2,1,0:T(8,128)(2,1)} %pack.4), calls=%async_computation | async-start | bytes 1310720 | tf_op jit(solution)/shard_map/all_to_all | solution.py:408
  42.3 16.3 %collective-permute-start.2 = (bf16[128,2176]{1,0:T(8,128)(2,1)}, bf16[128,2176]{1,0:T(8,128)(2,1)}, u32[]{:S(2)}, u32[]{:S(2)}) collective-permute-start(bf16[128,2176]{1,0:T(8,128)(2,1)} %collective-permute-done.1.refs_3_), channel_id=1, source_target_pairs={{0,4},{4,8},{8,12},{12,16},{16,20},{20,24},{24,28},{28,0},{1,5},{5... | collective-permute-start | bytes 1671176 | tf_op jit(solution)/shard_map/ppermute | solution.py:402
  44.3 15.6 %collective-permute-start.5 = (bf16[128,2176]{1,0:T(8,128)(2,1)}, bf16[128,2176]{1,0:T(8,128)(2,1)}, u32[]{:S(2)}, u32[]{:S(2)}) collective-permute-start(bf16[128,2176]{1,0:T(8,128)(2,1)} %collective-permute-done.4.refs_4_), channel_id=1, source_target_pairs={{0,28},{4,0},{8,4},{12,8},{16,12},{20,16},{24,20},{28,24},{1,29},{... | collective-permute-start | bytes 1671176 | tf_op jit(solution)/shard_map/ppermute | solution.py:402
  53.5 15.9 %copy-start.1 = (bf16[4,40,2048]{2,1,0:T(8,128)(2,1)}, bf16[4,40,2048]{2,1,0:T(8,128)(2,1)S(1)}, u32[]{:S(2)}) copy-start(bf16[4,40,2048]{2,1,0:T(8,128)(2,1)S(1)} %all-to-all-done) | copy-start | bytes 1966084
  53.5 31.4 %all-to-all-start.1 = ((bf16[4,144,2048]{2,1,0:T(8,128)(2,1)}), bf16[4,144,2048]{2,1,0:T(8,128)(2,1)S(1)}, u32[]{:S(2)}, u32[]{:S(2)}) async-start(bf16[4,144,2048]{2,1,0:T(8,128)(2,1)} %pack.3), calls=%async_computation.1 | async-start | bytes 4718592 | tf_op jit(solution)/shard_map/all_to_all | solution.py:408
  60.8 12.6 %collective-permute-start.6 = (bf16[64,2176]{1,0:T(8,128)(2,1)S(1)}, bf16[64,2176]{1,0:T(8,128)(2,1)S(1)}, u32[]{:S(2)}, u32[]{:S(2)}) collective-permute-start(bf16[64,2176]{1,0:T(8,128)(2,1)S(1)} %slice.12), channel_id=1, source_target_pairs={{0,4},{4,8},{8,12},{12,16},{16,20},{20,24},{24,28},{28,0},{1,5},{5... | collective-permute-start | bytes 835592 | tf_op jit(solution)/shard_map/ppermute | solution.py:402
  63.7 9.7 %collective-permute-start.7 = (bf16[64,2176]{1,0:T(8,128)(2,1)S(1)}, bf16[64,2176]{1,0:T(8,128)(2,1)S(1)}, u32[]{:S(2)}, u32[]{:S(2)}) collective-permute-start(bf16[64,2176]{1,0:T(8,128)(2,1)S(1)} %slice.13), channel_id=1, source_target_pairs={{0,28},{4,0},{8,4},{12,8},{16,12},{20,16},{24,20},{28,24},{1,29},{... | collective-permute-start | bytes 835592 | tf_op jit(solution)/shard_map/ppermute | solution.py:402
  84.9 12.3 %copy-start = (bf16[4,144,2048]{2,1,0:T(8,128)(2,1)}, bf16[4,144,2048]{2,1,0:T(8,128)(2,1)S(1)}, u32[]{:S(2)}) copy-start(bf16[4,144,2048]{2,1,0:T(8,128)(2,1)S(1)} %all-to-all-done.1) | copy-start | bytes 7077892
  84.9 25.0 %all-to-all-start.2 = ((bf16[4,112,2048]{2,1,0:T(8,128)(2,1)}), bf16[4,112,2048]{2,1,0:T(8,128)(2,1)}, u32[]{:S(2)}, u32[]{:S(2)}) async-start(bf16[4,112,2048]{2,1,0:T(8,128)(2,1)} %pack.5), calls=%async_computation.2 | async-start | bytes 3670016 | tf_op jit(solution)/shard_map/all_to_all | solution.py:408
  116.9 63.1 %all-to-all-start.3 = ((bf16[32,40,1024]{2,1,0:T(8,128)(2,1)}), bf16[32,40,1024]{2,1,0:T(8,128)(2,1)}, u32[]{:S(2)}, u32[]{:S(2)}) async-start(bf16[32,40,1024]{2,1,0:T(8,128)(2,1)} %get-tuple-element.47), calls=%async_computation.3 | async-start | bytes 5242880 | tf_op jit(solution)/shard_map/all_to_all | solution.py:449
  130.6 4.9 %collective-permute-start.8 = (bf16[8,64,1152]{2,1,0:T(8,128)(2,1)}, bf16[8,64,1152]{2,1,0:T(8,128)(2,1)S(1)}, u32[]{:S(2)}, u32[]{:S(2)}) collective-permute-start(bf16[8,64,1152]{2,1,0:T(8,128)(2,1)} %get-tuple-element.52), channel_id=1, source_target_pairs={{0,32},{32,0},{1,33},{33,1},{2,34},{34,2},{3,35},{35,3},{4,36},{36... | collective-permute-start | bytes 3538952 | tf_op jit(solution)/shard_map/ppermute | solution.py:458
  137.4 20.3 %collective-permute-start.10 = (bf16[64,1152]{1,0:T(8,128)(2,1)S(1)}, bf16[64,1152]{1,0:T(8,128)(2,1)S(1)}, u32[]{:S(2)}, u32[]{:S(2)}) collective-permute-start(bf16[64,1152]{1,0:T(8,128)(2,1)S(1)} %get-tuple-element.54), channel_id=1, source_target_pairs={{0,128},{64,192},{128,256},{192,320},{256,384},{320,448},{384,0},{... | collective-permute-start | bytes 442376 | tf_op jit(solution)/shard_map/ppermute | solution.py:462
  139.4 20.9 %collective-permute-start.11 = (bf16[64,1152]{1,0:T(8,128)(2,1)S(1)}, bf16[64,1152]{1,0:T(8,128)(2,1)S(1)}, u32[]{:S(2)}, u32[]{:S(2)}) collective-permute-start(bf16[64,1152]{1,0:T(8,128)(2,1)S(1)} %get-tuple-element.55), channel_id=1, source_target_pairs={{0,192},{64,256},{128,320},{192,384},{256,448},{320,0},{384,64},{4... | collective-permute-start | bytes 442376 | tf_op jit(solution)/shard_map/ppermute | solution.py:462
  144.7 38.3 %collective-permute-start.12 = (bf16[64,1152]{1,0:T(8,128)(2,1)S(1)}, bf16[64,1152]{1,0:T(8,128)(2,1)S(1)}, u32[]{:S(2)}, u32[]{:S(2)}) collective-permute-start(bf16[64,1152]{1,0:T(8,128)(2,1)S(1)} %get-tuple-element.56), channel_id=1, source_target_pairs={{0,256},{64,320},{128,384},{192,448},{256,0},{320,64},{384,128},{4... | collective-permute-start | bytes 442376 | tf_op jit(solution)/shard_map/ppermute | solution.py:462
  149.8 33.2 %collective-permute-start.13 = (bf16[64,1152]{1,0:T(8,128)(2,1)S(1)}, bf16[64,1152]{1,0:T(8,128)(2,1)S(1)}, u32[]{:S(2)}, u32[]{:S(2)}) collective-permute-start(bf16[64,1152]{1,0:T(8,128)(2,1)S(1)} %get-tuple-element.57), channel_id=1, source_target_pairs={{0,320},{64,384},{128,448},{192,0},{256,64},{320,128},{384,192},{4... | collective-permute-start | bytes 442376 | tf_op jit(solution)/shard_map/ppermute | solution.py:462
  155.8 27.2 %collective-permute-start.14 = (bf16[64,1152]{1,0:T(8,128)(2,1)S(1)}, bf16[64,1152]{1,0:T(8,128)(2,1)S(1)}, u32[]{:S(2)}, u32[]{:S(2)}) collective-permute-start(bf16[64,1152]{1,0:T(8,128)(2,1)S(1)} %get-tuple-element.58), channel_id=1, source_target_pairs={{0,384},{64,448},{128,0},{192,64},{256,128},{320,192},{384,256},{4... | collective-permute-start | bytes 442376 | tf_op jit(solution)/shard_map/ppermute | solution.py:462
  157.8 25.3 %collective-permute-start.15 = (bf16[64,1152]{1,0:T(8,128)(2,1)S(1)}, bf16[64,1152]{1,0:T(8,128)(2,1)S(1)}, u32[]{:S(2)}, u32[]{:S(2)}) collective-permute-start(bf16[64,1152]{1,0:T(8,128)(2,1)S(1)} %get-tuple-element.59), channel_id=1, source_target_pairs={{0,448},{64,0},{128,64},{192,128},{256,192},{320,256},{384,320},{4... | collective-permute-start | bytes 442376 | tf_op jit(solution)/shard_map/ppermute | solution.py:462
  160.3 22.8 %collective-permute-start.9 = (bf16[64,1152]{1,0:T(8,128)(2,1)S(1)}, bf16[64,1152]{1,0:T(8,128)(2,1)S(1)}, u32[]{:S(2)}, u32[]{:S(2)}) collective-permute-start(bf16[64,1152]{1,0:T(8,128)(2,1)S(1)} %get-tuple-element.53), channel_id=1, source_target_pairs={{0,64},{64,128},{128,192},{192,256},{256,320},{320,384},{384,448},... | collective-permute-start | bytes 442376 | tf_op jit(solution)/shard_map/ppermute | solution.py:462

commit v6 on v5

--- a/solution.py
+++ b/solution.py
@@ -180,9 +180,10 @@
         started(down_ref, down_in, in_sems.at[2]),
         started(turned_ref, turned_in, in_sems.at[4]),
     ]
-    for copy in copies:
-        copy.wait()
+    copies[0].wait()
+    copies[1].wait()
     projected = jnp.dot(rows_in[:, :width], proj_in[...], preferred_element_type=F32)
+    copies[2].wait()
     grad_hidden = jnp.dot(rows_in[:, width:], down_in[...], preferred_element_type=F32)
     gate_pre = projected[:, :hidden_units]
     up_part = projected[:, hidden_units:]
@@ -194,6 +195,7 @@
     terms[:, 2 * hidden_units :] = (activated * up_part).astype(BF16)
     terms_copy = started(terms, terms_ref, in_sems.at[3])
     back[count:] = jnp.zeros((back.shape[0] - count, width), F32)
+    copies[3].wait()
     back[:count] = jnp.dot(
         terms[:, : 2 * hidden_units], turned_in[...], preferred_element_type=F32
     )
@@ -331,17 +333,14 @@
     )(y_index, in_hbm(keep), other)
 
 
-def combine_kernel(experts, routes_ref, rows_ref, out_ref, routes_in, rows_in, made, sems):
+def choose_kernel(experts, routes_ref, pick_ref):
     top, tokens = routes_ref.shape
-    total_rows = rows_ref.shape[0]
+    total_rows = pick_ref.shape[1]
     slot_rows = total_rows // experts
-    routes_copy = started(routes_ref, routes_in, sems.at[0])
-    rows_copy = started(rows_ref, rows_in, sems.at[1])
-    routes_copy.wait()
     labels = lax.broadcasted_iota(jnp.int32, (LANES, tokens), 0)
     mask = jnp.zeros((LANES, tokens), F32)
     for entry in range(top):
-        mask += jnp.where(routes_in[entry : entry + 1] == labels, 1.0, 0.0)
+        mask += jnp.where(routes_ref[entry : entry + 1] == labels, 1.0, 0.0)
     mask = mask.T[:, :experts]
     before = (
         lax.broadcasted_iota(jnp.int32, (tokens, tokens), 1)
@@ -357,30 +356,40 @@
     held = jnp.dot(
         jnp.where(mask > 0.0, rank, -1.0).astype(BF16), spread, preferred_element_type=F32
     )
-    pick = jnp.where(held == wanted, 1.0, 0.0).astype(BF16)
-    rows_copy.wait()
-    made[...] = jnp.dot(pick, rows_in[...], preferred_element_type=F32).astype(BF16)
-    started(made, out_ref, sems.at[2]).wait()
-
-
-def combine(routes, rows_back, experts):
-    top, tokens = routes.shape
-    total_rows, width = rows_back.shape
-    return pl.pallas_call(
-        functools.partial(combine_kernel, experts),
+    pick_ref[...] = jnp.where(held == wanted, 1.0, 0.0).astype(BF16)
+
+
+def choose(routes, experts, slot_rows):
+    tokens = routes.shape[1]
+    return pl.pallas_call(
+        functools.partial(choose_kernel, experts),
+        out_shape=jax.ShapeDtypeStruct((tokens, experts * slot_rows), BF16),
+        compiler_params=params(8),
+        cost_estimate=cost(4 * tokens * experts * experts * slot_rows, 1e6),
+        name="choose",
+    )(routes)
+
+
+def combine_kernel(pick_ref, rows_ref, out_ref, made, sems):
+    made[...] = jnp.dot(
+        pick_ref[...], rows_ref[...], preferred_element_type=F32
+    ).astype(BF16)
+    started(made, out_ref, sems.at[0]).wait()
+
+
+def combine(pick, rows_back):
+    tokens, total_rows = pick.shape
+    width = rows_back.shape[1]
+    return pl.pallas_call(
+        combine_kernel,
         out_shape=pltpu.HBM((tokens, width), BF16),
-        in_specs=[IN_HBM] * 2,
+        in_specs=[pl.BlockSpec(memory_space=pltpu.VMEM)] * 2,
         out_specs=IN_HBM,
-        scratch_shapes=[
-            pltpu.VMEM((top, tokens), jnp.int32),
-            pltpu.VMEM((total_rows, width), BF16),
-            pltpu.VMEM((tokens, width), BF16),
-            DMA((3,)),
-        ],
-        compiler_params=params(16),
+        scratch_shapes=[pltpu.VMEM((tokens, width), BF16), DMA((1,))],
+        compiler_params=params(8),
         cost_estimate=cost(2 * tokens * total_rows * width, 2 * (total_rows + tokens) * width),
         name="combine",
-    )(in_hbm(routes), in_hbm(rows_back))
+    )(pick, rows_back)
 
 
 def per_device(x_in, grad_out, routes, gate_probs, gate_up, down):
@@ -428,20 +437,20 @@
     own = payload(x_in, grad_out, routes, gate_probs.T)
     fore1, back1 = shift(own, 1), shift(own, -1)
     fore2, back2 = shift(fore1, 1), shift(back1, -1)
-    packed0 = packed(own)
-    rows0 = crossed(packed0)
+    rows0 = crossed(packed(own, fore1, back1))
     fore3, back3 = shift(fore2, 1), shift(back2, -1)
-    packed1, rows0 = lax.optimization_barrier((packed(fore1, back1, fore2, back2), rows0))
+    packed1 = packed(fore2, back2)
+    onward_f, onward_b, _ = lax.optimization_barrier((fore3, back3, packed1))
+    packed1, rows0 = lax.optimization_barrier((packed1, rows0))
     rows1 = crossed(packed1)
-    onward_f, onward_b, _ = lax.optimization_barrier((fore3, back3, packed1))
     fore4, back4 = shift(onward_f[:half], 1), shift(onward_b[half:], -1)
     rows0 = flat(rows0)
-    away, terms0 = run(places(0), rows0, None)
+    away, terms0 = run(places(0, -1, 1), rows0, None)
     packed2 = packed(fore3, back3, fore4, back4)
     packed2, rows1, away = lax.optimization_barrier((packed2, rows1, away))
     rows2 = crossed(packed2)
     rows1 = flat(rows1)
-    away, terms1 = run(places(-1, 1, -2, 2), rows1, away)
+    away, terms1 = run(places(-2, 2), rows1, away)
     rows2, away = lax.optimization_barrier((rows2, away))
     rows2 = flat(rows2)
     away, terms2 = run(places(-3, 3, 4), rows2, away)
@@ -462,13 +471,15 @@
         lax.ppermute(shares[by], "y", [(i, (i + by) % y_size) for i in range(y_size)])
         for by in range(1, y_size)
     ]
-    grad_in = combine(routes, home.reshape(-1, width), experts)
-    grad_in, *moved = lax.optimization_barrier((grad_in, *moved))
     total = shares[0].astype(F32)
     for share in moved:
         total = total + share.astype(F32)
     split = total.shape[1] // 3 * 2
-    return (grad_in, total[None, :, :split], total[None, :, split:])
+    grads = (total[None, :, :split], total[None, :, split:])
+    pick = choose(routes, experts, slot_rows)
+    home, pick, grads = lax.optimization_barrier((home, pick, grads))
+    grad_in = combine(pick, home.reshape(-1, width))
+    return (grad_in, *grads)
 
 
 def solution(mesh):

time: 186 us -> 185 us (level)
  the two profiles are of different devices: /device:TPU:48 before, /device:TPU:1 now
where the time goes in v6:
time: 185 us; the launch traced here: 182 us
  starting transfers between devices  87.1 us (47%)
  waiting for transfers between devices  46.1 us (25%)
  Pallas kernels  42.2 us (23%)
  local copies, waits for them, and re-layouts  5.43 us (3%)
    ppermute x8, starting transfers between devices, shift(): lax.ppermute(value, 'z', [(i, (i + by) % z_size) for i in range(z_size)])  33.6 us
    ppermute x7, starting transfers between devices, per_device(): lax.ppermute(shares[by], 'y', [(i, (i + by) % y_size) for i in range(y_si...  28.4 us
    pallas_call x3, Pallas kernels, expert_rows(): pl.pallas_call(functools.partial(expert_kernel, capacity, slot_rows), out...  18.1 us
    ppermute x8, waiting for transfers between devices, shift(): lax.ppermute(value, 'z', [(i, (i + by) % z_size) for i in range(z_size)])  16.9 us
    all_to_all x3, waiting for transfers between devices, crossed(): return lax.all_to_all(value, 'x', split_axis=0, concat_axis=0, tiled=True)  16 us
    all_to_all x3, starting transfers between devices, crossed(): return lax.all_to_all(value, 'x', split_axis=0, concat_axis=0, tiled=True)  11.9 us
    ppermute x7, waiting for transfers between devices, per_device(): lax.ppermute(shares[by], 'y', [(i, (i + by) % y_size) for i in range(y_si...  10.6 us
    pallas_call x3, Pallas kernels, pack(): pl.pallas_call(functools.partial(pack_kernel, top, capacity, width, token...  9.26 us
  transfers between devices with their start and end apart: 20, of which 9 were waited for; matrix products, arithmetic and copies ran while one was open for 3% of the time, Pallas kernels for 17%

profile of v6, /device:TPU:1, one launch (start us, length us, event | category | flops | bytes accessed | tf_op | source)
XLA Modules:
  0.0 182.2 jit_solution(12929924553153257886)
XLA Ops:
  1.8 5.0 %collective-permute-start = (bf16[128,2176]{1,0:T(8,128)(2,1)S(1)}, bf16[128,2176]{1,0:T(8,128)(2,1)S(1)}, u32[]{:S(2)}, u32[]{:S(2)}) collective-permute-start(bf16[128,2176]{1,0:T(8,128)(2,1)S(1)} %payload.1.refs_1_), channel_id=1, source_target_pairs={{0,4},{4,8},{8,12},{12,16},{16,20},{20,24},{24,28},{28,0},{1,5},{5... | collective-permute-start | bytes 1671176 | tf_op jit(solution)/shard_map/ppermute | solution.py:411
  6.8 8.6 %collective-permute-start.3 = (bf16[128,2176]{1,0:T(8,128)(2,1)S(1)}, bf16[128,2176]{1,0:T(8,128)(2,1)S(1)}, u32[]{:S(2)}, u32[]{:S(2)}) collective-permute-start(bf16[128,2176]{1,0:T(8,128)(2,1)S(1)} %payload.1.refs_1_), channel_id=1, source_target_pairs={{0,28},{4,0},{8,4},{12,8},{16,12},{20,16},{24,20},{28,24},{1,29},{... | collective-permute-start | bytes 1671176 | tf_op jit(solution)/shard_map/ppermute | solution.py:411
  15.4 2.6 %copy.14 = bf16[1,1024,768]{1,2,0:T(8,128)(2,1)} copy(bf16[1,1024,768]{2,1,0:T(8,128)(2,1)} %param.13) | data formatting | bytes 3145728 | tf_op args[4]
  18.0 7.8 %collective-permute-done.refs_2_ = bf16[128,2176]{1,0:T(8,128)(2,1)S(1)} collective-permute-done((bf16[128,2176]{1,0:T(8,128)(2,1)S(1)}, bf16[128,2176]{1,0:T(8,128)(2,1)S(1)}, u32[]{:S(2)}, u32[]{:S(2)}) %collective-permute-start) | collective-permute-done | bytes 557088 | tf_op jit(solution)/shard_map/ppermute | solution.py:411
  27.7 4.6 %collective-permute-start.4 = (bf16[128,2176]{1,0:T(8,128)(2,1)S(1)}, bf16[128,2176]{1,0:T(8,128)(2,1)}, u32[]{:S(2)}, u32[]{:S(2)}) collective-permute-start(bf16[128,2176]{1,0:T(8,128)(2,1)S(1)} %collective-permute-done.3.refs_3_), channel_id=1, source_target_pairs={{0,28},{4,0},{8,4},{12,8},{16,12},{20,16},{24,20},{28,24},{1,29},{... | collective-permute-start | bytes 1671176 | tf_op jit(solution)/shard_map/ppermute | solution.py:411
  32.3 3.2 %pack.5 = bf16[4,112,2048]{2,1,0:T(8,128)(2,1)} custom-call(s32[1]{0:T(128)} %bitcast.refs_0_, bf16[128,2176]{1,0:T(8,128)(2,1)S(1)} %payload.1.refs_1_, bf16[128,2176]{1,0:T(8,128)(2,1)S(1)} %collective-permute-done.refs_2_, bf16[128,2176]{1,0:T(8,128)(2,1)S(1)} %collective-permute-done.3.refs_3_), custom_call_target="tpu_custom_call" | custom-call | flops 42278584320 | bytes 204472320 | tf_op jit(solution)/shard_map/pack/pallas_call | solution.py:151
  35.4 4.0 %all-to-all-start = ((bf16[4,112,2048]{2,1,0:T(8,128)(2,1)}), bf16[4,112,2048]{2,1,0:T(8,128)(2,1)S(1)}, u32[]{:S(2)}, u32[]{:S(2)}) async-start(bf16[4,112,2048]{2,1,0:T(8,128)(2,1)} %pack.5), calls=%async_computation | async-start | bytes 3670016 | tf_op jit(solution)/shard_map/all_to_all | solution.py:417
  43.7 4.6 %collective-permute-start.5 = (bf16[128,2176]{1,0:T(8,128)(2,1)}, bf16[128,2176]{1,0:T(8,128)(2,1)S(1)}, u32[]{:S(2)}, u32[]{:S(2)}) collective-permute-start(bf16[128,2176]{1,0:T(8,128)(2,1)} %collective-permute-done.4.refs_2_), channel_id=1, source_target_pairs={{0,28},{4,0},{8,4},{12,8},{16,12},{20,16},{24,20},{28,24},{1,29},{... | collective-permute-start | bytes 1671176 | tf_op jit(solution)/shard_map/ppermute | solution.py:411
  48.2 2.9 %pack.3 = bf16[4,72,2048]{2,1,0:T(8,128)(2,1)} custom-call(s32[1]{0:T(128)} %bitcast.refs_0_, bf16[128,2176]{1,0:T(8,128)(2,1)S(1)} %collective-permute-done.1.refs_1_, bf16[128,2176]{1,0:T(8,128)(2,1)} %collective-permute-done.4.refs_2_), custom_call_target="tpu_custom_call" | custom-call | flops 18119393280 | bytes 133693440 | tf_op jit(solution)/shard_map/pack/pallas_call | solution.py:151
  51.2 5.6 %collective-permute-done.2.refs_1_ = bf16[128,2176]{1,0:T(8,128)(2,1)S(1)} collective-permute-done((bf16[128,2176]{1,0:T(8,128)(2,1)S(1)}, bf16[128,2176]{1,0:T(8,128)(2,1)S(1)}, u32[]{:S(2)}, u32[]{:S(2)}) %collective-permute-start.2) | collective-permute-done | bytes 557088 | tf_op jit(solution)/shard_map/ppermute | solution.py:411
  61.4 5.2 %collective-permute-start.7 = (bf16[64,2176]{1,0:T(8,128)(2,1)}, bf16[64,2176]{1,0:T(8,128)(2,1)S(1)}, u32[]{:S(2)}, u32[]{:S(2)}) collective-permute-start(bf16[64,2176]{1,0:T(8,128)(2,1)} %slice.13), channel_id=1, source_target_pairs={{0,28},{4,0},{8,4},{12,8},{16,12},{20,16},{24,20},{28,24},{1,29},{... | collective-permute-start | bytes 835592 | tf_op jit(solution)/shard_map/ppermute | solution.py:411
  66.7 4.3 %all-to-all-start.1 = ((bf16[4,72,2048]{2,1,0:T(8,128)(2,1)}), bf16[4,72,2048]{2,1,0:T(8,128)(2,1)}, u32[]{:S(2)}, u32[]{:S(2)}) async-start(bf16[4,72,2048]{2,1,0:T(8,128)(2,1)} %pack.3), calls=%async_computation.1 | async-start | bytes 2359296 | tf_op jit(solution)/shard_map/all_to_all | solution.py:417
  71.0 6.3 %expert.3 = (bf16[32,40,1024]{2,1,0:T(8,128)(2,1)}, bf16[448,1152]{1,0:T(8,128)(2,1)}) custom-call(s32[3]{0:T(128)S(1)} %get-tuple-element.62.refs_0_, bf16[448,2048]{1,0:T(8,128)(2,1)S(1)} %bitcast.18, bf16[1024,768]{1,0:T(8,128)(2,1)} %bitcast.26, bf16[1024,384]{1,0:T(8,128)(2,1)} %bitcast.33, bf16[768,1024]{1,0:T(8,128)(2,1)} %bitcast.29), custom_call_target="tpu_custom_call" | custom-call | flops 105696460800 | bytes 361758720 | tf_op jit(solution)/shard_map/expert/pallas_call | solution.py:225
  77.3 3.1 %pack.4 = bf16[4,112,2048]{2,1,0:T(8,128)(2,1)} custom-call(s32[1]{0:T(128)} %bitcast.refs_0_, bf16[128,2176]{1,0:T(8,128)(2,1)S(1)} %collective-permute-done.2.refs_1_, bf16[128,2176]{1,0:T(8,128)(2,1)S(1)} %collective-permute-done.5.refs_2_, bf16[64,2176]{1,0:T(8,128)(2,1)S(1)} %collective-permute-done.6.refs_3_, ...), custom_call_target="tpu_custom_call" | custom-call | flops 42278584320 | bytes 204472320 | tf_op jit(solution)/shard_map/pack/pallas_call | solution.py:151
  80.5 3.1 %all-to-all-done.1 = bf16[4,72,2048]{2,1,0:T(8,128)(2,1)} async-done(((bf16[4,72,2048]{2,1,0:T(8,128)(2,1)}), bf16[4,72,2048]{2,1,0:T(8,128)(2,1)}, u32[]{:S(2)}, u32[]{:S(2)}) %all-to-all-start.1) | async-done | bytes 1179680 | tf_op jit(solution)/shard_map/all_to_all | solution.py:417
  83.6 3.6 %all-to-all-start.2 = ((bf16[4,112,2048]{2,1,0:T(8,128)(2,1)}), bf16[4,112,2048]{2,1,0:T(8,128)(2,1)S(1)}, u32[]{:S(2)}, u32[]{:S(2)}) async-start(bf16[4,112,2048]{2,1,0:T(8,128)(2,1)} %pack.4), calls=%async_computation.2 | async-start | bytes 3670016 | tf_op jit(solution)/shard_map/all_to_all | solution.py:417
  87.2 5.4 %expert.4 = (bf16[32,40,1024]{2,1,0:T(8,128)(2,1)}, bf16[288,1152]{1,0:T(8,128)(2,1)}) custom-call(s32[2]{0:T(128)S(1)} %fusion.5.refs_0_, bf16[288,2048]{1,0:T(8,128)(2,1)} %bitcast.8.refs_1_.refs_4_.refs_5_, bf16[1024,768]{1,0:T(8,128)(2,1)} %bitcast.27, bf16[1024,384]{1,0:T(8,128)(2,1)} %bitcast.34, ...), custom_call_target="tpu_custom_call", output_to_operand_aliasing={{0}: (5, {})} | custom-call | flops 67947724800 | bytes 283115520 | tf_op jit(solution)/shard_map/expert/pallas_call | solution.py:225
  92.6 12.9 %all-to-all-done.2 = bf16[4,112,2048]{2,1,0:T(8,128)(2,1)S(1)} async-done(((bf16[4,112,2048]{2,1,0:T(8,128)(2,1)}), bf16[4,112,2048]{2,1,0:T(8,128)(2,1)S(1)}, u32[]{:S(2)}, u32[]{:S(2)}) %all-to-all-start.2) | async-done | bytes 1835040 | tf_op jit(solution)/shard_map/all_to_all | solution.py:417
  105.5 6.3 %expert.5 = (bf16[32,40,1024]{2,1,0:T(8,128)(2,1)}, bf16[448,1152]{1,0:T(8,128)(2,1)}) custom-call(s32[3]{0:T(128)S(1)} %get-tuple-element.61.refs_0_, bf16[448,2048]{1,0:T(8,128)(2,1)S(1)} %bitcast.21, bf16[1024,768]{1,0:T(8,128)(2,1)} %bitcast.28, bf16[1024,384]{1,0:T(8,128)(2,1)} %bitcast.35, ...), custom_call_target="tpu_custom_call", output_to_operand_aliasing={{0}: (5, {})} | custom-call | flops 105696460800 | bytes 361758720 | tf_op jit(solution)/shard_map/expert/pallas_call | solution.py:225
  111.8 5.0 %all-to-all-start.3 = ((bf16[32,40,1024]{2,1,0:T(8,128)(2,1)}), bf16[32,40,1024]{2,1,0:T(8,128)(2,1)}, u32[]{:S(2)}, u32[]{:S(2)}) async-start(bf16[32,40,1024]{2,1,0:T(8,128)(2,1)} %get-tuple-element.43), calls=%async_computation.3 | async-start | bytes 5242880 | tf_op jit(solution)/shard_map/all_to_all | solution.py:458
  116.8 8.4 %weight_terms.1 = (f32[8,64,1152]{2,1,0:T(8,128)}, bf16[8,64,1152]{2,1,0:T(8,128)(2,1)}) custom-call(s32[1]{0:T(128)} %bitcast.12.refs_0_, bf16[448,2048]{1,0:T(8,128)(2,1)} %bitcast.19, bf16[448,2048]{1,0:T(8,128)(2,1)} %bitcast.20, bf16[448,1152]{1,0:T(8,128)(2,1)} %get-tuple-element.44.refs_3_, bf16[288,2048]{1,0:T(8,128)(2,1)} %bitcast.8.refs_1_.refs_4_.refs_5_, ...), custom_call_target="tpu_custom_call" | custom-call | flops 167604387840 | bytes 666992640 | tf_op jit(solution)/shard_map/weight_terms/pallas_call | solution.py:295
  125.2 8.1 %collective-permute-start.8 = (bf16[8,64,1152]{2,1,0:T(8,128)(2,1)}, bf16[8,64,1152]{2,1,0:T(8,128)(2,1)S(1)}, u32[]{:S(2)}, u32[]{:S(2)}) collective-permute-start(bf16[8,64,1152]{2,1,0:T(8,128)(2,1)} %get-tuple-element.48), channel_id=1, source_target_pairs={{0,32},{32,0},{1,33},{33,1},{2,34},{34,2},{3,35},{35,3},{4,36},{36... | collective-permute-start | bytes 3538952 | tf_op jit(solution)/shard_map/ppermute | solution.py:467
  133.4 2.7 %collective-permute-done.8.other_ref = bf16[8,64,1152]{2,1,0:T(8,128)(2,1)S(1)} collective-permute-done((bf16[8,64,1152]{2,1,0:T(8,128)(2,1)}, bf16[8,64,1152]{2,1,0:T(8,128)(2,1)S(1)}, u32[]{:S(2)}, u32[]{:S(2)}) %collective-permute-start.8) | collective-permute-done | bytes 1179680 | tf_op jit(solution)/shard_map/ppermute | solution.py:467
  138.0 4.2 %collective-permute-start.10 = (bf16[64,1152]{1,0:T(8,128)(2,1)S(1)}, bf16[64,1152]{1,0:T(8,128)(2,1)S(1)}, u32[]{:S(2)}, u32[]{:S(2)}) collective-permute-start(bf16[64,1152]{1,0:T(8,128)(2,1)S(1)} %get-tuple-element.51), channel_id=1, source_target_pairs={{0,128},{64,192},{128,256},{192,320},{256,384},{320,448},{384,0},{... | collective-permute-start | bytes 442376 | tf_op jit(solution)/shard_map/ppermute | solution.py:471
  142.2 5.5 %collective-permute-start.11 = (bf16[64,1152]{1,0:T(8,128)(2,1)S(1)}, bf16[64,1152]{1,0:T(8,128)(2,1)S(1)}, u32[]{:S(2)}, u32[]{:S(2)}) collective-permute-start(bf16[64,1152]{1,0:T(8,128)(2,1)S(1)} %get-tuple-element.52), channel_id=1, source_target_pairs={{0,192},{64,256},{128,320},{192,384},{256,448},{320,0},{384,64},{4... | collective-permute-start | bytes 442376 | tf_op jit(solution)/shard_map/ppermute | solution.py:471
  147.7 2.6 %collective-permute-start.12 = (bf16[64,1152]{1,0:T(8,128)(2,1)S(1)}, bf16[64,1152]{1,0:T(8,128)(2,1)S(1)}, u32[]{:S(2)}, u32[]{:S(2)}) collective-permute-start(bf16[64,1152]{1,0:T(8,128)(2,1)S(1)} %get-tuple-element.53), channel_id=1, source_target_pairs={{0,256},{64,320},{128,384},{192,448},{256,0},{320,64},{384,128},{4... | collective-permute-start | bytes 442376 | tf_op jit(solution)/shard_map/ppermute | solution.py:471
  150.4 5.8 %collective-permute-start.13 = (bf16[64,1152]{1,0:T(8,128)(2,1)S(1)}, bf16[64,1152]{1,0:T(8,128)(2,1)S(1)}, u32[]{:S(2)}, u32[]{:S(2)}) collective-permute-start(bf16[64,1152]{1,0:T(8,128)(2,1)S(1)} %get-tuple-element.54), channel_id=1, source_target_pairs={{0,320},{64,384},{128,448},{192,0},{256,64},{320,128},{384,192},{4... | collective-permute-start | bytes 442376 | tf_op jit(solution)/shard_map/ppermute | solution.py:471
  156.2 5.0 %collective-permute-start.14 = (bf16[64,1152]{1,0:T(8,128)(2,1)S(1)}, bf16[64,1152]{1,0:T(8,128)(2,1)S(1)}, u32[]{:S(2)}, u32[]{:S(2)}) collective-permute-start(bf16[64,1152]{1,0:T(8,128)(2,1)S(1)} %get-tuple-element.55), channel_id=1, source_target_pairs={{0,384},{64,448},{128,0},{192,64},{256,128},{320,192},{384,256},{4... | collective-permute-start | bytes 442376 | tf_op jit(solution)/shard_map/ppermute | solution.py:471
  163.1 3.4 %collective-permute-start.9 = (bf16[64,1152]{1,0:T(8,128)(2,1)S(1)}, bf16[64,1152]{1,0:T(8,128)(2,1)S(1)}, u32[]{:S(2)}, u32[]{:S(2)}) collective-permute-start(bf16[64,1152]{1,0:T(8,128)(2,1)S(1)} %get-tuple-element.50), channel_id=1, source_target_pairs={{0,64},{64,128},{128,192},{192,256},{256,320},{320,384},{384,448},... | collective-permute-start | bytes 442376 | tf_op jit(solution)/shard_map/ppermute | solution.py:471
  167.0 2.5 %collective-permute-done.13 = bf16[64,1152]{1,0:T(8,128)(2,1)S(1)} collective-permute-done((bf16[64,1152]{1,0:T(8,128)(2,1)S(1)}, bf16[64,1152]{1,0:T(8,128)(2,1)S(1)}, u32[]{:S(2)}, u32[]{:S(2)}) %collective-permute-start.13) | collective-permute-done | bytes 147488 | tf_op jit(solution)/shard_map/ppermute | solution.py:471
  169.5 8.1 %collective-permute-done.14 = bf16[64,1152]{1,0:T(8,128)(2,1)S(1)} collective-permute-done((bf16[64,1152]{1,0:T(8,128)(2,1)S(1)}, bf16[64,1152]{1,0:T(8,128)(2,1)S(1)}, u32[]{:S(2)}, u32[]{:S(2)}) %collective-permute-start.14) | collective-permute-done | bytes 147488 | tf_op jit(solution)/shard_map/ppermute | solution.py:471
  179.1 3.0 %combine.1 = bf16[128,1024]{1,0:T(8,128)(2,1)} custom-call(bf16[128,1280]{1,0:T(8,128)(2,1)S(1)} %choose.1.pick_ref, bf16[1280,1024]{1,0:T(8,128)(2,1)} %bitcast.15.rows_ref), custom_call_target="tpu_custom_call" | custom-call | flops 20132659200 | bytes 173015040 | tf_op jit(solution)/shard_map/combine/pallas_call | solution.py:383
  (37 shorter events, 17.6 us)
Async XLA Ops:
  1.7 16.2 %copy-start.4 = (s32[2]{0:T(128)S(1)}, s32[2]{0:T(128)}, u32[]{:S(2)}) copy-start(s32[2]{0:T(128)} %constant.55.clone) | copy-start | bytes 28
  1.8 16.2 %copy-start.2 = (s32[3]{0:T(128)S(1)}, s32[3]{0:T(128)}, u32[]{:S(2)}) copy-start(s32[3]{0:T(128)} %constant.54.clone) | copy-start | bytes 40
  1.8 16.2 %copy-start.3 = (s32[3]{0:T(128)S(1)}, s32[3]{0:T(128)}, u32[]{:S(2)}) copy-start(s32[3]{0:T(128)} %constant.56.clone) | copy-start | bytes 40
  1.8 24.0 %collective-permute-start = (bf16[128,2176]{1,0:T(8,128)(2,1)S(1)}, bf16[128,2176]{1,0:T(8,128)(2,1)S(1)}, u32[]{:S(2)}, u32[]{:S(2)}) collective-permute-start(bf16[128,2176]{1,0:T(8,128)(2,1)S(1)} %payload.1.refs_1_), channel_id=1, source_target_pairs={{0,4},{4,8},{8,12},{12,16},{16,20},{20,24},{24,28},{28,0},{1,5},{5... | collective-permute-start | bytes 1671176 | tf_op jit(solution)/shard_map/ppermute | solution.py:411
  6.8 20.9 %collective-permute-start.3 = (bf16[128,2176]{1,0:T(8,128)(2,1)S(1)}, bf16[128,2176]{1,0:T(8,128)(2,1)S(1)}, u32[]{:S(2)}, u32[]{:S(2)}) collective-permute-start(bf16[128,2176]{1,0:T(8,128)(2,1)S(1)} %payload.1.refs_1_), channel_id=1, source_target_pairs={{0,28},{4,0},{8,4},{12,8},{16,12},{20,16},{24,20},{28,24},{1,29},{... | collective-permute-start | bytes 1671176 | tf_op jit(solution)/shard_map/ppermute | solution.py:411
  25.8 16.0 %collective-permute-start.1 = (bf16[128,2176]{1,0:T(8,128)(2,1)S(1)}, bf16[128,2176]{1,0:T(8,128)(2,1)S(1)}, u32[]{:S(2)}, u32[]{:S(2)}) collective-permute-start(bf16[128,2176]{1,0:T(8,128)(2,1)S(1)} %collective-permute-done.refs_2_), channel_id=1, source_target_pairs={{0,4},{4,8},{8,12},{12,16},{16,20},{20,24},{24,28},{28,0},{1,5},{5... | collective-permute-start | bytes 1671176 | tf_op jit(solution)/shard_map/ppermute | solution.py:411
  27.7 16.0 %collective-permute-start.4 = (bf16[128,2176]{1,0:T(8,128)(2,1)S(1)}, bf16[128,2176]{1,0:T(8,128)(2,1)}, u32[]{:S(2)}, u32[]{:S(2)}) collective-permute-start(bf16[128,2176]{1,0:T(8,128)(2,1)S(1)} %collective-permute-done.3.refs_3_), channel_id=1, source_target_pairs={{0,28},{4,0},{8,4},{12,8},{16,12},{20,16},{24,20},{28,24},{1,29},{... | collective-permute-start | bytes 1671176 | tf_op jit(solution)/shard_map/ppermute | solution.py:411
  35.4 31.2 %all-to-all-start = ((bf16[4,112,2048]{2,1,0:T(8,128)(2,1)}), bf16[4,112,2048]{2,1,0:T(8,128)(2,1)S(1)}, u32[]{:S(2)}, u32[]{:S(2)}) async-start(bf16[4,112,2048]{2,1,0:T(8,128)(2,1)} %pack.5), calls=%async_computation | async-start | bytes 3670016 | tf_op jit(solution)/shard_map/all_to_all | solution.py:417
  41.7 15.1 %collective-permute-start.2 = (bf16[128,2176]{1,0:T(8,128)(2,1)S(1)}, bf16[128,2176]{1,0:T(8,128)(2,1)S(1)}, u32[]{:S(2)}, u32[]{:S(2)}) collective-permute-start(bf16[128,2176]{1,0:T(8,128)(2,1)S(1)} %collective-permute-done.1.refs_1_), channel_id=1, source_target_pairs={{0,4},{4,8},{8,12},{12,16},{16,20},{20,24},{24,28},{28,0},{1,5},{5... | collective-permute-start | bytes 1671176 | tf_op jit(solution)/shard_map/ppermute | solution.py:411
  43.7 14.4 %collective-permute-start.5 = (bf16[128,2176]{1,0:T(8,128)(2,1)}, bf16[128,2176]{1,0:T(8,128)(2,1)S(1)}, u32[]{:S(2)}, u32[]{:S(2)}) collective-permute-start(bf16[128,2176]{1,0:T(8,128)(2,1)} %collective-permute-done.4.refs_2_), channel_id=1, source_target_pairs={{0,28},{4,0},{8,4},{12,8},{16,12},{20,16},{24,20},{28,24},{1,29},{... | collective-permute-start | bytes 1671176 | tf_op jit(solution)/shard_map/ppermute | solution.py:411
  58.8 18.5 %collective-permute-start.6 = (bf16[64,2176]{1,0:T(8,128)(2,1)}, bf16[64,2176]{1,0:T(8,128)(2,1)S(1)}, u32[]{:S(2)}, u32[]{:S(2)}) collective-permute-start(bf16[64,2176]{1,0:T(8,128)(2,1)} %slice.12), channel_id=1, source_target_pairs={{0,4},{4,8},{8,12},{12,16},{16,20},{20,24},{24,28},{28,0},{1,5},{5... | collective-permute-start | bytes 835592 | tf_op jit(solution)/shard_map/ppermute | solution.py:411
  61.4 15.9 %collective-permute-start.7 = (bf16[64,2176]{1,0:T(8,128)(2,1)}, bf16[64,2176]{1,0:T(8,128)(2,1)S(1)}, u32[]{:S(2)}, u32[]{:S(2)}) collective-permute-start(bf16[64,2176]{1,0:T(8,128)(2,1)} %slice.13), channel_id=1, source_target_pairs={{0,28},{4,0},{8,4},{12,8},{16,12},{20,16},{24,20},{28,24},{1,29},{... | collective-permute-start | bytes 835592 | tf_op jit(solution)/shard_map/ppermute | solution.py:411
  66.6 10.6 %copy-start = (bf16[4,112,2048]{2,1,0:T(8,128)(2,1)}, bf16[4,112,2048]{2,1,0:T(8,128)(2,1)S(1)}, u32[]{:S(2)}) copy-start(bf16[4,112,2048]{2,1,0:T(8,128)(2,1)S(1)} %all-to-all-done) | copy-start | bytes 5505028
  66.7 16.9 %all-to-all-start.1 = ((bf16[4,72,2048]{2,1,0:T(8,128)(2,1)}), bf16[4,72,2048]{2,1,0:T(8,128)(2,1)}, u32[]{:S(2)}, u32[]{:S(2)}) async-start(bf16[4,72,2048]{2,1,0:T(8,128)(2,1)} %pack.3), calls=%async_computation.1 | async-start | bytes 2359296 | tf_op jit(solution)/shard_map/all_to_all | solution.py:417
  83.6 21.9 %all-to-all-start.2 = ((bf16[4,112,2048]{2,1,0:T(8,128)(2,1)}), bf16[4,112,2048]{2,1,0:T(8,128)(2,1)S(1)}, u32[]{:S(2)}, u32[]{:S(2)}) async-start(bf16[4,112,2048]{2,1,0:T(8,128)(2,1)} %pack.4), calls=%async_computation.2 | async-start | bytes 3670016 | tf_op jit(solution)/shard_map/all_to_all | solution.py:417
  111.8 67.3 %all-to-all-start.3 = ((bf16[32,40,1024]{2,1,0:T(8,128)(2,1)}), bf16[32,40,1024]{2,1,0:T(8,128)(2,1)}, u32[]{:S(2)}, u32[]{:S(2)}) async-start(bf16[32,40,1024]{2,1,0:T(8,128)(2,1)} %get-tuple-element.43), calls=%async_computation.3 | async-start | bytes 5242880 | tf_op jit(solution)/shard_map/all_to_all | solution.py:458
  125.2 41.2 %copy-start.1 = (s32[128,8]{0,1:T(8,128)S(1)}, s32[128,8]{0,1:T(8,128)}, u32[]{:S(2)}) copy-start(s32[128,8]{0,1:T(8,128)} %param.11) | copy-start | bytes 12292
  125.2 10.8 %collective-permute-start.8 = (bf16[8,64,1152]{2,1,0:T(8,128)(2,1)}, bf16[8,64,1152]{2,1,0:T(8,128)(2,1)S(1)}, u32[]{:S(2)}, u32[]{:S(2)}) collective-permute-start(bf16[8,64,1152]{2,1,0:T(8,128)(2,1)} %get-tuple-element.48), channel_id=1, source_target_pairs={{0,32},{32,0},{1,33},{33,1},{2,34},{34,2},{3,35},{35,3},{4,36},{36... | collective-permute-start | bytes 3538952 | tf_op jit(solution)/shard_map/ppermute | solution.py:467
  138.0 23.2 %collective-permute-start.10 = (bf16[64,1152]{1,0:T(8,128)(2,1)S(1)}, bf16[64,1152]{1,0:T(8,128)(2,1)S(1)}, u32[]{:S(2)}, u32[]{:S(2)}) collective-permute-start(bf16[64,1152]{1,0:T(8,128)(2,1)S(1)} %get-tuple-element.51), channel_id=1, source_target_pairs={{0,128},{64,192},{128,256},{192,320},{256,384},{320,448},{384,0},{... | collective-permute-start | bytes 442376 | tf_op jit(solution)/shard_map/ppermute | solution.py:471
  142.2 20.9 %collective-permute-start.11 = (bf16[64,1152]{1,0:T(8,128)(2,1)S(1)}, bf16[64,1152]{1,0:T(8,128)(2,1)S(1)}, u32[]{:S(2)}, u32[]{:S(2)}) collective-permute-start(bf16[64,1152]{1,0:T(8,128)(2,1)S(1)} %get-tuple-element.52), channel_id=1, source_target_pairs={{0,192},{64,256},{128,320},{192,384},{256,448},{320,0},{384,64},{4... | collective-permute-start | bytes 442376 | tf_op jit(solution)/shard_map/ppermute | solution.py:471
  147.7 19.2 %collective-permute-start.12 = (bf16[64,1152]{1,0:T(8,128)(2,1)S(1)}, bf16[64,1152]{1,0:T(8,128)(2,1)S(1)}, u32[]{:S(2)}, u32[]{:S(2)}) collective-permute-start(bf16[64,1152]{1,0:T(8,128)(2,1)S(1)} %get-tuple-element.53), channel_id=1, source_target_pairs={{0,256},{64,320},{128,384},{192,448},{256,0},{320,64},{384,128},{4... | collective-permute-start | bytes 442376 | tf_op jit(solution)/shard_map/ppermute | solution.py:471
  150.4 19.1 %collective-permute-start.13 = (bf16[64,1152]{1,0:T(8,128)(2,1)S(1)}, bf16[64,1152]{1,0:T(8,128)(2,1)S(1)}, u32[]{:S(2)}, u32[]{:S(2)}) collective-permute-start(bf16[64,1152]{1,0:T(8,128)(2,1)S(1)} %get-tuple-element.54), channel_id=1, source_target_pairs={{0,320},{64,384},{128,448},{192,0},{256,64},{320,128},{384,192},{4... | collective-permute-start | bytes 442376 | tf_op jit(solution)/shard_map/ppermute | solution.py:471
  156.2 21.4 %collective-permute-start.14 = (bf16[64,1152]{1,0:T(8,128)(2,1)S(1)}, bf16[64,1152]{1,0:T(8,128)(2,1)S(1)}, u32[]{:S(2)}, u32[]{:S(2)}) collective-permute-start(bf16[64,1152]{1,0:T(8,128)(2,1)S(1)} %get-tuple-element.55), channel_id=1, source_target_pairs={{0,384},{64,448},{128,0},{192,64},{256,128},{320,192},{384,256},{4... | collective-permute-start | bytes 442376 | tf_op jit(solution)/shard_map/ppermute | solution.py:471
  161.2 16.4 %collective-permute-start.15 = (bf16[64,1152]{1,0:T(8,128)(2,1)S(1)}, bf16[64,1152]{1,0:T(8,128)(2,1)S(1)}, u32[]{:S(2)}, u32[]{:S(2)}) collective-permute-start(bf16[64,1152]{1,0:T(8,128)(2,1)S(1)} %get-tuple-element.56), channel_id=1, source_target_pairs={{0,448},{64,0},{128,64},{192,128},{256,192},{320,256},{384,320},{4... | collective-permute-start | bytes 442376 | tf_op jit(solution)/shard_map/ppermute | solution.py:471
  163.1 14.5 %collective-permute-start.9 = (bf16[64,1152]{1,0:T(8,128)(2,1)S(1)}, bf16[64,1152]{1,0:T(8,128)(2,1)S(1)}, u32[]{:S(2)}, u32[]{:S(2)}) collective-permute-start(bf16[64,1152]{1,0:T(8,128)(2,1)S(1)} %get-tuple-element.50), channel_id=1, source_target_pairs={{0,64},{64,128},{128,192},{192,256},{256,320},{320,384},{384,448},... | collective-permute-start | bytes 442376 | tf_op jit(solution)/shard_map/ppermute | solution.py:471

commit v7 on v6

--- a/solution.py
+++ b/solution.py
@@ -27,9 +27,9 @@
     return pltpu.with_memory_space_constraint(value, pltpu.HBM)
 
 
-def cost(flops, bytes_accessed):
+def cost(flops, bytes_accessed, hint=HINT):
     return pl.CostEstimate(
-        flops=int(HINT * flops), bytes_accessed=int(HINT * bytes_accessed), transcendentals=0
+        flops=int(hint * flops), bytes_accessed=int(hint * bytes_accessed), transcendentals=0
     )
 
 
@@ -144,7 +144,7 @@
         copy.wait()
 
 
-def pack(base, pieces, top, capacity, width, tokens):
+def pack(base, pieces, top, capacity, width, tokens, hint):
     total = sum(piece.shape[0] for piece in pieces)
     count = total // tokens
     rows = -(-capacity * count // 8) * 8
@@ -161,7 +161,9 @@
             DMA((X_RING,)),
         ],
         compiler_params=params(12),
-        cost_estimate=cost(16 * rows * total * width, 16 * rows * width + 4 * total * width),
+        cost_estimate=cost(
+            16 * rows * total * width, 16 * rows * width + 4 * total * width, hint
+        ),
         name="pack",
     )(base, *pieces)
 
@@ -410,8 +412,8 @@
     def shift(value, by):
         return lax.ppermute(value, "z", [(i, (i + by) % z_size) for i in range(z_size)])
 
-    def packed(*pieces):
-        return pack(base, pieces, top, capacity, width, tokens)
+    def packed(*pieces, hint=HINT):
+        return pack(base, pieces, top, capacity, width, tokens, hint)
 
     def crossed(value):
         return lax.all_to_all(value, "x", split_axis=0, concat_axis=0, tiled=True)
@@ -439,14 +441,14 @@
     fore2, back2 = shift(fore1, 1), shift(back1, -1)
     rows0 = crossed(packed(own, fore1, back1))
     fore3, back3 = shift(fore2, 1), shift(back2, -1)
+    fore4, back4 = shift(fore2[:half], 2), shift(back2[half:], -2)
     packed1 = packed(fore2, back2)
-    onward_f, onward_b, _ = lax.optimization_barrier((fore3, back3, packed1))
     packed1, rows0 = lax.optimization_barrier((packed1, rows0))
     rows1 = crossed(packed1)
-    fore4, back4 = shift(onward_f[:half], 1), shift(onward_b[half:], -1)
     rows0 = flat(rows0)
     away, terms0 = run(places(0, -1, 1), rows0, None)
-    packed2 = packed(fore3, back3, fore4, back4)
+    fore3, back3, fore4, back4, _ = lax.optimization_barrier((fore3, back3, fore4, back4, away))
+    packed2 = packed(fore3, back3, fore4, back4, hint=1)
     packed2, rows1, away = lax.optimization_barrier((packed2, rows1, away))
     rows2 = crossed(packed2)
     rows1 = flat(rows1)

time: 185 us -> 185 us (level)
  the two profiles are of different devices: /device:TPU:1 before, /device:TPU:12 now
where the time goes in v7:
time: 185 us; the launch traced here: 183 us
  starting transfers between devices  90.7 us (49%)
  Pallas kernels  43.1 us (23%)
  waiting for transfers between devices  40.8 us (22%)
  local copies, waits for them, and re-layouts  7.37 us (4%)
    ppermute x8, starting transfers between devices, shift(): lax.ppermute(value, 'z', [(i, (i + by) % z_size) for i in range(z_size)])  35 us
    ppermute x7, starting transfers between devices, per_device(): lax.ppermute(shares[by], 'y', [(i, (i + by) % y_size) for i in range(y_si...  28.8 us
    pallas_call x3, Pallas kernels, expert_rows(): pl.pallas_call(functools.partial(expert_kernel, capacity, slot_rows), out...  17.9 us
    all_to_all x3, starting transfers between devices, crossed(): return lax.all_to_all(value, 'x', split_axis=0, concat_axis=0, tiled=True)  16 us
    ppermute x7, waiting for transfers between devices, per_device(): lax.ppermute(shares[by], 'y', [(i, (i + by) % y_size) for i in range(y_si...  13.1 us
    all_to_all x3, waiting for transfers between devices, crossed(): return lax.all_to_all(value, 'x', split_axis=0, concat_axis=0, tiled=True)  12.8 us
    ppermute x8, waiting for transfers between devices, shift(): lax.ppermute(value, 'z', [(i, (i + by) % z_size) for i in range(z_size)])  10.7 us
    pallas_call x3, Pallas kernels, pack(): pl.pallas_call(functools.partial(pack_kernel, top, capacity, width, token...  10.3 us
  transfers between devices with their start and end apart: 20, of which 9 were waited for; matrix products, arithmetic and copies ran while one was open for 4% of the time, Pallas kernels for 18%

profile of v7, /device:TPU:12, one launch (start us, length us, event | category | flops | bytes accessed | tf_op | source)
XLA Modules:
  0.0 183.4 jit_solution(2978386366893115083)
XLA Ops:
  1.8 4.4 %collective-permute-start = (bf16[128,2176]{1,0:T(8,128)(2,1)S(1)}, bf16[128,2176]{1,0:T(8,128)(2,1)S(1)}, u32[]{:S(2)}, u32[]{:S(2)}) collective-permute-start(bf16[128,2176]{1,0:T(8,128)(2,1)S(1)} %payload.1.refs_1_), channel_id=1, source_target_pairs={{0,4},{4,8},{8,12},{12,16},{16,20},{20,24},{24,28},{28,0},{1,5},{5... | collective-permute-start | bytes 1671176 | tf_op jit(solution)/shard_map/ppermute | solution.py:413
  6.2 8.6 %collective-permute-start.3 = (bf16[128,2176]{1,0:T(8,128)(2,1)S(1)}, bf16[128,2176]{1,0:T(8,128)(2,1)S(1)}, u32[]{:S(2)}, u32[]{:S(2)}) collective-permute-start(bf16[128,2176]{1,0:T(8,128)(2,1)S(1)} %payload.1.refs_1_), channel_id=1, source_target_pairs={{0,28},{4,0},{8,4},{12,8},{16,12},{20,16},{24,20},{28,24},{1,29},{... | collective-permute-start | bytes 1671176 | tf_op jit(solution)/shard_map/ppermute | solution.py:413
  14.8 2.6 %copy.14 = bf16[1,1024,768]{1,2,0:T(8,128)(2,1)} copy(bf16[1,1024,768]{2,1,0:T(8,128)(2,1)} %param.13) | data formatting | bytes 3145728 | tf_op args[4]
  17.5 8.0 %collective-permute-done.refs_2_ = bf16[128,2176]{1,0:T(8,128)(2,1)S(1)} collective-permute-done((bf16[128,2176]{1,0:T(8,128)(2,1)S(1)}, bf16[128,2176]{1,0:T(8,128)(2,1)S(1)}, u32[]{:S(2)}, u32[]{:S(2)}) %collective-permute-start) | collective-permute-done | bytes 557088 | tf_op jit(solution)/shard_map/ppermute | solution.py:413
  27.4 5.1 %collective-permute-start.4 = (bf16[128,2176]{1,0:T(8,128)(2,1)S(1)}, bf16[128,2176]{1,0:T(8,128)(2,1)}, u32[]{:S(2)}, u32[]{:S(2)}) collective-permute-start(bf16[128,2176]{1,0:T(8,128)(2,1)S(1)} %collective-permute-done.3.refs_3_), channel_id=1, source_target_pairs={{0,28},{4,0},{8,4},{12,8},{16,12},{20,16},{24,20},{28,24},{1,29},{... | collective-permute-start | bytes 1671176 | tf_op jit(solution)/shard_map/ppermute | solution.py:413
  32.6 3.2 %pack.4 = bf16[4,112,2048]{2,1,0:T(8,128)(2,1)} custom-call(s32[1]{0:T(128)} %bitcast.refs_0_, bf16[128,2176]{1,0:T(8,128)(2,1)S(1)} %payload.1.refs_1_, bf16[128,2176]{1,0:T(8,128)(2,1)S(1)} %collective-permute-done.refs_2_, bf16[128,2176]{1,0:T(8,128)(2,1)S(1)} %collective-permute-done.3.refs_3_), custom_call_target="tpu_custom_call" | custom-call | flops 42278584320 | bytes 204472320 | tf_op jit(solution)/shard_map/pack/pallas_call | solution.py:151
  35.7 4.8 %all-to-all-start = ((bf16[4,112,2048]{2,1,0:T(8,128)(2,1)}), bf16[4,112,2048]{2,1,0:T(8,128)(2,1)S(1)}, u32[]{:S(2)}, u32[]{:S(2)}) async-start(bf16[4,112,2048]{2,1,0:T(8,128)(2,1)} %pack.4), calls=%async_computation | async-start | bytes 3670016 | tf_op jit(solution)/shard_map/all_to_all | solution.py:419
  40.6 1.9 %collective-permute-done.1.refs_1_ = bf16[128,2176]{1,0:T(8,128)(2,1)} collective-permute-done((bf16[128,2176]{1,0:T(8,128)(2,1)S(1)}, bf16[128,2176]{1,0:T(8,128)(2,1)}, u32[]{:S(2)}, u32[]{:S(2)}) %collective-permute-start.1) | collective-permute-done | bytes 557088 | tf_op jit(solution)/shard_map/ppermute | solution.py:413
  47.8 6.0 %collective-permute-start.7 = (bf16[64,2176]{1,0:T(8,128)(2,1)}, bf16[64,2176]{1,0:T(8,128)(2,1)}, u32[]{:S(2)}, u32[]{:S(2)}) collective-permute-start(bf16[64,2176]{1,0:T(8,128)(2,1)} %slice.17), channel_id=1, source_target_pairs={{0,24},{4,28},{8,0},{12,4},{16,8},{20,12},{24,16},{28,20},{1,25},{... | collective-permute-start | bytes 835592 | tf_op jit(solution)/shard_map/ppermute | solution.py:413
  53.8 1.9 %collective-permute-start.2 = (bf16[128,2176]{1,0:T(8,128)(2,1)}, bf16[128,2176]{1,0:T(8,128)(2,1)}, u32[]{:S(2)}, u32[]{:S(2)}) collective-permute-start(bf16[128,2176]{1,0:T(8,128)(2,1)} %collective-permute-done.1.refs_1_), channel_id=1, source_target_pairs={{0,4},{4,8},{8,12},{12,16},{16,20},{20,24},{24,28},{28,0},{1,5},{5... | collective-permute-start | bytes 1671176 | tf_op jit(solution)/shard_map/ppermute | solution.py:413
  55.8 5.1 %collective-permute-start.5 = (bf16[128,2176]{1,0:T(8,128)(2,1)}, bf16[128,2176]{1,0:T(8,128)(2,1)}, u32[]{:S(2)}, u32[]{:S(2)}) collective-permute-start(bf16[128,2176]{1,0:T(8,128)(2,1)} %collective-permute-done.4.refs_2_), channel_id=1, source_target_pairs={{0,28},{4,0},{8,4},{12,8},{16,12},{20,16},{24,20},{28,24},{1,29},{... | collective-permute-start | bytes 1671176 | tf_op jit(solution)/shard_map/ppermute | solution.py:413
  60.9 3.2 %pack.3 = bf16[4,72,2048]{2,1,0:T(8,128)(2,1)} custom-call(s32[1]{0:T(128)} %bitcast.refs_0_, bf16[128,2176]{1,0:T(8,128)(2,1)} %collective-permute-done.1.refs_1_, bf16[128,2176]{1,0:T(8,128)(2,1)} %collective-permute-done.4.refs_2_), custom_call_target="tpu_custom_call" | custom-call | flops 18119393280 | bytes 133693440 | tf_op jit(solution)/shard_map/pack/pallas_call | solution.py:151
  64.1 4.8 %all-to-all-start.1 = ((bf16[4,72,2048]{2,1,0:T(8,128)(2,1)}), bf16[4,72,2048]{2,1,0:T(8,128)(2,1)S(1)}, u32[]{:S(2)}, u32[]{:S(2)}) async-start(bf16[4,72,2048]{2,1,0:T(8,128)(2,1)} %pack.3), calls=%async_computation.1 | async-start | bytes 2359296 | tf_op jit(solution)/shard_map/all_to_all | solution.py:419
  68.9 6.3 %expert.3 = (bf16[32,40,1024]{2,1,0:T(8,128)(2,1)}, bf16[448,1152]{1,0:T(8,128)(2,1)}) custom-call(s32[3]{0:T(128)S(1)} %get-tuple-element.66.refs_0_, bf16[448,2048]{1,0:T(8,128)(2,1)S(1)} %bitcast.18, bf16[1024,768]{1,0:T(8,128)(2,1)} %bitcast.29, bf16[1024,384]{1,0:T(8,128)(2,1)} %bitcast.36, bf16[768,1024]{1,0:T(8,128)(2,1)} %bitcast.32), custom_call_target="tpu_custom_call" | custom-call | flops 105696460800 | bytes 361758720 | tf_op jit(solution)/shard_map/expert/pallas_call | solution.py:227
  76.0 4.0 %pack.5 = bf16[4,112,2048]{2,1,0:T(8,128)(2,1)} custom-call(s32[1]{0:T(128)} %bitcast.refs_0_, bf16[128,2176]{1,0:T(8,128)(2,1)} %collective-permute-done.2.refs_1_, bf16[128,2176]{1,0:T(8,128)(2,1)} %collective-permute-done.5.refs_2_, bf16[64,2176]{1,0:T(8,128)(2,1)S(1)} %collective-permute-done.6.refs_3_, bf16[64,2176]{1,0:T(8,128)(2,1)} %collective-permute-done.7.refs_4_), custom_call_target="tpu_custom_call" | custom-call | flops 704643072 | bytes 3407872 | tf_op jit(solution)/shard_map/pack/pallas_call | solution.py:151
  80.0 6.4 %all-to-all-start.2 = ((bf16[4,112,2048]{2,1,0:T(8,128)(2,1)}), bf16[4,112,2048]{2,1,0:T(8,128)(2,1)S(1)}, u32[]{:S(2)}, u32[]{:S(2)}) async-start(bf16[4,112,2048]{2,1,0:T(8,128)(2,1)} %pack.5), calls=%async_computation.2 | async-start | bytes 3670016 | tf_op jit(solution)/shard_map/all_to_all | solution.py:419
  86.4 5.3 %expert.4 = (bf16[32,40,1024]{2,1,0:T(8,128)(2,1)}, bf16[288,1152]{1,0:T(8,128)(2,1)}) custom-call(s32[2]{0:T(128)S(1)} %fusion.5.refs_0_, bf16[288,2048]{1,0:T(8,128)(2,1)S(1)} %bitcast.24, bf16[1024,768]{1,0:T(8,128)(2,1)} %bitcast.30, bf16[1024,384]{1,0:T(8,128)(2,1)} %bitcast.37, bf16[768,1024]{1,0:T(8,128)(2,1)} %bitcast.33, ...), custom_call_target="tpu_custom_call", output_to_operand_aliasing={{0}: (5, {})} | custom-call | flops 67947724800 | bytes 283115520 | tf_op jit(solution)/shard_map/expert/pallas_call | solution.py:227
  91.7 12.8 %all-to-all-done.2 = bf16[4,112,2048]{2,1,0:T(8,128)(2,1)S(1)} async-done(((bf16[4,112,2048]{2,1,0:T(8,128)(2,1)}), bf16[4,112,2048]{2,1,0:T(8,128)(2,1)S(1)}, u32[]{:S(2)}, u32[]{:S(2)}) %all-to-all-start.2) | async-done | bytes 1835040 | tf_op jit(solution)/shard_map/all_to_all | solution.py:419
  104.5 6.3 %expert.5 = (bf16[32,40,1024]{2,1,0:T(8,128)(2,1)}, bf16[448,1152]{1,0:T(8,128)(2,1)}) custom-call(s32[3]{0:T(128)S(1)} %get-tuple-element.65.refs_0_, bf16[448,2048]{1,0:T(8,128)(2,1)S(1)} %bitcast.21, bf16[1024,768]{1,0:T(8,128)(2,1)} %bitcast.31, bf16[1024,384]{1,0:T(8,128)(2,1)} %bitcast.38, ...), custom_call_target="tpu_custom_call", output_to_operand_aliasing={{0}: (5, {})} | custom-call | flops 105696460800 | bytes 361758720 | tf_op jit(solution)/shard_map/expert/pallas_call | solution.py:227
  110.8 8.8 %all-to-all-start.3 = ((bf16[32,40,1024]{2,1,0:T(8,128)(2,1)}), bf16[32,40,1024]{2,1,0:T(8,128)(2,1)}, u32[]{:S(2)}, u32[]{:S(2)}) async-start(bf16[32,40,1024]{2,1,0:T(8,128)(2,1)} %get-tuple-element.47), calls=%async_computation.3 | async-start | bytes 5242880 | tf_op jit(solution)/shard_map/all_to_all | solution.py:460
  119.6 8.5 %weight_terms.1 = (f32[8,64,1152]{2,1,0:T(8,128)}, bf16[8,64,1152]{2,1,0:T(8,128)(2,1)}) custom-call(s32[1]{0:T(128)} %bitcast.12.refs_0_, bf16[448,2048]{1,0:T(8,128)(2,1)} %bitcast.19, bf16[448,2048]{1,0:T(8,128)(2,1)} %bitcast.20, bf16[448,1152]{1,0:T(8,128)(2,1)} %get-tuple-element.48.refs_3_, bf16[288,2048]{1,0:T(8,128)(2,1)} %bitcast.25, ...), custom_call_target="tpu_custom_call" | custom-call | flops 167604387840 | bytes 666992640 | tf_op jit(solution)/shard_map/weight_terms/pallas_call | solution.py:297
  128.1 2.0 %collective-permute-start.8 = (bf16[8,64,1152]{2,1,0:T(8,128)(2,1)}, bf16[8,64,1152]{2,1,0:T(8,128)(2,1)S(1)}, u32[]{:S(2)}, u32[]{:S(2)}) collective-permute-start(bf16[8,64,1152]{2,1,0:T(8,128)(2,1)} %get-tuple-element.52), channel_id=1, source_target_pairs={{0,32},{32,0},{1,33},{33,1},{2,34},{34,2},{3,35},{35,3},{4,36},{36... | collective-permute-start | bytes 3538952 | tf_op jit(solution)/shard_map/ppermute | solution.py:469
  130.1 3.0 %collective-permute-done.8.other_ref = bf16[8,64,1152]{2,1,0:T(8,128)(2,1)S(1)} collective-permute-done((bf16[8,64,1152]{2,1,0:T(8,128)(2,1)}, bf16[8,64,1152]{2,1,0:T(8,128)(2,1)S(1)}, u32[]{:S(2)}, u32[]{:S(2)}) %collective-permute-start.8) | collective-permute-done | bytes 1179680 | tf_op jit(solution)/shard_map/ppermute | solution.py:469
  135.1 4.5 %collective-permute-start.10 = (bf16[64,1152]{1,0:T(8,128)(2,1)S(1)}, bf16[64,1152]{1,0:T(8,128)(2,1)S(1)}, u32[]{:S(2)}, u32[]{:S(2)}) collective-permute-start(bf16[64,1152]{1,0:T(8,128)(2,1)S(1)} %get-tuple-element.55), channel_id=1, source_target_pairs={{0,128},{64,192},{128,256},{192,320},{256,384},{320,448},{384,0},{... | collective-permute-start | bytes 442376 | tf_op jit(solution)/shard_map/ppermute | solution.py:473
  139.5 4.9 %collective-permute-start.11 = (bf16[64,1152]{1,0:T(8,128)(2,1)S(1)}, bf16[64,1152]{1,0:T(8,128)(2,1)S(1)}, u32[]{:S(2)}, u32[]{:S(2)}) collective-permute-start(bf16[64,1152]{1,0:T(8,128)(2,1)S(1)} %get-tuple-element.56), channel_id=1, source_target_pairs={{0,192},{64,256},{128,320},{192,384},{256,448},{320,0},{384,64},{4... | collective-permute-start | bytes 442376 | tf_op jit(solution)/shard_map/ppermute | solution.py:473
  144.5 3.8 %collective-permute-start.12 = (bf16[64,1152]{1,0:T(8,128)(2,1)S(1)}, bf16[64,1152]{1,0:T(8,128)(2,1)S(1)}, u32[]{:S(2)}, u32[]{:S(2)}) collective-permute-start(bf16[64,1152]{1,0:T(8,128)(2,1)S(1)} %get-tuple-element.57), channel_id=1, source_target_pairs={{0,256},{64,320},{128,384},{192,448},{256,0},{320,64},{384,128},{4... | collective-permute-start | bytes 442376 | tf_op jit(solution)/shard_map/ppermute | solution.py:473
  148.3 5.2 %collective-permute-start.13 = (bf16[64,1152]{1,0:T(8,128)(2,1)S(1)}, bf16[64,1152]{1,0:T(8,128)(2,1)S(1)}, u32[]{:S(2)}, u32[]{:S(2)}) collective-permute-start(bf16[64,1152]{1,0:T(8,128)(2,1)S(1)} %get-tuple-element.58), channel_id=1, source_target_pairs={{0,320},{64,384},{128,448},{192,0},{256,64},{320,128},{384,192},{4... | collective-permute-start | bytes 442376 | tf_op jit(solution)/shard_map/ppermute | solution.py:473
  153.5 4.0 %collective-permute-start.14 = (bf16[64,1152]{1,0:T(8,128)(2,1)S(1)}, bf16[64,1152]{1,0:T(8,128)(2,1)S(1)}, u32[]{:S(2)}, u32[]{:S(2)}) collective-permute-start(bf16[64,1152]{1,0:T(8,128)(2,1)S(1)} %get-tuple-element.59), channel_id=1, source_target_pairs={{0,384},{64,448},{128,0},{192,64},{256,128},{320,192},{384,256},{4... | collective-permute-start | bytes 442376 | tf_op jit(solution)/shard_map/ppermute | solution.py:473
  157.5 4.5 %collective-permute-start.15 = (bf16[64,1152]{1,0:T(8,128)(2,1)S(1)}, bf16[64,1152]{1,0:T(8,128)(2,1)S(1)}, u32[]{:S(2)}, u32[]{:S(2)}) collective-permute-start(bf16[64,1152]{1,0:T(8,128)(2,1)S(1)} %get-tuple-element.60), channel_id=1, source_target_pairs={{0,448},{64,0},{128,64},{192,128},{256,192},{320,256},{384,320},{4... | collective-permute-start | bytes 442376 | tf_op jit(solution)/shard_map/ppermute | solution.py:473
  164.4 2.9 %collective-permute-done.13 = bf16[64,1152]{1,0:T(8,128)(2,1)S(1)} collective-permute-done((bf16[64,1152]{1,0:T(8,128)(2,1)S(1)}, bf16[64,1152]{1,0:T(8,128)(2,1)S(1)}, u32[]{:S(2)}, u32[]{:S(2)}) %collective-permute-start.13) | collective-permute-done | bytes 147488 | tf_op jit(solution)/shard_map/ppermute | solution.py:473
  167.4 8.3 %collective-permute-done.14 = bf16[64,1152]{1,0:T(8,128)(2,1)S(1)} collective-permute-done((bf16[64,1152]{1,0:T(8,128)(2,1)S(1)}, bf16[64,1152]{1,0:T(8,128)(2,1)S(1)}, u32[]{:S(2)}, u32[]{:S(2)}) %collective-permute-start.14) | collective-permute-done | bytes 147488 | tf_op jit(solution)/shard_map/ppermute | solution.py:473
  180.3 3.0 %combine.1 = bf16[128,1024]{1,0:T(8,128)(2,1)} custom-call(bf16[128,1280]{1,0:T(8,128)(2,1)S(1)} %choose.1.pick_ref, bf16[1280,1024]{1,0:T(8,128)(2,1)} %bitcast.15.rows_ref), custom_call_target="tpu_custom_call" | custom-call | flops 20132659200 | bytes 173015040 | tf_op jit(solution)/shard_map/combine/pallas_call | solution.py:385
  (39 shorter events, 18.0 us)
Async XLA Ops:
  1.7 15.7 %copy-start.5 = (s32[2]{0:T(128)S(1)}, s32[2]{0:T(128)}, u32[]{:S(2)}) copy-start(s32[2]{0:T(128)} %constant.55.clone) | copy-start | bytes 28
  1.8 15.7 %copy-start.3 = (s32[3]{0:T(128)S(1)}, s32[3]{0:T(128)}, u32[]{:S(2)}) copy-start(s32[3]{0:T(128)} %constant.54.clone) | copy-start | bytes 40
  1.8 15.7 %copy-start.4 = (s32[3]{0:T(128)S(1)}, s32[3]{0:T(128)}, u32[]{:S(2)}) copy-start(s32[3]{0:T(128)} %constant.56.clone) | copy-start | bytes 40
  1.8 23.7 %collective-permute-start = (bf16[128,2176]{1,0:T(8,128)(2,1)S(1)}, bf16[128,2176]{1,0:T(8,128)(2,1)S(1)}, u32[]{:S(2)}, u32[]{:S(2)}) collective-permute-start(bf16[128,2176]{1,0:T(8,128)(2,1)S(1)} %payload.1.refs_1_), channel_id=1, source_target_pairs={{0,4},{4,8},{8,12},{12,16},{16,20},{20,24},{24,28},{28,0},{1,5},{5... | collective-permute-start | bytes 1671176 | tf_op jit(solution)/shard_map/ppermute | solution.py:413
  6.2 21.2 %collective-permute-start.3 = (bf16[128,2176]{1,0:T(8,128)(2,1)S(1)}, bf16[128,2176]{1,0:T(8,128)(2,1)S(1)}, u32[]{:S(2)}, u32[]{:S(2)}) collective-permute-start(bf16[128,2176]{1,0:T(8,128)(2,1)S(1)} %payload.1.refs_1_), channel_id=1, source_target_pairs={{0,28},{4,0},{8,4},{12,8},{16,12},{20,16},{24,20},{28,24},{1,29},{... | collective-permute-start | bytes 1671176 | tf_op jit(solution)/shard_map/ppermute | solution.py:413
  25.5 17.0 %collective-permute-start.1 = (bf16[128,2176]{1,0:T(8,128)(2,1)S(1)}, bf16[128,2176]{1,0:T(8,128)(2,1)}, u32[]{:S(2)}, u32[]{:S(2)}) collective-permute-start(bf16[128,2176]{1,0:T(8,128)(2,1)S(1)} %collective-permute-done.refs_2_), channel_id=1, source_target_pairs={{0,4},{4,8},{8,12},{12,16},{16,20},{20,24},{24,28},{28,0},{1,5},{5... | collective-permute-start | bytes 1671176 | tf_op jit(solution)/shard_map/ppermute | solution.py:413
  27.4 18.7 %collective-permute-start.4 = (bf16[128,2176]{1,0:T(8,128)(2,1)S(1)}, bf16[128,2176]{1,0:T(8,128)(2,1)}, u32[]{:S(2)}, u32[]{:S(2)}) collective-permute-start(bf16[128,2176]{1,0:T(8,128)(2,1)S(1)} %collective-permute-done.3.refs_3_), channel_id=1, source_target_pairs={{0,28},{4,0},{8,4},{12,8},{16,12},{20,16},{24,20},{28,24},{1,29},{... | collective-permute-start | bytes 1671176 | tf_op jit(solution)/shard_map/ppermute | solution.py:413
  35.7 28.3 %all-to-all-start = ((bf16[4,112,2048]{2,1,0:T(8,128)(2,1)}), bf16[4,112,2048]{2,1,0:T(8,128)(2,1)S(1)}, u32[]{:S(2)}, u32[]{:S(2)}) async-start(bf16[4,112,2048]{2,1,0:T(8,128)(2,1)} %pack.4), calls=%async_computation | async-start | bytes 3670016 | tf_op jit(solution)/shard_map/all_to_all | solution.py:419
  44.2 31.1 %collective-permute-start.6 = (bf16[64,2176]{1,0:T(8,128)(2,1)}, bf16[64,2176]{1,0:T(8,128)(2,1)S(1)}, u32[]{:S(2)}, u32[]{:S(2)}) collective-permute-start(bf16[64,2176]{1,0:T(8,128)(2,1)} %slice.16), channel_id=1, source_target_pairs={{0,8},{4,12},{8,16},{12,20},{16,24},{20,28},{24,0},{28,4},{1,9},{5... | collective-permute-start | bytes 835592 | tf_op jit(solution)/shard_map/ppermute | solution.py:413
  47.8 27.4 %collective-permute-start.7 = (bf16[64,2176]{1,0:T(8,128)(2,1)}, bf16[64,2176]{1,0:T(8,128)(2,1)}, u32[]{:S(2)}, u32[]{:S(2)}) collective-permute-start(bf16[64,2176]{1,0:T(8,128)(2,1)} %slice.17), channel_id=1, source_target_pairs={{0,24},{4,28},{8,0},{12,4},{16,8},{20,12},{24,16},{28,20},{1,25},{... | collective-permute-start | bytes 835592 | tf_op jit(solution)/shard_map/ppermute | solution.py:413
  53.8 21.4 %collective-permute-start.2 = (bf16[128,2176]{1,0:T(8,128)(2,1)}, bf16[128,2176]{1,0:T(8,128)(2,1)}, u32[]{:S(2)}, u32[]{:S(2)}) collective-permute-start(bf16[128,2176]{1,0:T(8,128)(2,1)} %collective-permute-done.1.refs_1_), channel_id=1, source_target_pairs={{0,4},{4,8},{8,12},{12,16},{16,20},{20,24},{24,28},{28,0},{1,5},{5... | collective-permute-start | bytes 1671176 | tf_op jit(solution)/shard_map/ppermute | solution.py:413
  55.8 20.2 %collective-permute-start.5 = (bf16[128,2176]{1,0:T(8,128)(2,1)}, bf16[128,2176]{1,0:T(8,128)(2,1)}, u32[]{:S(2)}, u32[]{:S(2)}) collective-permute-start(bf16[128,2176]{1,0:T(8,128)(2,1)} %collective-permute-done.4.refs_2_), channel_id=1, source_target_pairs={{0,28},{4,0},{8,4},{12,8},{16,12},{20,16},{24,20},{28,24},{1,29},{... | collective-permute-start | bytes 1671176 | tf_op jit(solution)/shard_map/ppermute | solution.py:413
  64.1 11.1 %copy-start = (bf16[4,112,2048]{2,1,0:T(8,128)(2,1)}, bf16[4,112,2048]{2,1,0:T(8,128)(2,1)S(1)}, u32[]{:S(2)}) copy-start(bf16[4,112,2048]{2,1,0:T(8,128)(2,1)S(1)} %all-to-all-done) | copy-start | bytes 5505028
  64.1 15.9 %all-to-all-start.1 = ((bf16[4,72,2048]{2,1,0:T(8,128)(2,1)}), bf16[4,72,2048]{2,1,0:T(8,128)(2,1)S(1)}, u32[]{:S(2)}, u32[]{:S(2)}) async-start(bf16[4,72,2048]{2,1,0:T(8,128)(2,1)} %pack.3), calls=%async_computation.1 | async-start | bytes 2359296 | tf_op jit(solution)/shard_map/all_to_all | solution.py:419
  80.0 6.4 %copy-start.1 = (bf16[4,72,2048]{2,1,0:T(8,128)(2,1)}, bf16[4,72,2048]{2,1,0:T(8,128)(2,1)S(1)}, u32[]{:S(2)}) copy-start(bf16[4,72,2048]{2,1,0:T(8,128)(2,1)S(1)} %all-to-all-done.1) | copy-start | bytes 3538948
  80.0 24.5 %all-to-all-start.2 = ((bf16[4,112,2048]{2,1,0:T(8,128)(2,1)}), bf16[4,112,2048]{2,1,0:T(8,128)(2,1)S(1)}, u32[]{:S(2)}, u32[]{:S(2)}) async-start(bf16[4,112,2048]{2,1,0:T(8,128)(2,1)} %pack.5), calls=%async_computation.2 | async-start | bytes 3670016 | tf_op jit(solution)/shard_map/all_to_all | solution.py:419
  110.8 69.5 %all-to-all-start.3 = ((bf16[32,40,1024]{2,1,0:T(8,128)(2,1)}), bf16[32,40,1024]{2,1,0:T(8,128)(2,1)}, u32[]{:S(2)}, u32[]{:S(2)}) async-start(bf16[32,40,1024]{2,1,0:T(8,128)(2,1)} %get-tuple-element.47), calls=%async_computation.3 | async-start | bytes 5242880 | tf_op jit(solution)/shard_map/all_to_all | solution.py:460
  128.1 35.9 %copy-start.2 = (s32[128,8]{0,1:T(8,128)S(1)}, s32[128,8]{0,1:T(8,128)}, u32[]{:S(2)}) copy-start(s32[128,8]{0,1:T(8,128)} %param.11) | copy-start | bytes 12292
  128.1 5.1 %collective-permute-start.8 = (bf16[8,64,1152]{2,1,0:T(8,128)(2,1)}, bf16[8,64,1152]{2,1,0:T(8,128)(2,1)S(1)}, u32[]{:S(2)}, u32[]{:S(2)}) collective-permute-start(bf16[8,64,1152]{2,1,0:T(8,128)(2,1)} %get-tuple-element.52), channel_id=1, source_target_pairs={{0,32},{32,0},{1,33},{33,1},{2,34},{34,2},{3,35},{35,3},{4,36},{36... | collective-permute-start | bytes 3538952 | tf_op jit(solution)/shard_map/ppermute | solution.py:469
  135.1 22.5 %collective-permute-start.10 = (bf16[64,1152]{1,0:T(8,128)(2,1)S(1)}, bf16[64,1152]{1,0:T(8,128)(2,1)S(1)}, u32[]{:S(2)}, u32[]{:S(2)}) collective-permute-start(bf16[64,1152]{1,0:T(8,128)(2,1)S(1)} %get-tuple-element.55), channel_id=1, source_target_pairs={{0,128},{64,192},{128,256},{192,320},{256,384},{320,448},{384,0},{... | collective-permute-start | bytes 442376 | tf_op jit(solution)/shard_map/ppermute | solution.py:473
  139.5 22.4 %collective-permute-start.11 = (bf16[64,1152]{1,0:T(8,128)(2,1)S(1)}, bf16[64,1152]{1,0:T(8,128)(2,1)S(1)}, u32[]{:S(2)}, u32[]{:S(2)}) collective-permute-start(bf16[64,1152]{1,0:T(8,128)(2,1)S(1)} %get-tuple-element.56), channel_id=1, source_target_pairs={{0,192},{64,256},{128,320},{192,384},{256,448},{320,0},{384,64},{4... | collective-permute-start | bytes 442376 | tf_op jit(solution)/shard_map/ppermute | solution.py:473
  144.5 20.0 %collective-permute-start.12 = (bf16[64,1152]{1,0:T(8,128)(2,1)S(1)}, bf16[64,1152]{1,0:T(8,128)(2,1)S(1)}, u32[]{:S(2)}, u32[]{:S(2)}) collective-permute-start(bf16[64,1152]{1,0:T(8,128)(2,1)S(1)} %get-tuple-element.57), channel_id=1, source_target_pairs={{0,256},{64,320},{128,384},{192,448},{256,0},{320,64},{384,128},{4... | collective-permute-start | bytes 442376 | tf_op jit(solution)/shard_map/ppermute | solution.py:473
  148.3 19.1 %collective-permute-start.13 = (bf16[64,1152]{1,0:T(8,128)(2,1)S(1)}, bf16[64,1152]{1,0:T(8,128)(2,1)S(1)}, u32[]{:S(2)}, u32[]{:S(2)}) collective-permute-start(bf16[64,1152]{1,0:T(8,128)(2,1)S(1)} %get-tuple-element.58), channel_id=1, source_target_pairs={{0,320},{64,384},{128,448},{192,0},{256,64},{320,128},{384,192},{4... | collective-permute-start | bytes 442376 | tf_op jit(solution)/shard_map/ppermute | solution.py:473
  153.5 22.2 %collective-permute-start.14 = (bf16[64,1152]{1,0:T(8,128)(2,1)S(1)}, bf16[64,1152]{1,0:T(8,128)(2,1)S(1)}, u32[]{:S(2)}, u32[]{:S(2)}) collective-permute-start(bf16[64,1152]{1,0:T(8,128)(2,1)S(1)} %get-tuple-element.59), channel_id=1, source_target_pairs={{0,384},{64,448},{128,0},{192,64},{256,128},{320,192},{384,256},{4... | collective-permute-start | bytes 442376 | tf_op jit(solution)/shard_map/ppermute | solution.py:473
  157.5 20.0 %collective-permute-start.15 = (bf16[64,1152]{1,0:T(8,128)(2,1)S(1)}, bf16[64,1152]{1,0:T(8,128)(2,1)S(1)}, u32[]{:S(2)}, u32[]{:S(2)}) collective-permute-start(bf16[64,1152]{1,0:T(8,128)(2,1)S(1)} %get-tuple-element.60), channel_id=1, source_target_pairs={{0,448},{64,0},{128,64},{192,128},{256,192},{320,256},{384,320},{4... | collective-permute-start | bytes 442376 | tf_op jit(solution)/shard_map/ppermute | solution.py:473
  162.0 15.5 %collective-permute-start.9 = (bf16[64,1152]{1,0:T(8,128)(2,1)S(1)}, bf16[64,1152]{1,0:T(8,128)(2,1)S(1)}, u32[]{:S(2)}, u32[]{:S(2)}) collective-permute-start(bf16[64,1152]{1,0:T(8,128)(2,1)S(1)} %get-tuple-element.54), channel_id=1, source_target_pairs={{0,64},{64,128},{128,192},{192,256},{256,320},{320,384},{384,448},... | collective-permute-start | bytes 442376 | tf_op jit(solution)/shard_map/ppermute | solution.py:473

commit v8 on v7

--- a/solution.py
+++ b/solution.py
@@ -198,18 +198,24 @@
     terms_copy = started(terms, terms_ref, in_sems.at[3])
     back[count:] = jnp.zeros((back.shape[0] - count, width), F32)
     copies[3].wait()
-    back[:count] = jnp.dot(
-        terms[:, : 2 * hidden_units], turned_in[...], preferred_element_type=F32
-    )
     out_copies = []
-    for column in range(X_RING):
-        for b in range(blocks):
-            first = column * per_x + b * capacity
-            slot = column * blocks + b
-            made[slot] = back[first : first + slot_rows].astype(BF16)
-            out_copies.append(
-                started(made.at[slot], away_ref.at[place_ref[b] + column], out_sems.at[slot])
-            )
+    sent = set()
+    middle = count // 2
+    for low, high in ((0, middle), (middle, count)):
+        back[low:high] = jnp.dot(
+            terms[low:high, : 2 * hidden_units], turned_in[...], preferred_element_type=F32
+        )
+        for column in range(X_RING):
+            for b in range(blocks):
+                first = column * per_x + b * capacity
+                slot = column * blocks + b
+                if slot in sent or (high < count and first + slot_rows > high):
+                    continue
+                sent.add(slot)
+                made[slot] = back[first : first + slot_rows].astype(BF16)
+                out_copies.append(
+                    started(made.at[slot], away_ref.at[place_ref[b] + column], out_sems.at[slot])
+                )
     terms_copy.wait()
     for copy in out_copies:
         copy.wait()
@@ -372,26 +378,41 @@
     )(routes)
 
 
-def combine_kernel(pick_ref, rows_ref, out_ref, made, sems):
-    made[...] = jnp.dot(
-        pick_ref[...], rows_ref[...], preferred_element_type=F32
-    ).astype(BF16)
-    started(made, out_ref, sems.at[0]).wait()
+def combine_kernel(pick_ref, rows_ref, out_ref, rows_in, made, sems):
+    pieces = rows_in.shape[0]
+    piece = rows_in.shape[1]
+    copies = [
+        started(rows_ref.at[pl.ds(i * piece, piece)], rows_in.at[i], sems.at[i])
+        for i in range(pieces)
+    ]
+    total = jnp.zeros(made.shape, F32)
+    for i in range(pieces):
+        copies[i].wait()
+        total += jnp.dot(
+            pick_ref[:, i * piece : (i + 1) * piece], rows_in[i], preferred_element_type=F32
+        )
+    made[...] = total.astype(BF16)
+    started(made, out_ref, sems.at[pieces]).wait()
 
 
 def combine(pick, rows_back):
     tokens, total_rows = pick.shape
     width = rows_back.shape[1]
+    pieces = total_rows // (5 * LANES)
     return pl.pallas_call(
         combine_kernel,
         out_shape=pltpu.HBM((tokens, width), BF16),
-        in_specs=[pl.BlockSpec(memory_space=pltpu.VMEM)] * 2,
+        in_specs=[pl.BlockSpec(memory_space=pltpu.VMEM), IN_HBM],
         out_specs=IN_HBM,
-        scratch_shapes=[pltpu.VMEM((tokens, width), BF16), DMA((1,))],
+        scratch_shapes=[
+            pltpu.VMEM((pieces, total_rows // pieces, width), BF16),
+            pltpu.VMEM((tokens, width), BF16),
+            DMA((pieces + 1,)),
+        ],
         compiler_params=params(8),
         cost_estimate=cost(2 * tokens * total_rows * width, 2 * (total_rows + tokens) * width),
         name="combine",
-    )(pick, rows_back)
+    )(pick, in_hbm(rows_back))
 
 
 def per_device(x_in, grad_out, routes, gate_probs, gate_up, down):

time: 185 us -> 184 us (level)
  no operation moved by 1% of the time
where the time goes in v8:
time: 184 us; the launch traced here: 183 us
  starting transfers between devices  90.7 us (49%)
  Pallas kernels  42.1 us (23%)
  waiting for transfers between devices  41.5 us (23%)
  local copies, waits for them, and re-layouts  7.37 us (4%)
    ppermute x8, starting transfers between devices, shift(): lax.ppermute(value, 'z', [(i, (i + by) % z_size) for i in range(z_size)])  35 us
    ppermute x7, starting transfers between devices, per_device(): lax.ppermute(shares[by], 'y', [(i, (i + by) % y_size) for i in range(y_si...  28.8 us
    pallas_call x3, Pallas kernels, expert_rows(): pl.pallas_call(functools.partial(expert_kernel, capacity, slot_rows), out...  16.8 us
    all_to_all x3, starting transfers between devices, crossed(): return lax.all_to_all(value, 'x', split_axis=0, concat_axis=0, tiled=True)  16 us
    ppermute x7, waiting for transfers between devices, per_device(): lax.ppermute(shares[by], 'y', [(i, (i + by) % y_size) for i in range(y_si...  13.1 us
    all_to_all x3, waiting for transfers between devices, crossed(): return lax.all_to_all(value, 'x', split_axis=0, concat_axis=0, tiled=True)  13 us
    ppermute x8, waiting for transfers between devices, shift(): lax.ppermute(value, 'z', [(i, (i + by) % z_size) for i in range(z_size)])  11.1 us
    pallas_call x3, Pallas kernels, pack(): pl.pallas_call(functools.partial(pack_kernel, top, capacity, width, token...  10.3 us
  transfers between devices with their start and end apart: 20, of which 9 were waited for; matrix products, arithmetic and copies ran while one was open for 4% of the time, Pallas kernels for 18%

profile of v8, /device:TPU:12, one launch (start us, length us, event | category | flops | bytes accessed | tf_op | source)
XLA Modules:
  0.0 183.0 jit_solution(14912422267917356004)
XLA Ops:
  1.8 4.4 %collective-permute-start = (bf16[128,2176]{1,0:T(8,128)(2,1)S(1)}, bf16[128,2176]{1,0:T(8,128)(2,1)S(1)}, u32[]{:S(2)}, u32[]{:S(2)}) collective-permute-start(bf16[128,2176]{1,0:T(8,128)(2,1)S(1)} %payload.1.refs_1_), channel_id=1, source_target_pairs={{0,4},{4,8},{8,12},{12,16},{16,20},{20,24},{24,28},{28,0},{1,5},{5... | collective-permute-start | bytes 1671176 | tf_op jit(solution)/shard_map/ppermute | solution.py:434
  6.2 8.6 %collective-permute-start.3 = (bf16[128,2176]{1,0:T(8,128)(2,1)S(1)}, bf16[128,2176]{1,0:T(8,128)(2,1)S(1)}, u32[]{:S(2)}, u32[]{:S(2)}) collective-permute-start(bf16[128,2176]{1,0:T(8,128)(2,1)S(1)} %payload.1.refs_1_), channel_id=1, source_target_pairs={{0,28},{4,0},{8,4},{12,8},{16,12},{20,16},{24,20},{28,24},{1,29},{... | collective-permute-start | bytes 1671176 | tf_op jit(solution)/shard_map/ppermute | solution.py:434
  14.8 2.6 %copy.14 = bf16[1,1024,768]{1,2,0:T(8,128)(2,1)} copy(bf16[1,1024,768]{2,1,0:T(8,128)(2,1)} %param.13) | data formatting | bytes 3145728 | tf_op args[4]
  17.5 8.0 %collective-permute-done.refs_2_ = bf16[128,2176]{1,0:T(8,128)(2,1)S(1)} collective-permute-done((bf16[128,2176]{1,0:T(8,128)(2,1)S(1)}, bf16[128,2176]{1,0:T(8,128)(2,1)S(1)}, u32[]{:S(2)}, u32[]{:S(2)}) %collective-permute-start) | collective-permute-done | bytes 557088 | tf_op jit(solution)/shard_map/ppermute | solution.py:434
  27.4 5.1 %collective-permute-start.4 = (bf16[128,2176]{1,0:T(8,128)(2,1)S(1)}, bf16[128,2176]{1,0:T(8,128)(2,1)}, u32[]{:S(2)}, u32[]{:S(2)}) collective-permute-start(bf16[128,2176]{1,0:T(8,128)(2,1)S(1)} %collective-permute-done.3.refs_3_), channel_id=1, source_target_pairs={{0,28},{4,0},{8,4},{12,8},{16,12},{20,16},{24,20},{28,24},{1,29},{... | collective-permute-start | bytes 1671176 | tf_op jit(solution)/shard_map/ppermute | solution.py:434
  32.6 3.2 %pack.4 = bf16[4,112,2048]{2,1,0:T(8,128)(2,1)} custom-call(s32[1]{0:T(128)} %bitcast.refs_0_, bf16[128,2176]{1,0:T(8,128)(2,1)S(1)} %payload.1.refs_1_, bf16[128,2176]{1,0:T(8,128)(2,1)S(1)} %collective-permute-done.refs_2_, bf16[128,2176]{1,0:T(8,128)(2,1)S(1)} %collective-permute-done.3.refs_3_), custom_call_target="tpu_custom_call" | custom-call | flops 42278584320 | bytes 204472320 | tf_op jit(solution)/shard_map/pack/pallas_call | solution.py:151
  35.7 4.8 %all-to-all-start = ((bf16[4,112,2048]{2,1,0:T(8,128)(2,1)}), bf16[4,112,2048]{2,1,0:T(8,128)(2,1)S(1)}, u32[]{:S(2)}, u32[]{:S(2)}) async-start(bf16[4,112,2048]{2,1,0:T(8,128)(2,1)} %pack.4), calls=%async_computation | async-start | bytes 3670016 | tf_op jit(solution)/shard_map/all_to_all | solution.py:440
  40.6 1.9 %collective-permute-done.1.refs_1_ = bf16[128,2176]{1,0:T(8,128)(2,1)} collective-permute-done((bf16[128,2176]{1,0:T(8,128)(2,1)S(1)}, bf16[128,2176]{1,0:T(8,128)(2,1)}, u32[]{:S(2)}, u32[]{:S(2)}) %collective-permute-start.1) | collective-permute-done | bytes 557088 | tf_op jit(solution)/shard_map/ppermute | solution.py:434
  47.8 6.0 %collective-permute-start.7 = (bf16[64,2176]{1,0:T(8,128)(2,1)}, bf16[64,2176]{1,0:T(8,128)(2,1)}, u32[]{:S(2)}, u32[]{:S(2)}) collective-permute-start(bf16[64,2176]{1,0:T(8,128)(2,1)} %slice.17), channel_id=1, source_target_pairs={{0,24},{4,28},{8,0},{12,4},{16,8},{20,12},{24,16},{28,20},{1,25},{... | collective-permute-start | bytes 835592 | tf_op jit(solution)/shard_map/ppermute | solution.py:434
  53.8 1.9 %collective-permute-start.2 = (bf16[128,2176]{1,0:T(8,128)(2,1)}, bf16[128,2176]{1,0:T(8,128)(2,1)}, u32[]{:S(2)}, u32[]{:S(2)}) collective-permute-start(bf16[128,2176]{1,0:T(8,128)(2,1)} %collective-permute-done.1.refs_1_), channel_id=1, source_target_pairs={{0,4},{4,8},{8,12},{12,16},{16,20},{20,24},{24,28},{28,0},{1,5},{5... | collective-permute-start | bytes 1671176 | tf_op jit(solution)/shard_map/ppermute | solution.py:434
  55.8 5.1 %collective-permute-start.5 = (bf16[128,2176]{1,0:T(8,128)(2,1)}, bf16[128,2176]{1,0:T(8,128)(2,1)}, u32[]{:S(2)}, u32[]{:S(2)}) collective-permute-start(bf16[128,2176]{1,0:T(8,128)(2,1)} %collective-permute-done.4.refs_2_), channel_id=1, source_target_pairs={{0,28},{4,0},{8,4},{12,8},{16,12},{20,16},{24,20},{28,24},{1,29},{... | collective-permute-start | bytes 1671176 | tf_op jit(solution)/shard_map/ppermute | solution.py:434
  60.9 3.2 %pack.3 = bf16[4,72,2048]{2,1,0:T(8,128)(2,1)} custom-call(s32[1]{0:T(128)} %bitcast.refs_0_, bf16[128,2176]{1,0:T(8,128)(2,1)} %collective-permute-done.1.refs_1_, bf16[128,2176]{1,0:T(8,128)(2,1)} %collective-permute-done.4.refs_2_), custom_call_target="tpu_custom_call" | custom-call | flops 18119393280 | bytes 133693440 | tf_op jit(solution)/shard_map/pack/pallas_call | solution.py:151
  64.1 4.8 %all-to-all-start.1 = ((bf16[4,72,2048]{2,1,0:T(8,128)(2,1)}), bf16[4,72,2048]{2,1,0:T(8,128)(2,1)S(1)}, u32[]{:S(2)}, u32[]{:S(2)}) async-start(bf16[4,72,2048]{2,1,0:T(8,128)(2,1)} %pack.3), calls=%async_computation.1 | async-start | bytes 2359296 | tf_op jit(solution)/shard_map/all_to_all | solution.py:440
  68.9 5.9 %expert.3 = (bf16[32,40,1024]{2,1,0:T(8,128)(2,1)}, bf16[448,1152]{1,0:T(8,128)(2,1)}) custom-call(s32[3]{0:T(128)S(1)} %get-tuple-element.66.refs_0_, bf16[448,2048]{1,0:T(8,128)(2,1)S(1)} %bitcast.18, bf16[1024,768]{1,0:T(8,128)(2,1)} %bitcast.29, bf16[1024,384]{1,0:T(8,128)(2,1)} %bitcast.36, bf16[768,1024]{1,0:T(8,128)(2,1)} %bitcast.32), custom_call_target="tpu_custom_call" | custom-call | flops 105696460800 | bytes 361758720 | tf_op jit(solution)/shard_map/expert/pallas_call | solution.py:233
  76.0 4.0 %pack.5 = bf16[4,112,2048]{2,1,0:T(8,128)(2,1)} custom-call(s32[1]{0:T(128)} %bitcast.refs_0_, bf16[128,2176]{1,0:T(8,128)(2,1)} %collective-permute-done.2.refs_1_, bf16[128,2176]{1,0:T(8,128)(2,1)} %collective-permute-done.5.refs_2_, bf16[64,2176]{1,0:T(8,128)(2,1)S(1)} %collective-permute-done.6.refs_3_, bf16[64,2176]{1,0:T(8,128)(2,1)} %collective-permute-done.7.refs_4_), custom_call_target="tpu_custom_call" | custom-call | flops 704643072 | bytes 3407872 | tf_op jit(solution)/shard_map/pack/pallas_call | solution.py:151
  80.0 6.4 %all-to-all-start.2 = ((bf16[4,112,2048]{2,1,0:T(8,128)(2,1)}), bf16[4,112,2048]{2,1,0:T(8,128)(2,1)S(1)}, u32[]{:S(2)}, u32[]{:S(2)}) async-start(bf16[4,112,2048]{2,1,0:T(8,128)(2,1)} %pack.5), calls=%async_computation.2 | async-start | bytes 3670016 | tf_op jit(solution)/shard_map/all_to_all | solution.py:440
  86.4 5.1 %expert.4 = (bf16[32,40,1024]{2,1,0:T(8,128)(2,1)}, bf16[288,1152]{1,0:T(8,128)(2,1)}) custom-call(s32[2]{0:T(128)S(1)} %fusion.5.refs_0_, bf16[288,2048]{1,0:T(8,128)(2,1)S(1)} %bitcast.24, bf16[1024,768]{1,0:T(8,128)(2,1)} %bitcast.30, bf16[1024,384]{1,0:T(8,128)(2,1)} %bitcast.37, bf16[768,1024]{1,0:T(8,128)(2,1)} %bitcast.33, ...), custom_call_target="tpu_custom_call", output_to_operand_aliasing={{0}: (5, {})} | custom-call | flops 67947724800 | bytes 283115520 | tf_op jit(solution)/shard_map/expert/pallas_call | solution.py:233
  91.5 13.0 %all-to-all-done.2 = bf16[4,112,2048]{2,1,0:T(8,128)(2,1)S(1)} async-done(((bf16[4,112,2048]{2,1,0:T(8,128)(2,1)}), bf16[4,112,2048]{2,1,0:T(8,128)(2,1)S(1)}, u32[]{:S(2)}, u32[]{:S(2)}) %all-to-all-start.2) | async-done | bytes 1835040 | tf_op jit(solution)/shard_map/all_to_all | solution.py:440
  104.5 5.9 %expert.5 = (bf16[32,40,1024]{2,1,0:T(8,128)(2,1)}, bf16[448,1152]{1,0:T(8,128)(2,1)}) custom-call(s32[3]{0:T(128)S(1)} %get-tuple-element.65.refs_0_, bf16[448,2048]{1,0:T(8,128)(2,1)S(1)} %bitcast.21, bf16[1024,768]{1,0:T(8,128)(2,1)} %bitcast.31, bf16[1024,384]{1,0:T(8,128)(2,1)} %bitcast.38, ...), custom_call_target="tpu_custom_call", output_to_operand_aliasing={{0}: (5, {})} | custom-call | flops 105696460800 | bytes 361758720 | tf_op jit(solution)/shard_map/expert/pallas_call | solution.py:233
  110.4 8.8 %all-to-all-start.3 = ((bf16[32,40,1024]{2,1,0:T(8,128)(2,1)}), bf16[32,40,1024]{2,1,0:T(8,128)(2,1)}, u32[]{:S(2)}, u32[]{:S(2)}) async-start(bf16[32,40,1024]{2,1,0:T(8,128)(2,1)} %get-tuple-element.47), calls=%async_computation.3 | async-start | bytes 5242880 | tf_op jit(solution)/shard_map/all_to_all | solution.py:481
  119.2 8.5 %weight_terms.1 = (f32[8,64,1152]{2,1,0:T(8,128)}, bf16[8,64,1152]{2,1,0:T(8,128)(2,1)}) custom-call(s32[1]{0:T(128)} %bitcast.12.refs_0_, bf16[448,2048]{1,0:T(8,128)(2,1)} %bitcast.19, bf16[448,2048]{1,0:T(8,128)(2,1)} %bitcast.20, bf16[448,1152]{1,0:T(8,128)(2,1)} %get-tuple-element.48.refs_3_, bf16[288,2048]{1,0:T(8,128)(2,1)} %bitcast.25, ...), custom_call_target="tpu_custom_call" | custom-call | flops 167604387840 | bytes 666992640 | tf_op jit(solution)/shard_map/weight_terms/pallas_call | solution.py:303
  127.7 2.0 %collective-permute-start.8 = (bf16[8,64,1152]{2,1,0:T(8,128)(2,1)}, bf16[8,64,1152]{2,1,0:T(8,128)(2,1)S(1)}, u32[]{:S(2)}, u32[]{:S(2)}) collective-permute-start(bf16[8,64,1152]{2,1,0:T(8,128)(2,1)} %get-tuple-element.52), channel_id=1, source_target_pairs={{0,32},{32,0},{1,33},{33,1},{2,34},{34,2},{3,35},{35,3},{4,36},{36... | collective-permute-start | bytes 3538952 | tf_op jit(solution)/shard_map/ppermute | solution.py:490
  129.7 3.0 %collective-permute-done.8.other_ref = bf16[8,64,1152]{2,1,0:T(8,128)(2,1)S(1)} collective-permute-done((bf16[8,64,1152]{2,1,0:T(8,128)(2,1)}, bf16[8,64,1152]{2,1,0:T(8,128)(2,1)S(1)}, u32[]{:S(2)}, u32[]{:S(2)}) %collective-permute-start.8) | collective-permute-done | bytes 1179680 | tf_op jit(solution)/shard_map/ppermute | solution.py:490
  134.6 4.5 %collective-permute-start.10 = (bf16[64,1152]{1,0:T(8,128)(2,1)S(1)}, bf16[64,1152]{1,0:T(8,128)(2,1)S(1)}, u32[]{:S(2)}, u32[]{:S(2)}) collective-permute-start(bf16[64,1152]{1,0:T(8,128)(2,1)S(1)} %get-tuple-element.55), channel_id=1, source_target_pairs={{0,128},{64,192},{128,256},{192,320},{256,384},{320,448},{384,0},{... | collective-permute-start | bytes 442376 | tf_op jit(solution)/shard_map/ppermute | solution.py:494
  139.1 4.9 %collective-permute-start.11 = (bf16[64,1152]{1,0:T(8,128)(2,1)S(1)}, bf16[64,1152]{1,0:T(8,128)(2,1)S(1)}, u32[]{:S(2)}, u32[]{:S(2)}) collective-permute-start(bf16[64,1152]{1,0:T(8,128)(2,1)S(1)} %get-tuple-element.56), channel_id=1, source_target_pairs={{0,192},{64,256},{128,320},{192,384},{256,448},{320,0},{384,64},{4... | collective-permute-start | bytes 442376 | tf_op jit(solution)/shard_map/ppermute | solution.py:494
  144.0 3.8 %collective-permute-start.12 = (bf16[64,1152]{1,0:T(8,128)(2,1)S(1)}, bf16[64,1152]{1,0:T(8,128)(2,1)S(1)}, u32[]{:S(2)}, u32[]{:S(2)}) collective-permute-start(bf16[64,1152]{1,0:T(8,128)(2,1)S(1)} %get-tuple-element.57), channel_id=1, source_target_pairs={{0,256},{64,320},{128,384},{192,448},{256,0},{320,64},{384,128},{4... | collective-permute-start | bytes 442376 | tf_op jit(solution)/shard_map/ppermute | solution.py:494
  147.9 5.2 %collective-permute-start.13 = (bf16[64,1152]{1,0:T(8,128)(2,1)S(1)}, bf16[64,1152]{1,0:T(8,128)(2,1)S(1)}, u32[]{:S(2)}, u32[]{:S(2)}) collective-permute-start(bf16[64,1152]{1,0:T(8,128)(2,1)S(1)} %get-tuple-element.58), channel_id=1, source_target_pairs={{0,320},{64,384},{128,448},{192,0},{256,64},{320,128},{384,192},{4... | collective-permute-start | bytes 442376 | tf_op jit(solution)/shard_map/ppermute | solution.py:494
  153.0 4.0 %collective-permute-start.14 = (bf16[64,1152]{1,0:T(8,128)(2,1)S(1)}, bf16[64,1152]{1,0:T(8,128)(2,1)S(1)}, u32[]{:S(2)}, u32[]{:S(2)}) collective-permute-start(bf16[64,1152]{1,0:T(8,128)(2,1)S(1)} %get-tuple-element.59), channel_id=1, source_target_pairs={{0,384},{64,448},{128,0},{192,64},{256,128},{320,192},{384,256},{4... | collective-permute-start | bytes 442376 | tf_op jit(solution)/shard_map/ppermute | solution.py:494
  157.1 4.5 %collective-permute-start.15 = (bf16[64,1152]{1,0:T(8,128)(2,1)S(1)}, bf16[64,1152]{1,0:T(8,128)(2,1)S(1)}, u32[]{:S(2)}, u32[]{:S(2)}) collective-permute-start(bf16[64,1152]{1,0:T(8,128)(2,1)S(1)} %get-tuple-element.60), channel_id=1, source_target_pairs={{0,448},{64,0},{128,64},{192,128},{256,192},{320,256},{384,320},{4... | collective-permute-start | bytes 442376 | tf_op jit(solution)/shard_map/ppermute | solution.py:494
  164.0 2.9 %collective-permute-done.13 = bf16[64,1152]{1,0:T(8,128)(2,1)S(1)} collective-permute-done((bf16[64,1152]{1,0:T(8,128)(2,1)S(1)}, bf16[64,1152]{1,0:T(8,128)(2,1)S(1)}, u32[]{:S(2)}, u32[]{:S(2)}) %collective-permute-start.13) | collective-permute-done | bytes 147488 | tf_op jit(solution)/shard_map/ppermute | solution.py:494
  166.9 8.3 %collective-permute-done.14 = bf16[64,1152]{1,0:T(8,128)(2,1)S(1)} collective-permute-done((bf16[64,1152]{1,0:T(8,128)(2,1)S(1)}, bf16[64,1152]{1,0:T(8,128)(2,1)S(1)}, u32[]{:S(2)}, u32[]{:S(2)}) %collective-permute-start.14) | collective-permute-done | bytes 147488 | tf_op jit(solution)/shard_map/ppermute | solution.py:494
  179.8 3.0 %combine.1 = bf16[128,1024]{1,0:T(8,128)(2,1)} custom-call(bf16[128,1280]{1,0:T(8,128)(2,1)S(1)} %choose.1.pick_ref, bf16[1280,1024]{1,0:T(8,128)(2,1)} %bitcast.15.rows_ref), custom_call_target="tpu_custom_call" | custom-call | flops 20132659200 | bytes 173015040 | tf_op jit(solution)/shard_map/combine/pallas_call | solution.py:402
  (39 shorter events, 18.4 us)
Async XLA Ops:
  1.7 15.7 %copy-start.5 = (s32[2]{0:T(128)S(1)}, s32[2]{0:T(128)}, u32[]{:S(2)}) copy-start(s32[2]{0:T(128)} %constant.55.clone) | copy-start | bytes 28
  1.8 15.7 %copy-start.3 = (s32[3]{0:T(128)S(1)}, s32[3]{0:T(128)}, u32[]{:S(2)}) copy-start(s32[3]{0:T(128)} %constant.54.clone) | copy-start | bytes 40
  1.8 15.7 %copy-start.4 = (s32[3]{0:T(128)S(1)}, s32[3]{0:T(128)}, u32[]{:S(2)}) copy-start(s32[3]{0:T(128)} %constant.56.clone) | copy-start | bytes 40
  1.8 23.7 %collective-permute-start = (bf16[128,2176]{1,0:T(8,128)(2,1)S(1)}, bf16[128,2176]{1,0:T(8,128)(2,1)S(1)}, u32[]{:S(2)}, u32[]{:S(2)}) collective-permute-start(bf16[128,2176]{1,0:T(8,128)(2,1)S(1)} %payload.1.refs_1_), channel_id=1, source_target_pairs={{0,4},{4,8},{8,12},{12,16},{16,20},{20,24},{24,28},{28,0},{1,5},{5... | collective-permute-start | bytes 1671176 | tf_op jit(solution)/shard_map/ppermute | solution.py:434
  6.2 21.2 %collective-permute-start.3 = (bf16[128,2176]{1,0:T(8,128)(2,1)S(1)}, bf16[128,2176]{1,0:T(8,128)(2,1)S(1)}, u32[]{:S(2)}, u32[]{:S(2)}) collective-permute-start(bf16[128,2176]{1,0:T(8,128)(2,1)S(1)} %payload.1.refs_1_), channel_id=1, source_target_pairs={{0,28},{4,0},{8,4},{12,8},{16,12},{20,16},{24,20},{28,24},{1,29},{... | collective-permute-start | bytes 1671176 | tf_op jit(solution)/shard_map/ppermute | solution.py:434
  25.5 17.0 %collective-permute-start.1 = (bf16[128,2176]{1,0:T(8,128)(2,1)S(1)}, bf16[128,2176]{1,0:T(8,128)(2,1)}, u32[]{:S(2)}, u32[]{:S(2)}) collective-permute-start(bf16[128,2176]{1,0:T(8,128)(2,1)S(1)} %collective-permute-done.refs_2_), channel_id=1, source_target_pairs={{0,4},{4,8},{8,12},{12,16},{16,20},{20,24},{24,28},{28,0},{1,5},{5... | collective-permute-start | bytes 1671176 | tf_op jit(solution)/shard_map/ppermute | solution.py:434
  27.4 18.7 %collective-permute-start.4 = (bf16[128,2176]{1,0:T(8,128)(2,1)S(1)}, bf16[128,2176]{1,0:T(8,128)(2,1)}, u32[]{:S(2)}, u32[]{:S(2)}) collective-permute-start(bf16[128,2176]{1,0:T(8,128)(2,1)S(1)} %collective-permute-done.3.refs_3_), channel_id=1, source_target_pairs={{0,28},{4,0},{8,4},{12,8},{16,12},{20,16},{24,20},{28,24},{1,29},{... | collective-permute-start | bytes 1671176 | tf_op jit(solution)/shard_map/ppermute | solution.py:434
  35.7 28.3 %all-to-all-start = ((bf16[4,112,2048]{2,1,0:T(8,128)(2,1)}), bf16[4,112,2048]{2,1,0:T(8,128)(2,1)S(1)}, u32[]{:S(2)}, u32[]{:S(2)}) async-start(bf16[4,112,2048]{2,1,0:T(8,128)(2,1)} %pack.4), calls=%async_computation | async-start | bytes 3670016 | tf_op jit(solution)/shard_map/all_to_all | solution.py:440
  44.2 30.6 %collective-permute-start.6 = (bf16[64,2176]{1,0:T(8,128)(2,1)}, bf16[64,2176]{1,0:T(8,128)(2,1)S(1)}, u32[]{:S(2)}, u32[]{:S(2)}) collective-permute-start(bf16[64,2176]{1,0:T(8,128)(2,1)} %slice.16), channel_id=1, source_target_pairs={{0,8},{4,12},{8,16},{12,20},{16,24},{20,28},{24,0},{28,4},{1,9},{5... | collective-permute-start | bytes 835592 | tf_op jit(solution)/shard_map/ppermute | solution.py:434
  47.8 27.0 %collective-permute-start.7 = (bf16[64,2176]{1,0:T(8,128)(2,1)}, bf16[64,2176]{1,0:T(8,128)(2,1)}, u32[]{:S(2)}, u32[]{:S(2)}) collective-permute-start(bf16[64,2176]{1,0:T(8,128)(2,1)} %slice.17), channel_id=1, source_target_pairs={{0,24},{4,28},{8,0},{12,4},{16,8},{20,12},{24,16},{28,20},{1,25},{... | collective-permute-start | bytes 835592 | tf_op jit(solution)/shard_map/ppermute | solution.py:434
  53.8 21.0 %collective-permute-start.2 = (bf16[128,2176]{1,0:T(8,128)(2,1)}, bf16[128,2176]{1,0:T(8,128)(2,1)}, u32[]{:S(2)}, u32[]{:S(2)}) collective-permute-start(bf16[128,2176]{1,0:T(8,128)(2,1)} %collective-permute-done.1.refs_1_), channel_id=1, source_target_pairs={{0,4},{4,8},{8,12},{12,16},{16,20},{20,24},{24,28},{28,0},{1,5},{5... | collective-permute-start | bytes 1671176 | tf_op jit(solution)/shard_map/ppermute | solution.py:434
  55.8 20.2 %collective-permute-start.5 = (bf16[128,2176]{1,0:T(8,128)(2,1)}, bf16[128,2176]{1,0:T(8,128)(2,1)}, u32[]{:S(2)}, u32[]{:S(2)}) collective-permute-start(bf16[128,2176]{1,0:T(8,128)(2,1)} %collective-permute-done.4.refs_2_), channel_id=1, source_target_pairs={{0,28},{4,0},{8,4},{12,8},{16,12},{20,16},{24,20},{28,24},{1,29},{... | collective-permute-start | bytes 1671176 | tf_op jit(solution)/shard_map/ppermute | solution.py:434
  64.1 10.7 %copy-start = (bf16[4,112,2048]{2,1,0:T(8,128)(2,1)}, bf16[4,112,2048]{2,1,0:T(8,128)(2,1)S(1)}, u32[]{:S(2)}) copy-start(bf16[4,112,2048]{2,1,0:T(8,128)(2,1)S(1)} %all-to-all-done) | copy-start | bytes 5505028
  64.1 15.9 %all-to-all-start.1 = ((bf16[4,72,2048]{2,1,0:T(8,128)(2,1)}), bf16[4,72,2048]{2,1,0:T(8,128)(2,1)S(1)}, u32[]{:S(2)}, u32[]{:S(2)}) async-start(bf16[4,72,2048]{2,1,0:T(8,128)(2,1)} %pack.3), calls=%async_computation.1 | async-start | bytes 2359296 | tf_op jit(solution)/shard_map/all_to_all | solution.py:440
  80.0 6.4 %copy-start.1 = (bf16[4,72,2048]{2,1,0:T(8,128)(2,1)}, bf16[4,72,2048]{2,1,0:T(8,128)(2,1)S(1)}, u32[]{:S(2)}) copy-start(bf16[4,72,2048]{2,1,0:T(8,128)(2,1)S(1)} %all-to-all-done.1) | copy-start | bytes 3538948
  80.0 24.5 %all-to-all-start.2 = ((bf16[4,112,2048]{2,1,0:T(8,128)(2,1)}), bf16[4,112,2048]{2,1,0:T(8,128)(2,1)S(1)}, u32[]{:S(2)}, u32[]{:S(2)}) async-start(bf16[4,112,2048]{2,1,0:T(8,128)(2,1)} %pack.5), calls=%async_computation.2 | async-start | bytes 3670016 | tf_op jit(solution)/shard_map/all_to_all | solution.py:440
  110.4 69.5 %all-to-all-start.3 = ((bf16[32,40,1024]{2,1,0:T(8,128)(2,1)}), bf16[32,40,1024]{2,1,0:T(8,128)(2,1)}, u32[]{:S(2)}, u32[]{:S(2)}) async-start(bf16[32,40,1024]{2,1,0:T(8,128)(2,1)} %get-tuple-element.47), calls=%async_computation.3 | async-start | bytes 5242880 | tf_op jit(solution)/shard_map/all_to_all | solution.py:481
  127.6 35.9 %copy-start.2 = (s32[128,8]{0,1:T(8,128)S(1)}, s32[128,8]{0,1:T(8,128)}, u32[]{:S(2)}) copy-start(s32[128,8]{0,1:T(8,128)} %param.11) | copy-start | bytes 12292
  127.7 5.1 %collective-permute-start.8 = (bf16[8,64,1152]{2,1,0:T(8,128)(2,1)}, bf16[8,64,1152]{2,1,0:T(8,128)(2,1)S(1)}, u32[]{:S(2)}, u32[]{:S(2)}) collective-permute-start(bf16[8,64,1152]{2,1,0:T(8,128)(2,1)} %get-tuple-element.52), channel_id=1, source_target_pairs={{0,32},{32,0},{1,33},{33,1},{2,34},{34,2},{3,35},{35,3},{4,36},{36... | collective-permute-start | bytes 3538952 | tf_op jit(solution)/shard_map/ppermute | solution.py:490
  134.6 22.5 %collective-permute-start.10 = (bf16[64,1152]{1,0:T(8,128)(2,1)S(1)}, bf16[64,1152]{1,0:T(8,128)(2,1)S(1)}, u32[]{:S(2)}, u32[]{:S(2)}) collective-permute-start(bf16[64,1152]{1,0:T(8,128)(2,1)S(1)} %get-tuple-element.55), channel_id=1, source_target_pairs={{0,128},{64,192},{128,256},{192,320},{256,384},{320,448},{384,0},{... | collective-permute-start | bytes 442376 | tf_op jit(solution)/shard_map/ppermute | solution.py:494
  139.1 22.5 %collective-permute-start.11 = (bf16[64,1152]{1,0:T(8,128)(2,1)S(1)}, bf16[64,1152]{1,0:T(8,128)(2,1)S(1)}, u32[]{:S(2)}, u32[]{:S(2)}) collective-permute-start(bf16[64,1152]{1,0:T(8,128)(2,1)S(1)} %get-tuple-element.56), channel_id=1, source_target_pairs={{0,192},{64,256},{128,320},{192,384},{256,448},{320,0},{384,64},{4... | collective-permute-start | bytes 442376 | tf_op jit(solution)/shard_map/ppermute | solution.py:494
  144.0 20.0 %collective-permute-start.12 = (bf16[64,1152]{1,0:T(8,128)(2,1)S(1)}, bf16[64,1152]{1,0:T(8,128)(2,1)S(1)}, u32[]{:S(2)}, u32[]{:S(2)}) collective-permute-start(bf16[64,1152]{1,0:T(8,128)(2,1)S(1)} %get-tuple-element.57), channel_id=1, source_target_pairs={{0,256},{64,320},{128,384},{192,448},{256,0},{320,64},{384,128},{4... | collective-permute-start | bytes 442376 | tf_op jit(solution)/shard_map/ppermute | solution.py:494
  147.9 19.1 %collective-permute-start.13 = (bf16[64,1152]{1,0:T(8,128)(2,1)S(1)}, bf16[64,1152]{1,0:T(8,128)(2,1)S(1)}, u32[]{:S(2)}, u32[]{:S(2)}) collective-permute-start(bf16[64,1152]{1,0:T(8,128)(2,1)S(1)} %get-tuple-element.58), channel_id=1, source_target_pairs={{0,320},{64,384},{128,448},{192,0},{256,64},{320,128},{384,192},{4... | collective-permute-start | bytes 442376 | tf_op jit(solution)/shard_map/ppermute | solution.py:494
  153.0 22.2 %collective-permute-start.14 = (bf16[64,1152]{1,0:T(8,128)(2,1)S(1)}, bf16[64,1152]{1,0:T(8,128)(2,1)S(1)}, u32[]{:S(2)}, u32[]{:S(2)}) collective-permute-start(bf16[64,1152]{1,0:T(8,128)(2,1)S(1)} %get-tuple-element.59), channel_id=1, source_target_pairs={{0,384},{64,448},{128,0},{192,64},{256,128},{320,192},{384,256},{4... | collective-permute-start | bytes 442376 | tf_op jit(solution)/shard_map/ppermute | solution.py:494
  157.1 20.0 %collective-permute-start.15 = (bf16[64,1152]{1,0:T(8,128)(2,1)S(1)}, bf16[64,1152]{1,0:T(8,128)(2,1)S(1)}, u32[]{:S(2)}, u32[]{:S(2)}) collective-permute-start(bf16[64,1152]{1,0:T(8,128)(2,1)S(1)} %get-tuple-element.60), channel_id=1, source_target_pairs={{0,448},{64,0},{128,64},{192,128},{256,192},{320,256},{384,320},{4... | collective-permute-start | bytes 442376 | tf_op jit(solution)/shard_map/ppermute | solution.py:494
  161.6 15.5 %collective-permute-start.9 = (bf16[64,1152]{1,0:T(8,128)(2,1)S(1)}, bf16[64,1152]{1,0:T(8,128)(2,1)S(1)}, u32[]{:S(2)}, u32[]{:S(2)}) collective-permute-start(bf16[64,1152]{1,0:T(8,128)(2,1)S(1)} %get-tuple-element.54), channel_id=1, source_target_pairs={{0,64},{64,128},{128,192},{192,256},{256,320},{320,384},{384,448},... | collective-permute-start | bytes 442376 | tf_op jit(solution)/shard_map/ppermute | solution.py:494
